TPU v7x, 256 devices: a whole 4x4x8 slice. The times are simulated.
256 devices in a mesh: ctx: 32 (over y, z), head: 8 (over x, core).
Axes of the slice: x: 4, y: 4, z: 8, core: 2. Of those that a mesh axis runs over, the one named last changes fastest.
Arguments:
- queries: bfloat16 [32768, 4096], P('ctx', 'head'), may hold values from -6 to 6
- keys: bfloat16 [32768, 1024], P('ctx', 'head'), may hold values from -6 to 6
- values: bfloat16 [32768, 1024], P('ctx', 'head'), may hold values from -6 to 6
- block_masks: int32 [32, 256], P('head', 'ctx'), may hold values from 0 to 255
- residual: bfloat16 [32768, 4096], P(('ctx', 'head')), may hold values from -1.5 to 1.5
- norm_gain: bfloat16 [4096], replicated, may hold values from 0.099609375 to 1.8984375
Outputs:
- stream: bfloat16 [32768, 4096], P(('ctx', 'head'))
- normed: bfloat16 [32768, 4096], P(('ctx', 'head'))
Inputs may be any that keep to these rules, and one draw needn't show every extreme that they name: Bit b of block_masks[h, i] says whether query block i of head h attends to block i XOR 2^b; it is read only where that block comes earlier, and bits from 8 up are zero.
All inputs are finite; a program needn't handle non-finite values.
Results may differ from a plain program's by a relative error of at most 0.0052.
Values may be sent and summed in bfloat16 or wider, within the bound.
No kernel may reach another device: no remote copies, remote signals or barrier semaphores. Data moves between devices by JAX's collectives and lax.ppermute only.
A program may use at most 64 MiB of HBM per device.

v0:
```python
import jax
import jax.numpy as jnp
from jax import lax
from jax.sharding import PartitionSpec as P

DH = 128
BLOCK = 128


MASKED_SCORE = -1e30
EPSILON = 1e-05


def passed_along(block, axis, distance):
    devices = range(lax.axis_size(axis))
    route = [(i - distance, i) for i in devices if i - distance in devices]
    return lax.ppermute(block, axis, route)


def split_upper(source, axis_at, stride):
    extent = source.shape
    length = extent[axis_at]
    folded = source.reshape(
        extent[:axis_at] + (length // (2 * stride), 2, stride) + extent[axis_at + 1 :]
    )
    low_part = lax.index_in_dim(folded, 0, axis_at + 1, keepdims=False)
    high_part = lax.index_in_dim(folded, 1, axis_at + 1, keepdims=False)
    flattened = extent[:axis_at] + (length // 2,) + extent[axis_at + 1 :]
    return (low_part.reshape(flattened), high_part.reshape(flattened))


def join_halves(low_part, high_part, axis_at, stride):
    extent = low_part.shape
    length = extent[axis_at]
    folded = extent[:axis_at] + (length // stride, 1, stride) + extent[axis_at + 1 :]
    stacked = jnp.concatenate(
        [low_part.reshape(folded), high_part.reshape(folded)], axis=axis_at + 1
    )
    return stacked.reshape(extent[:axis_at] + (length * 2,) + extent[axis_at + 1 :])


def to_blocks(source, head_count):
    length = source.shape[0]
    return source.reshape(length // BLOCK, BLOCK, head_count, DH).transpose(2, 0, 1, 3)


def level_flags(bitmap, bit_level):
    return jnp.right_shift(bitmap, bit_level) & 1 == 1


def fresh_state(groups, head_count, blocks):
    return (
        jnp.full((groups, head_count, blocks, BLOCK), MASKED_SCORE, jnp.float32),
        jnp.zeros((groups, head_count, blocks, BLOCK), jnp.float32),
        jnp.zeros((groups, head_count, blocks, BLOCK, DH), jnp.float32),
    )


def update(running, query_part, key_part, value_part, allowed):
    row_max, row_sum, weighted = running
    scores = jnp.einsum(
        "gjnqd,gnkd->gjnqk", query_part, key_part, preferred_element_type=jnp.float32
    ) * DH ** (-0.5)
    scores = jnp.where(allowed, scores, MASKED_SCORE)
    new_max = jnp.maximum(row_max, scores.max(-1))
    factor = jnp.exp(row_max - new_max)
    weights = jnp.where(allowed, jnp.exp(scores - new_max[..., None]), 0.0)
    new_sum = row_sum * factor + weights.sum(-1)
    new_weighted = weighted * factor[..., None] + jnp.einsum(
        "gjnqk,gnkd->gjnqd",
        weights.astype(jnp.bfloat16),
        value_part,
        preferred_element_type=jnp.float32,
    )
    return (new_max, new_sum, new_weighted)


def fetch_partner(keys, values, bit_level):
    return passed_along((keys, values), "ctx", 2**bit_level)


def shards(queries, keys, values, block_masks, residual, norm_gain):
    tokens = queries.shape[0]
    blocks = tokens // BLOCK
    groups = keys.shape[1] // DH
    per_group = queries.shape[1] // keys.shape[1]
    query_blocks = queries.reshape(blocks, BLOCK, groups, per_group, DH).transpose(2, 3, 0, 1, 4)
    key_blocks = to_blocks(keys, groups)
    value_blocks = to_blocks(values, groups)
    head_bits = block_masks.reshape(groups, per_group, blocks)
    local_bits = blocks.bit_length() - 1
    ctx_bits = lax.axis_size("ctx").bit_length() - 1
    ctx_index = lax.axis_index("ctx")
    causal = lax.broadcasted_iota(jnp.int32, (BLOCK, BLOCK), 0) >= lax.broadcasted_iota(
        jnp.int32, (BLOCK, BLOCK), 1
    )
    running = update(
        fresh_state(groups, per_group, blocks), query_blocks, key_blocks, value_blocks, causal
    )
    for bit_level in range(local_bits):
        stride = 2**bit_level
        _, query_high = split_upper(query_blocks, 2, stride)
        key_low, _ = split_upper(key_blocks, 1, stride)
        value_low, _ = split_upper(value_blocks, 1, stride)
        _, bits_high = split_upper(head_bits, 2, stride)
        allowed = level_flags(bits_high, bit_level)[..., None, None]
        divided = [split_upper(portion, 2, stride) for portion in running]
        upper_state = update(
            tuple((halves_pair[1] for halves_pair in divided)),
            query_high,
            key_low,
            value_low,
            allowed,
        )
        running = tuple(
            (
                join_halves(halves_pair[0], portion, 2, stride)
                for halves_pair, portion in zip(divided, upper_state)
            )
        )
    sequence_bits = list(range(ctx_bits))
    for bit_level in sequence_bits:
        far_keys, far_values = fetch_partner(keys, values, bit_level)
        bit_set = jnp.right_shift(ctx_index, bit_level) & 1 == 1
        far_key_blocks = to_blocks(far_keys, groups)
        far_value_blocks = to_blocks(far_values, groups)
        remote_allowed = level_flags(head_bits, local_bits + bit_level)[..., None, None]
        running = lax.cond(
            bit_set,
            lambda state: update(
                state, query_blocks, far_key_blocks, far_value_blocks, remote_allowed
            ),
            lambda state: state,
            running,
        )
    row_max, row_sum, weighted = running
    attended = (weighted / row_sum[..., None]).astype(jnp.bfloat16)
    attended = attended.transpose(2, 3, 0, 1, 4).reshape(tokens, groups * per_group * DH)
    gathered = lax.all_to_all(attended, "head", split_axis=0, concat_axis=1, tiled=True)
    summed = residual.astype(jnp.float32) + gathered.astype(jnp.float32)
    stream = summed.astype(jnp.bfloat16)
    normed = (
        summed
        * lax.rsqrt(jnp.mean(summed * summed, axis=-1, keepdims=True) + EPSILON)
        * norm_gain.astype(jnp.float32)
    )
    return (stream, normed.astype(jnp.bfloat16))


def solution(mesh):
    in_specs = (
        P("ctx", "head"),
        P("ctx", "head"),
        P("ctx", "head"),
        P("head", "ctx"),
        P(("ctx", "head"), None),
        P(),
    )
    out_specs = (P(("ctx", "head"), None), P(("ctx", "head"), None))
    return jax.shard_map(shards, mesh=mesh, in_specs=in_specs, out_specs=out_specs, check_vma=False)
```

profile of v0, /device:TPU:184, one launch (start us, length us, event | category | flops | bytes accessed | tf_op | source)
XLA Modules:
  0.0 132.7 jit_solution(12905347057561862740)
XLA Ops:
  0.6 2.9 %collective-permute-start = (bf16[1024,128]{1,0:T(8,128)(2,1)}, bf16[1024,128]{1,0:T(8,128)(2,1)}, u32[]{:S(2)}, u32[]{:S(2)}) collective-permute-start(bf16[1024,128]{1,0:T(8,128)(2,1)} %param.17), channel_id=1, source_target_pairs={{0,8},{8,16},{16,24},{24,32},{32,40},{40,48},{48,56},{56,64},{64,7... | collective-permute-start | bytes 786440 | tf_op jit(solution)/shard_map/ppermute | solution.py:17
  3.6 1.9 %collective-permute-start.2 = (bf16[1024,128]{1,0:T(8,128)(2,1)}, bf16[1024,128]{1,0:T(8,128)(2,1)}, u32[]{:S(2)}, u32[]{:S(2)}) collective-permute-start(bf16[1024,128]{1,0:T(8,128)(2,1)} %param.17), channel_id=1, source_target_pairs={{0,16},{8,24},{16,32},{24,40},{32,48},{40,56},{48,64},{56,72},{64,... | collective-permute-start | bytes 786440 | tf_op jit(solution)/shard_map/ppermute | solution.py:17
  5.5 2.3 %collective-permute-start.1 = (bf16[1024,128]{1,0:T(8,128)(2,1)}, bf16[1024,128]{1,0:T(8,128)(2,1)}, u32[]{:S(2)}, u32[]{:S(2)}) collective-permute-start(bf16[1024,128]{1,0:T(8,128)(2,1)} %param.18), channel_id=1, source_target_pairs={{0,8},{8,16},{16,24},{24,32},{32,40},{40,48},{48,56},{56,64},{64,7... | collective-permute-start | bytes 786440 | tf_op jit(solution)/shard_map/ppermute | solution.py:17
  7.8 1.9 %collective-permute-start.3 = (bf16[1024,128]{1,0:T(8,128)(2,1)}, bf16[1024,128]{1,0:T(8,128)(2,1)}, u32[]{:S(2)}, u32[]{:S(2)}) collective-permute-start(bf16[1024,128]{1,0:T(8,128)(2,1)} %param.18), channel_id=1, source_target_pairs={{0,16},{8,24},{16,32},{24,40},{32,48},{40,56},{48,64},{56,72},{64,... | collective-permute-start | bytes 786440 | tf_op jit(solution)/shard_map/ppermute | solution.py:17
  28.1 2.5 %bitcast_add_fusion.10 = f32[1,4,8,128,128]{4,3,1,2,0:T(8,128)S(1)} fusion(bf16[8,128,128,1]{2,1,3,0:T(8,128)(2,1)} %bitcast.147, f32[8,128,4,128]{3,1,2,0:T(8,128)} %copy-done, f32[4,8,128]{2,0,1:T(4,128)S(1)} %copy-done.15, f32[4,8,128]{2,0,1:T(4,128)S(1)} %copy-done.6, pred[128,128]{0,1:T(8,128)(4,1)S(1)} %iota_compare_fusion), kind=kOutput, calls=%fused_computation.119 | convolution fusion | flops 137363456 | bytes 4505600 | tf_op jit(solution)/shard_map/gjnqk,gnkd->gjnqd/dot_general | solution.py:69
  43.3 19.8 %collective-permute-done.3 = bf16[1024,128]{1,0:T(8,128)(2,1)} collective-permute-done((bf16[1024,128]{1,0:T(8,128)(2,1)}, bf16[1024,128]{1,0:T(8,128)(2,1)}, u32[]{:S(2)}, u32[]{:S(2)}) %collective-permute-start.3) | collective-permute-done | bytes 262176 | tf_op jit(solution)/shard_map/ppermute | solution.py:17
  65.8 8.7 %conditional.5 = (f32[1,4,8,128]{3,1,2,0:T(4,128)}, f32[1,4,8,128]{3,1,2,0:T(4,128)S(1)}, f32[1,4,8,128,128]{4,3,1,2,0:T(8,128)S(1)}) conditional(s32[]{:T(128)} %convert_element_type.73, (f32[1,4,8,128]{3,2,1,0:T(8,128)S(1)}, f32[1,4,8,128]{3,2,1,0:T(8,128)S(1)}, f32[1,4,8,128,128]{4,3,1,2,0:T(8,128)S(1)}) %tuple.150, ...), branch_computations={%region_8.9_spmd, %region_9.12_spmd} | conditional | flops 276312064 | bytes 14385336 | solution.py:128
  67.4 1.8 %fusion = (f32[4,8,128]{2,0,1:T(4,128)S(1)}, f32[8,128,4,128]{3,1,2,0:T(8,128)S(1)}) fusion(pred[4,8]{0,1:T(8,128)(4,1)S(1)} %copy.341, bf16[1,4,8,128,128]{4,3,1,2,0:T(8,128)(2,1)} %copy.395, bf16[1,8,128,128]{3,2,1,0:T(8,128)(2,1)} %get-tuple-element.154), kind=kOutput, calls=%fused_computation.3 | convolution fusion | flops 135786496 | bytes 3424288 | tf_op jit(solution)/shard_map/cond/branch_1_fun/gjnqd,gnkd->gjnqk/dot_general | solution.py:61
  71.9 2.5 %bitcast_add_fusion = f32[1,4,8,128,128]{4,3,1,2,0:T(8,128)S(1)} fusion(f32[1,4,8,128,128]{4,3,1,2,0:T(8,128)S(1)} %get-tuple-element.157, f32[8,128,4,128]{3,1,2,0:T(8,128)S(1)} %get-tuple-element.472, f32[4,8,128]{2,0,1:T(4,128)S(1)} %get-tuple-element.453, f32[4,8,128]{2,0,1:T(4,128)} %bitcast.8, pred[4,8]{0,1:T(8,128)(4,1)S(1)} %copy.341, ...), kind=kOutput, calls=%fused_computation | convolution fusion | flops 137887744 | bytes 6586400 | tf_op jit(solution)/shard_map/cond/branch_1_fun/gjnqk,gnkd->gjnqd/dot_general | solution.py:69
  74.7 8.7 %conditional.7 = ((f32[1,4,8,128]{3,1,2,0:T(4,128)}, f32[1,4,8,128]{3,1,2,0:T(4,128)S(1)}, f32[1,4,8,128,128]{4,3,1,2,0:T(8,128)S(1)})) conditional(s32[]{:T(128)} %convert_element_type.71, (f32[1,4,8,128]{3,1,2,0:T(4,128)}, f32[1,4,8,128]{3,1,2,0:T(4,128)S(1)}, f32[1,4,8,128,128]{4,3,1,2,0:T(8,128)S(1)}) %get-tuple-element.542, ...), branch_computations={%region_16.17_spmd, %region_17.20_spmd} | conditional | flops 276312064 | bytes 14418112 | solution.py:128
  76.2 1.8 %fusion.36 = (f32[4,8,128]{2,0,1:T(4,128)S(1)}, f32[8,128,4,128]{3,1,2,0:T(8,128)S(1)}) fusion(pred[4,8]{0,1:T(8,128)(4,1)S(1)} %copy.345, bf16[1,4,8,128,128]{4,3,1,2,0:T(8,128)(2,1)} %copy.399, bf16[1,8,128,128]{3,2,1,0:T(8,128)(2,1)} %get-tuple-element.168), kind=kOutput, calls=%fused_computation.50 | convolution fusion | flops 135786496 | bytes 3424288 | tf_op jit(solution)/shard_map/cond/branch_1_fun/gjnqd,gnkd->gjnqk/dot_general | solution.py:61
  80.9 2.5 %bitcast_add_fusion.4 = f32[1,4,8,128,128]{4,3,1,2,0:T(8,128)S(1)} fusion(f32[1,4,8,128,128]{4,3,1,2,0:T(8,128)S(1)} %get-tuple-element.171, f32[8,128,4,128]{3,1,2,0:T(8,128)S(1)} %get-tuple-element.476, f32[4,8,128]{2,0,1:T(4,128)S(1)} %get-tuple-element.457, f32[4,8,128]{2,0,1:T(4,128)S(1)} %bitcast.551, pred[4,8]{0,1:T(8,128)(4,1)S(1)} %copy.345, ...), kind=kOutput, calls=%fused_computation.47 | convolution fusion | flops 137887744 | bytes 6586400 | tf_op jit(solution)/shard_map/cond/branch_1_fun/gjnqk,gnkd->gjnqd/dot_general | solution.py:69
  83.4 8.7 %conditional.8 = ((f32[1,4,8,128]{3,1,2,0:T(4,128)}, f32[1,4,8,128]{3,1,2,0:T(4,128)S(1)}, f32[1,4,8,128,128]{4,3,1,2,0:T(8,128)S(1)})) conditional(s32[]{:T(128)} %convert_element_type.70, (f32[1,4,8,128]{3,1,2,0:T(4,128)}, f32[1,4,8,128]{3,1,2,0:T(4,128)S(1)}, f32[1,4,8,128,128]{4,3,1,2,0:T(8,128)S(1)}) %get-tuple-element.543, ...), branch_computations={%region_20.21_spmd, %region_21.24_spmd} | conditional | flops 276312160 | bytes 14418464 | solution.py:128
  84.9 1.8 %fusion.54 = (f32[4,8,128]{2,0,1:T(4,128)S(1)}, f32[8,128,4,128]{3,1,2,0:T(8,128)S(1)}) fusion(pred[4,8]{0,1:T(8,128)(4,1)S(1)} %and_compare_fusion, bf16[8,128,128,1]{2,1,3,0:T(8,128)(2,1)} %bitcast.56, bf16[1,4,8,128,128]{4,3,1,2,0:T(8,128)(2,1)} %copy.401), kind=kOutput, calls=%fused_computation.73 | convolution fusion | flops 135786496 | bytes 3424288 | tf_op jit(solution)/shard_map/cond/branch_1_fun/gjnqd,gnkd->gjnqk/dot_general | solution.py:61
  89.6 2.5 %bitcast_add_fusion.6 = f32[1,4,8,128,128]{4,3,1,2,0:T(8,128)S(1)} fusion(f32[1,4,8,128,128]{4,3,1,2,0:T(8,128)S(1)} %get-tuple-element.178, bf16[8,128,128,1]{2,1,3,0:T(8,128)(2,1)} %bitcast.67, f32[8,128,4,128]{3,1,2,0:T(8,128)S(1)} %get-tuple-element.478, f32[4,8,128]{2,0,1:T(4,128)S(1)} %get-tuple-element.459, f32[4,8,128]{2,0,1:T(4,128)S(1)} %bitcast.553, ...), kind=kOutput, calls=%fused_computation.70 | convolution fusion | flops 137887744 | bytes 6586400 | tf_op jit(solution)/shard_map/cond/branch_1_fun/gjnqk,gnkd->gjnqd/dot_general | solution.py:69
  92.1 11.9 %conditional.9 = (f32[1,4,8,128]{3,1,2,0:T(4,128)S(1)}, f32[1,4,8,128,128]{3,4,1,2,0:T(8,128)}) conditional(s32[]{:T(128)} %convert_element_type.69, (f32[1,4,8,128]{3,1,2,0:T(4,128)S(1)}, f32[1,4,8,128,128]{4,3,1,2,0:T(8,128)S(1)}) %tuple.53, (s32[4,8]{1,0:T(4,128)S(1)}, bf16[1024,128]{1,0:T(8,128)(2,1)}, ...), branch_computations={%region_24.25_spmd, %region_25.28_spmd} | conditional | flops 276316256 | bytes 18579984 | solution.py:128
  93.7 1.8 %fusion.70 = (f32[4,8,128]{2,0,1:T(4,128)S(1)}, f32[8,128,4,128]{3,1,2,0:T(8,128)S(1)}) fusion(pred[4,8]{0,1:T(8,128)(4,1)S(1)} %and_compare_fusion.1, bf16[8,128,128,1]{2,1,3,0:T(8,128)(2,1)} %bitcast.73, bf16[1,4,8,128,128]{4,3,1,2,0:T(8,128)(2,1)} %copy.403), kind=kOutput, calls=%fused_computation.95 | convolution fusion | flops 135786496 | bytes 3424288 | tf_op jit(solution)/shard_map/cond/branch_1_fun/gjnqd,gnkd->gjnqk/dot_general | solution.py:61
  97.7 3.4 %bitcast_add_fusion.8 = f32[1,4,8,128,128]{4,3,1,2,0:T(8,128)} fusion(f32[1,4,8,128,128]{4,3,1,2,0:T(8,128)S(1)} %get-tuple-element.185, bf16[8,128,128,1]{2,1,3,0:T(8,128)(2,1)} %bitcast.84, f32[8,128,4,128]{3,1,2,0:T(8,128)S(1)} %get-tuple-element.470, f32[4,8,128]{2,0,1:T(4,128)S(1)} %get-tuple-element.467, f32[4,8,128]{2,0,1:T(4,128)S(1)} %get-tuple-element.468, ...), kind=kOutput, calls=%fused_computation.92 | convolution fusion | flops 137887744 | bytes 6586400 | tf_op jit(solution)/shard_map/cond/branch_1_fun/gjnqk,gnkd->gjnqd/dot_general | solution.py:69
  101.1 2.9 %copy.440 = f32[1,4,8,128,128]{3,4,1,2,0:T(8,128)} copy(f32[1,4,8,128,128]{4,3,1,2,0:T(8,128)} %bitcast_add_fusion.8) | data formatting | bytes 4194304 | tf_op jit(solution)/shard_map/cond | solution.py:128
  104.0 2.8 %divide_convert_fusion = bf16[1,4,8,128,128]{3,4,1,2,0:T(8,128)(2,1)} fusion(f32[1,4,8,128,128]{3,4,1,2,0:T(8,128)} %get-tuple-element.452, f32[4,8,128]{2,0,1:T(4,128)S(1)} %bitcast.545), kind=kLoop, calls=%fused_computation.123 | loop fusion | flops 1048576 | bytes 3162112 | tf_op jit(solution)/shard_map/convert_element_type | solution.py:137
  106.8 4.3 %all-to-all-start = ((bf16[8,128,512]{1,2,0:T(8,128)(2,1)}), bf16[8,128,512]{1,2,0:T(8,128)(2,1)S(1)}, u32[]{:S(2)}, u32[]{:S(2)}) async-start(bf16[8,128,512]{1,2,0:T(8,128)(2,1)} %bitcast.196), calls=%async_computation | async-start | bytes 2097152 | tf_op jit(solution)/shard_map/all_to_all | solution.py:139
  111.1 15.9 %all-to-all-done = bf16[8,128,512]{1,2,0:T(8,128)(2,1)S(1)} async-done(((bf16[8,128,512]{1,2,0:T(8,128)(2,1)}), bf16[8,128,512]{1,2,0:T(8,128)(2,1)S(1)}, u32[]{:S(2)}, u32[]{:S(2)}) %all-to-all-start) | async-done | bytes 1048608 | tf_op jit(solution)/shard_map/all_to_all | solution.py:139
  128.5 2.0 %copy.405 = f32[128,4096]{1,0:T(8,128)S(1)} copy(f32[128,4096]{0,1:T(8,128)} %bitcast.531) | data formatting | bytes 4194304 | tf_op jit(solution)/shard_map/convert_element_type | solution.py:140
  131.0 1.8 %multiply_convert_fusion = (bf16[128,4096]{1,0:T(8,128)(2,1)}, bf16[128,4096]{1,0:T(8,128)(2,1)}) fusion(f32[4096]{0:T(1024)S(1)} %convert_element_type.83, f32[128]{0:T(128)S(1)} %add_rsqrt_fusion, f32[128,4096]{1,0:T(8,128)S(1)} %copy.405, bf16[128,4096]{1,0:T(8,128)(2,1)S(1)} %copy-done.1), kind=kLoop, calls=%fused_computation.121 | loop fusion | flops 3145728 | bytes 5259776 | tf_op jit(solution)/shard_map/convert_element_type | solution.py:147
  (152 shorter events, 52.0 us)
Async XLA Ops:
  0.6 38.7 %collective-permute-start = (bf16[1024,128]{1,0:T(8,128)(2,1)}, bf16[1024,128]{1,0:T(8,128)(2,1)}, u32[]{:S(2)}, u32[]{:S(2)}) collective-permute-start(bf16[1024,128]{1,0:T(8,128)(2,1)} %param.17), channel_id=1, source_target_pairs={{0,8},{8,16},{16,24},{24,32},{32,40},{40,48},{48,56},{56,64},{64,7... | collective-permute-start | bytes 786440 | tf_op jit(solution)/shard_map/ppermute | solution.py:17
  3.6 38.4 %collective-permute-start.2 = (bf16[1024,128]{1,0:T(8,128)(2,1)}, bf16[1024,128]{1,0:T(8,128)(2,1)}, u32[]{:S(2)}, u32[]{:S(2)}) collective-permute-start(bf16[1024,128]{1,0:T(8,128)(2,1)} %param.17), channel_id=1, source_target_pairs={{0,16},{8,24},{16,32},{24,40},{32,48},{40,56},{48,64},{56,72},{64,... | collective-permute-start | bytes 786440 | tf_op jit(solution)/shard_map/ppermute | solution.py:17
  5.5 35.1 %collective-permute-start.1 = (bf16[1024,128]{1,0:T(8,128)(2,1)}, bf16[1024,128]{1,0:T(8,128)(2,1)}, u32[]{:S(2)}, u32[]{:S(2)}) collective-permute-start(bf16[1024,128]{1,0:T(8,128)(2,1)} %param.18), channel_id=1, source_target_pairs={{0,8},{8,16},{16,24},{24,32},{32,40},{40,48},{48,56},{56,64},{64,7... | collective-permute-start | bytes 786440 | tf_op jit(solution)/shard_map/ppermute | solution.py:17
  7.8 55.3 %collective-permute-start.3 = (bf16[1024,128]{1,0:T(8,128)(2,1)}, bf16[1024,128]{1,0:T(8,128)(2,1)}, u32[]{:S(2)}, u32[]{:S(2)}) collective-permute-start(bf16[1024,128]{1,0:T(8,128)(2,1)} %param.18), channel_id=1, source_target_pairs={{0,16},{8,24},{16,32},{24,40},{32,48},{40,56},{48,64},{56,72},{64,... | collective-permute-start | bytes 786440 | tf_op jit(solution)/shard_map/ppermute | solution.py:17
  9.7 54.7 %collective-permute-start.4 = (bf16[1024,128]{1,0:T(8,128)(2,1)}, bf16[1024,128]{1,0:T(8,128)(2,1)}, u32[]{:S(2)}, u32[]{:S(2)}) collective-permute-start(bf16[1024,128]{1,0:T(8,128)(2,1)} %param.17), channel_id=1, source_target_pairs={{0,32},{8,40},{16,48},{24,56},{32,64},{40,72},{48,80},{56,88},{64,... | collective-permute-start | bytes 786440 | tf_op jit(solution)/shard_map/ppermute | solution.py:17
  12.4 2.1 %copy-start.11 = (s32[4,8]{1,0:T(4,128)S(1)}, s32[4,8]{1,0:T(4,128)}, u32[]{:S(2)}) copy-start(s32[4,8]{1,0:T(4,128)} %param.19) | copy-start | bytes 388
  12.4 2.8 %copy-start.4 = (bf16[1024,128]{1,0:T(8,128)(2,1)S(1)}, bf16[1024,128]{1,0:T(8,128)(2,1)}, u32[]{:S(2)}) copy-start(bf16[1024,128]{1,0:T(8,128)(2,1)} %param.17) | copy-start | bytes 786436
  18.2 3.3 %copy-start.3 = (bf16[8,128,1,4,128]{4,1,0,3,2:T(8,128)(2,1)S(1)}, bf16[8,128,1,4,128]{4,1,0,3,2:T(8,128)(2,1)}, u32[]{:S(2)}) copy-start(bf16[8,128,1,4,128]{4,1,0,3,2:T(8,128)(2,1)} %copy.435) | copy-start | bytes 3145732
  18.8 2.6 %copy-start.5 = (f32[4,8,128]{2,0,1:T(4,128)}, f32[4,8,128]{2,0,1:T(4,128)S(1)}, u32[]{:S(2)}) copy-start(f32[4,8,128]{2,0,1:T(4,128)S(1)} %get-tuple-element.488) | copy-start | bytes 49156
  21.4 3.1 %copy-start.9 = (f32[1,4,4,2,1,128]{5,1,2,4,3,0:T(4,128)S(1)}, f32[1,4,4,2,1,128]{5,1,2,4,3,0:T(4,128)}, u32[]{:S(2)}) copy-start(f32[1,4,4,2,1,128]{5,1,2,4,3,0:T(4,128)} %get-tuple-element.500) | copy-start | bytes 49156
  21.4 3.1 %copy-start.10 = (f32[1,4,4,2,1,128]{5,1,2,4,3,0:T(4,128)S(1)}, f32[1,4,4,2,1,128]{5,1,2,4,3,0:T(4,128)}, u32[]{:S(2)}) copy-start(f32[1,4,4,2,1,128]{5,1,2,4,3,0:T(4,128)} %get-tuple-element.499) | copy-start | bytes 49156
  21.4 4.6 %copy-start.14 = (f32[1,4,2,2,1,128]{5,4,2,1,3,0:T(1,128)S(1)}, f32[1,4,2,2,1,128]{5,4,2,1,3,0:T(1,128)}, u32[]{:S(2)}) copy-start(f32[1,4,2,2,1,128]{5,4,2,1,3,0:T(1,128)} %copy.359) | copy-start | bytes 24580
  21.5 4.6 %copy-start.18 = (pred[4,4]{0,1:T(4,128)(4,1)S(1)}, pred[4,4]{0,1:T(4,128)(4,1)}, u32[]{:S(2)}) copy-start(pred[4,4]{0,1:T(4,128)(4,1)} %eq.76) | copy-start | bytes 52
  23.7 2.7 %copy-start.7 = (f32[4,4,128]{2,0,1:T(4,128)}, f32[4,4,128]{2,0,1:T(4,128)S(1)}, u32[]{:S(2)}) copy-start(f32[4,4,128]{2,0,1:T(4,128)S(1)} %get-tuple-element.462) | copy-start | bytes 24580
  26.0 2.1 %copy-start.6 = (f32[4,8,128]{2,0,1:T(4,128)S(1)}, f32[4,8,128]{2,0,1:T(4,128)}, u32[]{:S(2)}) copy-start(f32[4,8,128]{2,0,1:T(4,128)} %copy-done.5) | copy-start | bytes 49156
  26.0 2.1 %copy-start.15 = (f32[4,8,128]{2,0,1:T(4,128)S(1)}, f32[4,8,128]{2,0,1:T(4,128)}, u32[]{:S(2)}) copy-start(f32[4,8,128]{2,0,1:T(4,128)} %get-tuple-element.487) | copy-start | bytes 49156
  39.1 26.7 %copy-start.12 = (s32[4,8]{1,0:T(4,128)S(1)}, s32[4,8]{1,0:T(4,128)}, u32[]{:S(2)}) copy-start(s32[4,8]{1,0:T(4,128)} %param.19) | copy-start | bytes 388
  39.3 35.3 %collective-permute-start.5 = (bf16[1024,128]{1,0:T(8,128)(2,1)}, bf16[1024,128]{1,0:T(8,128)(2,1)}, u32[]{:S(2)}, u32[]{:S(2)}) collective-permute-start(bf16[1024,128]{1,0:T(8,128)(2,1)} %param.18), channel_id=1, source_target_pairs={{0,32},{8,40},{16,48},{24,56},{32,64},{40,72},{48,80},{56,88},{64,... | collective-permute-start | bytes 786440 | tf_op jit(solution)/shard_map/ppermute | solution.py:17
  40.7 42.7 %collective-permute-start.6 = (bf16[1024,128]{1,0:T(8,128)(2,1)S(1)}, bf16[1024,128]{1,0:T(8,128)(2,1)}, u32[]{:S(2)}, u32[]{:S(2)}) collective-permute-start(bf16[1024,128]{1,0:T(8,128)(2,1)S(1)} %copy-done.4), channel_id=1, source_target_pairs={{0,64},{8,72},{16,80},{24,88},{32,96},{40,104},{48,112},{56,120},{... | collective-permute-start | bytes 786440 | tf_op jit(solution)/shard_map/ppermute | solution.py:17
  42.0 41.4 %collective-permute-start.7 = (bf16[1024,128]{1,0:T(8,128)(2,1)}, bf16[1024,128]{1,0:T(8,128)(2,1)}, u32[]{:S(2)}, u32[]{:S(2)}) collective-permute-start(bf16[1024,128]{1,0:T(8,128)(2,1)} %param.18), channel_id=1, source_target_pairs={{0,64},{8,72},{16,80},{24,88},{32,96},{40,104},{48,112},{56,120},{... | collective-permute-start | bytes 786440 | tf_op jit(solution)/shard_map/ppermute | solution.py:17
  63.1 29.0 %collective-permute-start.8 = (bf16[1024,128]{1,0:T(8,128)(2,1)S(1)}, bf16[1024,128]{1,0:T(8,128)(2,1)}, u32[]{:S(2)}, u32[]{:S(2)}) collective-permute-start(bf16[1024,128]{1,0:T(8,128)(2,1)S(1)} %copy-done.4), channel_id=1, source_target_pairs={{0,128},{8,136},{16,144},{24,152},{32,160},{40,168},{48,176},{56,1... | collective-permute-start | bytes 786440 | tf_op jit(solution)/shard_map/ppermute | solution.py:17
  64.4 27.7 %collective-permute-start.9 = (bf16[1024,128]{1,0:T(8,128)(2,1)}, bf16[1024,128]{1,0:T(8,128)(2,1)}, u32[]{:S(2)}, u32[]{:S(2)}) collective-permute-start(bf16[1024,128]{1,0:T(8,128)(2,1)} %param.18), channel_id=1, source_target_pairs={{0,128},{8,136},{16,144},{24,152},{32,160},{40,168},{48,176},{56,1... | collective-permute-start | bytes 786440 | tf_op jit(solution)/shard_map/ppermute | solution.py:17
  104.0 7.1 %copy-start.17 = (bf16[4096]{0:T(1024)(128)(2,1)S(1)}, bf16[4096]{0:T(1024)(128)(2,1)}, u32[]{:S(2)}) copy-start(bf16[4096]{0:T(1024)(128)(2,1)} %param.21) | copy-start | bytes 24580
  106.8 20.2 %all-to-all-start = ((bf16[8,128,512]{1,2,0:T(8,128)(2,1)}), bf16[8,128,512]{1,2,0:T(8,128)(2,1)S(1)}, u32[]{:S(2)}, u32[]{:S(2)}) async-start(bf16[8,128,512]{1,2,0:T(8,128)(2,1)} %bitcast.196), calls=%async_computation | async-start | bytes 2097152 | tf_op jit(solution)/shard_map/all_to_all | solution.py:139
  (8 other events, 10.4 us)
where the time goes:
time: 134 us; the launch traced here: 133 us
  waiting for transfers between devices  35.8 us (27%)
  matrix products  27.8 us (21%)
  local copies, waits for them, and re-layouts  25.1 us (19%)
  other arithmetic  21.2 us (16%)
  starting transfers between devices  21.1 us (16%)
  between operations  1.37 us (1%)
    ppermute x10, waiting for transfers between devices, passed_along(): return lax.ppermute(block, axis, route)  19.9 us
    dot_general x8, matrix products, update(): jnp.einsum('gjnqk,gnkd->gjnqd', weights.astype(jnp.bfloat16), value_part,...  17.6 us
    ppermute x10, starting transfers between devices, passed_along(): return lax.ppermute(block, axis, route)  16.8 us
    all_to_all x1, waiting for transfers between devices, shards(): lax.all_to_all(attended, 'head', split_axis=0, concat_axis=1, tiled=True)  15.9 us
    dot_general x8, matrix products, update(): jnp.einsum('gjnqd,gnkd->gjnqk', query_part, key_part, preferred_element_t...  10.2 us
    another operation x6, local copies, waits for them, and re-layouts  5.96 us
    reduce_sum x8, other arithmetic, update(): new_sum = row_sum * factor + weights.sum(-1)  5.53 us
    all_to_all x1, starting transfers between devices, shards(): lax.all_to_all(attended, 'head', split_axis=0, concat_axis=1, tiled=True)  4.3 us
  transfers between devices with their start and end apart: 11, of which 2 were waited for; matrix products, arithmetic and copies ran while one was open for 39% of the time, Pallas kernels for 0%

commit v1 on v0

v1 whole, which is shorter than its diff:
```python
import functools

import jax
import jax.numpy as jnp
from jax import lax
from jax.experimental import pallas as pl
from jax.experimental.pallas import tpu as pltpu
from jax.sharding import PartitionSpec as P

DH = 128
BLOCK = 128
EPSILON = 1e-05
NEG = -1e30
KERNEL_VMEM = 16 * 2**20
SCALE = DH ** (-0.5) * 1.4426950408889634
LATE = 2


def pairs(size, bit):
    return [(i - 2**bit, i) for i in range(size) if (i >> bit) & 1]


def params():
    return pltpu.CompilerParams(vmem_limit_bytes=KERNEL_VMEM)


def rows_at(index):
    return pl.ds(pl.multiple_of(index * BLOCK, BLOCK), BLOCK)


def column(tile, lane):
    return tile[:, lane : lane + 1]


def scores_of(q, k):
    return lax.dot_general(q, k, (((1,), (1,)), ((), ())), preferred_element_type=jnp.float32) * SCALE


def order_kernel(place_ref, k_ref, v_ref, all_ref, late_ref, rest_ref):
    blocks = k_ref.shape[0] // BLOCK
    for n in range(blocks):
        source = rows_at(place_ref[0] ^ n)
        key, val = k_ref[source, :], v_ref[source, :]
        part, at = (late_ref, n) if n < LATE else (rest_ref, n - LATE)
        for ref, first in ((all_ref, n), (part, at)):
            ref[first * BLOCK : (first + 1) * BLOCK, :DH] = key
            ref[first * BLOCK : (first + 1) * BLOCK, DH:] = val


def ordered(place, keys, values):
    rows = keys.shape[0]
    vmem = pl.BlockSpec(memory_space=pltpu.VMEM)
    return pl.pallas_call(
        order_kernel,
        in_specs=[pl.BlockSpec(memory_space=pltpu.SMEM), vmem, vmem],
        out_specs=[vmem] * 3,
        out_shape=[
            jax.ShapeDtypeStruct((n, 2 * DH), jnp.bfloat16)
            for n in (rows, LATE * BLOCK, rows - LATE * BLOCK)
        ],
        compiler_params=params(),
        name="order",
    )(place, keys, values)


def attend(q, keys, vals, biases, causal=None, before=None):
    s = scores_of(q, jnp.concatenate(keys, 0))
    parts = []
    for n, bias in enumerate(biases):
        part = s[:, n * BLOCK : (n + 1) * BLOCK]
        parts.append(jnp.where(causal, part, NEG) if bias is None else part + bias)
    top = functools.reduce(jnp.maximum, parts).max(-1, keepdims=True)
    if before is not None:
        top = jnp.maximum(top, before[1])
    weights = [jnp.exp2(part - top) for part in parts]
    total = functools.reduce(jnp.add, weights).sum(-1, keepdims=True)
    weight = jnp.concatenate([w.astype(jnp.bfloat16) for w in weights], 1)
    summed = jnp.dot(weight, jnp.concatenate(vals, 0), preferred_element_type=jnp.float32)
    if before is not None:
        factor = jnp.exp2(before[1] - top)
        total = total + factor
        summed = summed + before[0] * factor
    return summed / total, top + jnp.log2(total)


def bias_of(bitmap, level):
    allowed = lax.shift_right_logical(bitmap, level) & 1
    return (1 - allowed).astype(jnp.float32) * NEG


def local_kernel(heads, levels, place_ref, mask_ref, q_ref, kv_ref, part_ref, stat_ref):
    n = pl.program_id(0)
    j = place_ref[0] ^ n
    bits = [lax.shift_right_logical(j, b) & 1 for b in range(levels)]
    count = sum(bits)
    lanes = lax.broadcasted_iota(jnp.int32, (BLOCK, BLOCK), 1)
    causal = lax.broadcasted_iota(jnp.int32, (BLOCK, BLOCK), 0) >= lanes

    def body(number):
        chosen = []
        for at in range(number):
            level, seen = 0, 0
            for b, bit in enumerate(bits):
                level = level + jnp.where((bit == 1) & (seen == at), b, 0)
                seen = seen + bit
            chosen.append(level)
        blocks = [kv_ref[rows_at(n), :]]
        for level in chosen:
            blocks.append(kv_ref[rows_at(n ^ lax.shift_left(jnp.int32(1), level)), :])
        keys, vals = [b[:, :DH] for b in blocks], [b[:, DH:] for b in blocks]
        stats = jnp.zeros((BLOCK, BLOCK), jnp.float32)
        for h in range(heads):
            at = slice(h * DH, (h + 1) * DH)
            biases = [None] + [bias_of(mask_ref[h, j], level) for level in chosen]
            result, logsum = attend(q_ref[:, at], keys, vals, biases, causal)
            part_ref[0, :, at] = result
            stats = jnp.where(lanes == h, logsum, stats)
        stat_ref[0] = stats

    for number in range(levels + 1):
        pl.when(count == number)(functools.partial(body, number))


def local_part(place, block_masks, queries, kv):
    tokens, width = queries.shape
    heads, blocks = block_masks.shape
    return pl.pallas_call(
        functools.partial(local_kernel, heads, blocks.bit_length() - 1),
        grid_spec=pltpu.PrefetchScalarGridSpec(
            num_scalar_prefetch=2,
            grid=(blocks,),
            in_specs=[
                pl.BlockSpec((BLOCK, width), lambda n, place, mask: (place[0] ^ n, 0)),
                pl.BlockSpec(kv.shape, lambda n, place, mask: (0, 0)),
            ],
            out_specs=[
                pl.BlockSpec((1, BLOCK, width), lambda n, place, mask: (n, 0, 0)),
                pl.BlockSpec((1, BLOCK, BLOCK), lambda n, place, mask: (n, 0, 0)),
            ],
        ),
        out_shape=[
            jax.ShapeDtypeStruct((blocks, BLOCK, width), jnp.float32),
            jax.ShapeDtypeStruct((blocks, BLOCK, BLOCK), jnp.float32),
        ],
        cost_estimate=pl.CostEstimate(
            flops=3 * 4 * tokens * width * BLOCK, bytes_accessed=4_000_000, transcendentals=3 * tokens * heads * BLOCK
        ),
        compiler_params=params(),
        name="local",
    )(place, block_masks, queries, kv)


def far_kernel(heads, levels, first, final, place_ref, mask_ref, q_ref, part_ref, stat_ref, *refs):
    kv_refs, outs = refs[: len(levels)], refs[len(levels) :]
    i = pl.program_id(0)
    j = place_ref[0] ^ (i + first)
    lanes = lax.broadcasted_iota(jnp.int32, (BLOCK, BLOCK), 1)
    keys = [ref[:, :DH] for ref in kv_refs]
    vals = [ref[:, DH:] for ref in kv_refs]
    stats = stat_ref[0]
    new = jnp.zeros((BLOCK, BLOCK), jnp.float32)
    results = []
    for h in range(heads):
        at = slice(h * DH, (h + 1) * DH)
        bitmap = mask_ref[h, j] & place_ref[1]
        biases = [bias_of(bitmap, level) for level in levels]
        result, logsum = attend(q_ref[:, at], keys, vals, biases, None, (part_ref[0, :, at], column(stats, h)))
        if final:
            results.append(result.astype(jnp.bfloat16))
        else:
            outs[0][0, :, at] = result
            new = jnp.where(lanes == h, logsum, new)
    if final:
        whole = jnp.concatenate(results, 1)
        for n, out in enumerate(outs):

            @pl.when(i == n)
            def _(out=out):
                out[...] = whole
    else:
        outs[1][0] = new


def far_part(place, block_masks, queries, part, stats, kvs, levels, first, count, final):
    tokens, width = queries.shape
    heads, blocks = block_masks.shape

    def blocked(array):
        held = array.shape[0]
        offset = first if held == blocks else 0
        return pl.BlockSpec((1,) + array.shape[1:], lambda i, place, mask: (i + offset, 0, 0))

    def keyed(array):
        offset = first if array.shape[0] == tokens else 0
        return pl.BlockSpec((BLOCK, 2 * DH), lambda i, place, mask: (i + offset, 0))

    if final:
        out_specs = [pl.BlockSpec((BLOCK, width), lambda i, place, mask: (0, 0))] * count
        out_shape = [jax.ShapeDtypeStruct((BLOCK, width), jnp.bfloat16)] * count
    else:
        out_specs = [
            pl.BlockSpec((1, BLOCK, width), lambda i, place, mask: (i, 0, 0)),
            pl.BlockSpec((1, BLOCK, BLOCK), lambda i, place, mask: (i, 0, 0)),
        ]
        out_shape = [
            jax.ShapeDtypeStruct((count, BLOCK, width), jnp.float32),
            jax.ShapeDtypeStruct((count, BLOCK, BLOCK), jnp.float32),
        ]
    return pl.pallas_call(
        functools.partial(far_kernel, heads, levels, first, final),
        grid_spec=pltpu.PrefetchScalarGridSpec(
            num_scalar_prefetch=2,
            grid=(count,),
            in_specs=[
                pl.BlockSpec((BLOCK, width), lambda i, place, mask: (place[0] ^ (i + first), 0)),
                blocked(part),
                blocked(stats),
            ]
            + [keyed(kv) for kv in kvs],
            out_specs=out_specs,
        ),
        out_shape=out_shape,
        cost_estimate=pl.CostEstimate(
            flops=len(kvs) * 4 * count * BLOCK * width * BLOCK,
            bytes_accessed=4_000_000,
            transcendentals=len(kvs) * count * heads * BLOCK * BLOCK,
        ),
        compiler_params=params(),
        name="far",
    )(place, block_masks, queries, part, stats, *kvs)


def norm_kernel(groups, place_ref, *refs):
    parts = refs[:groups]
    res_ref, gain_ref, stream_ref, normed_ref, whole = refs[groups:]
    width = parts[0].shape[1]
    square = jnp.zeros((BLOCK, DH), jnp.float32)
    for n in range(groups):
        cols = pl.ds(pl.multiple_of((place_ref[0] ^ n) * width, width), width)
        summed = res_ref[:, cols].astype(jnp.float32) + parts[n][...].astype(jnp.float32)
        stream_ref[:, cols] = summed.astype(jnp.bfloat16)
        whole[:, cols] = summed
        for c in range(0, width, DH):
            piece = summed[:, c : c + DH]
            square = square + piece * piece
    mean = square.sum(-1, keepdims=True) / (groups * width)
    factor = lax.rsqrt(mean + EPSILON)
    for n in range(groups):
        cols = slice(n * width, (n + 1) * width)
        normed_ref[:, cols] = (whole[:, cols] * factor * gain_ref[:, cols].astype(jnp.float32)).astype(jnp.bfloat16)


def norm_part(place, parts, residual, gain):
    vmem = pl.BlockSpec(memory_space=pltpu.VMEM)
    return pl.pallas_call(
        functools.partial(norm_kernel, len(parts)),
        in_specs=[pl.BlockSpec(memory_space=pltpu.SMEM)] + [vmem] * (len(parts) + 2),
        out_specs=[vmem] * 2,
        out_shape=[jax.ShapeDtypeStruct(residual.shape, jnp.bfloat16)] * 2,
        scratch_shapes=[pltpu.VMEM(residual.shape, jnp.float32)],
        cost_estimate=pl.CostEstimate(flops=4_000_000, bytes_accessed=4_000_000, transcendentals=128),
        compiler_params=params(),
        name="norm",
    )(place, *parts, residual, gain)


def shards(queries, keys, values, block_masks, residual, norm_gain):
    _, blocks = block_masks.shape
    ctx_size = lax.axis_size("ctx")
    groups = lax.axis_size("head")
    local_bits = blocks.bit_length() - 1
    place = jnp.stack([lax.axis_index("head"), lax.axis_index("ctx") * blocks]).astype(jnp.int32)

    def fetched(array, bit):
        return lax.ppermute(array, "ctx", pairs(ctx_size, bit))

    def swapped(array, n):
        return lax.ppermute(array, "head", [(i, i ^ n) for i in range(groups)])

    def level(bits):
        return [local_bits + b for b in bits]

    kv, kv_late, kv_rest = ordered(place, keys, values)
    rest = {b: fetched(kv_rest, b) for b in (2, 1, 0)}
    far = {b: fetched(kv, b) for b in (4, 3)}
    late = {b: fetched(kv_late, b) for b in (2, 1, 0)}
    part, stats = local_part(place, block_masks, queries, kv)
    part, stats = far_part(place, block_masks, queries, part, stats, [far[4], far[3]], level((4, 3)), 0, blocks, False)
    sent = far_part(
        place,
        block_masks,
        queries,
        part,
        stats,
        [rest[b] for b in (2, 1, 0)],
        level((2, 1, 0)),
        LATE,
        blocks - LATE,
        True,
    )
    kept = far_part(
        place,
        block_masks,
        queries,
        part,
        stats,
        [late[b] for b in (2, 1, 0)],
        level((2, 1, 0)),
        0,
        LATE,
        True,
    )
    parts = [kept[0]] + [swapped(kept[n], n) for n in range(1, LATE)]
    parts += [swapped(sent[n - LATE], n) for n in range(LATE, blocks)]
    return norm_part(place, parts, residual, norm_gain.reshape(1, -1))


def solution(mesh):
    in_specs = (
        P("ctx", "head"),
        P("ctx", "head"),
        P("ctx", "head"),
        P("head", "ctx"),
        P(("ctx", "head"), None),
        P(),
    )
    out_specs = (P(("ctx", "head"), None), P(("ctx", "head"), None))
    return jax.shard_map(shards, mesh=mesh, in_specs=in_specs, out_specs=out_specs, check_vma=False)
```

time: 134 us -> 90.8 us (0.68)
  the two profiles are of different devices: /device:TPU:184 before, /device:TPU:97 now
where the time goes in v1:
time: 90.8 us; the launch traced here: 90.4 us
  Pallas kernels  37.7 us (42%)
  starting transfers between devices  29.7 us (33%)
  waiting for transfers between devices  18.3 us (20%)
  local copies, waits for them, and re-layouts  3.83 us (4%)
    pallas_call x3, Pallas kernels, far_part(): pl.pallas_call(functools.partial(far_kernel, heads, levels, first, final)...  25.8 us
    ppermute x8, starting transfers between devices, fetched(): return lax.ppermute(array, 'ctx', pairs(ctx_size, bit))  19.8 us
    ppermute x8, waiting for transfers between devices, fetched(): return lax.ppermute(array, 'ctx', pairs(ctx_size, bit))  11.6 us
    ppermute x7, starting transfers between devices, swapped(): return lax.ppermute(array, 'head', [(i, i ^ n) for i in range(groups)])  9.94 us
    pallas_call x1, Pallas kernels, local_part(): pl.pallas_call(functools.partial(local_kernel, heads, blocks.bit_length()...  8.72 us
    ppermute x7, waiting for transfers between devices, swapped(): return lax.ppermute(array, 'head', [(i, i ^ n) for i in range(groups)])  6.67 us
    unnamed x16, local copies, waits for them, and re-layouts  3.82 us
    pallas_call x1, Pallas kernels, norm_part(): pl.pallas_call(functools.partial(norm_kernel, len(parts)), in_specs=[pl.B...  2.45 us
  transfers between devices with their start and end apart: 15, of which 5 were waited for; matrix products, arithmetic and copies ran while one was open for 0% of the time, Pallas kernels for 38%

profile of v1, /device:TPU:97, one launch (start us, length us, event | category | flops | bytes accessed | tf_op | source)
XLA Modules:
  0.0 90.4 jit_solution(14084430766897206912)
XLA Ops:
  0.7 0.9 %copy-done.3 = bf16[1024,128]{1,0:T(8,128)(2,1)S(1)} copy-done((bf16[1024,128]{1,0:T(8,128)(2,1)S(1)}, bf16[1024,128]{1,0:T(8,128)(2,1)}, u32[]{:S(2)}) %copy-start.3) | copy-done | bytes 262168
  1.7 0.9 %copy-done.4 = bf16[1024,128]{1,0:T(8,128)(2,1)S(1)} copy-done((bf16[1024,128]{1,0:T(8,128)(2,1)S(1)}, bf16[1024,128]{1,0:T(8,128)(2,1)}, u32[]{:S(2)}) %copy-start.4) | copy-done | bytes 262168
  3.3 4.9 %collective-permute-start = (bf16[1024,256]{1,0:T(8,128)(2,1)S(1)}, bf16[1024,256]{1,0:T(8,128)(2,1)S(1)}, u32[]{:S(2)}, u32[]{:S(2)}) collective-permute-start(bf16[1024,256]{1,0:T(8,128)(2,1)S(1)} %get-tuple-element.17.kv_ref), channel_id=1, source_target_pairs={{0,128},{8,136},{16,144},{24,152},{32,160},{40,168},{48,176},{56,1... | collective-permute-start | bytes 1572872 | tf_op jit(solution)/shard_map/ppermute | solution.py:275
  8.2 2.3 %collective-permute-start.1 = (bf16[1024,256]{1,0:T(8,128)(2,1)S(1)}, bf16[1024,256]{1,0:T(8,128)(2,1)S(1)}, u32[]{:S(2)}, u32[]{:S(2)}) collective-permute-start(bf16[1024,256]{1,0:T(8,128)(2,1)S(1)} %get-tuple-element.17.kv_ref), channel_id=1, source_target_pairs={{0,64},{8,72},{16,80},{24,88},{32,96},{40,104},{48,112},{56,120},{... | collective-permute-start | bytes 1572872 | tf_op jit(solution)/shard_map/ppermute | solution.py:275
  10.5 6.1 %collective-permute-start.6 = (bf16[768,256]{1,0:T(8,128)(2,1)S(1)}, bf16[768,256]{1,0:T(8,128)(2,1)S(1)}, u32[]{:S(2)}, u32[]{:S(2)}) collective-permute-start(bf16[768,256]{1,0:T(8,128)(2,1)S(1)} %get-tuple-element.25), channel_id=1, source_target_pairs={{0,32},{8,40},{16,48},{24,56},{64,96},{72,104},{80,112},{88,120},{... | collective-permute-start | bytes 1179656 | tf_op jit(solution)/shard_map/ppermute | solution.py:275
  16.7 1.3 %collective-permute-start.7 = (bf16[768,256]{1,0:T(8,128)(2,1)S(1)}, bf16[768,256]{1,0:T(8,128)(2,1)S(1)}, u32[]{:S(2)}, u32[]{:S(2)}) collective-permute-start(bf16[768,256]{1,0:T(8,128)(2,1)S(1)} %get-tuple-element.25), channel_id=1, source_target_pairs={{0,16},{8,24},{32,48},{40,56},{64,80},{72,88},{96,112},{104,120},{... | collective-permute-start | bytes 1179656 | tf_op jit(solution)/shard_map/ppermute | solution.py:275
  18.0 1.3 %collective-permute-start.8 = (bf16[768,256]{1,0:T(8,128)(2,1)S(1)}, bf16[768,256]{1,0:T(8,128)(2,1)S(1)}, u32[]{:S(2)}, u32[]{:S(2)}) collective-permute-start(bf16[768,256]{1,0:T(8,128)(2,1)S(1)} %get-tuple-element.25), channel_id=1, source_target_pairs={{0,8},{16,24},{32,40},{48,56},{64,72},{80,88},{96,104},{112,120},{... | collective-permute-start | bytes 1179656 | tf_op jit(solution)/shard_map/ppermute | solution.py:275
  19.3 1.2 %copy-done = bf16[1024,512]{1,0:T(8,128)(2,1)S(1)} copy-done((bf16[1024,512]{1,0:T(8,128)(2,1)S(1)}, bf16[1024,512]{1,0:T(8,128)(2,1)}, u32[]{:S(2)}) %copy-start) | copy-done | bytes 1048600
  21.2 8.7 %local.1 = (f32[8,128,512]{2,1,0:T(8,128)S(1)}, f32[8,128,128]{2,1,0:T(8,128)S(1)}) custom-call(s32[2]{0:T(128)S(1)} %pad_add_fusion.place_ref, s32[4,8]{1,0:T(4,128)S(1)} %copy-done.5, bf16[1024,512]{1,0:T(8,128)(2,1)S(1)} %copy-done, bf16[1024,256]{1,0:T(8,128)(2,1)S(1)} %get-tuple-element.17.kv_ref), custom_call_target="tpu_custom_call" | custom-call | flops 805306368 | bytes 4000000 | tf_op jit(solution)/shard_map/local/pallas_call | solution.py:127
  29.9 1.3 %collective-permute-start.2 = (bf16[256,256]{1,0:T(8,128)(2,1)S(1)}, bf16[256,256]{1,0:T(8,128)(2,1)S(1)}, u32[]{:S(2)}, u32[]{:S(2)}) collective-permute-start(bf16[256,256]{1,0:T(8,128)(2,1)S(1)} %get-tuple-element.22), channel_id=1, source_target_pairs={{0,32},{8,40},{16,48},{24,56},{64,96},{72,104},{80,112},{88,120},{... | collective-permute-start | bytes 393224 | tf_op jit(solution)/shard_map/ppermute | solution.py:275
  31.2 1.3 %collective-permute-start.3 = (bf16[256,256]{1,0:T(8,128)(2,1)S(1)}, bf16[256,256]{1,0:T(8,128)(2,1)S(1)}, u32[]{:S(2)}, u32[]{:S(2)}) collective-permute-start(bf16[256,256]{1,0:T(8,128)(2,1)S(1)} %get-tuple-element.22), channel_id=1, source_target_pairs={{0,16},{8,24},{32,48},{40,56},{64,80},{72,88},{96,112},{104,120},{... | collective-permute-start | bytes 393224 | tf_op jit(solution)/shard_map/ppermute | solution.py:275
  32.5 11.5 %far.3 = (f32[8,128,512]{2,1,0:T(8,128)S(1)}, f32[8,128,128]{2,1,0:T(8,128)S(1)}) custom-call(s32[2]{0:T(128)S(1)} %pad_add_fusion.place_ref, s32[4,8]{1,0:T(4,128)S(1)} %copy-done.5, bf16[1024,512]{1,0:T(8,128)(2,1)S(1)} %copy-done.1, f32[8,128,512]{2,1,0:T(8,128)S(1)} %get-tuple-element.18.part_ref, f32[8,128,128]{2,1,0:T(8,128)S(1)} %get-tuple-element.19.stat_ref, ...), custom_call_target="tpu_custom_call" | custom-call | flops 536870912 | bytes 4000000 | tf_op jit(solution)/shard_map/far/pallas_call | solution.py:209
  44.1 1.3 %collective-permute-start.4 = (bf16[256,256]{1,0:T(8,128)(2,1)S(1)}, bf16[256,256]{1,0:T(8,128)(2,1)S(1)}, u32[]{:S(2)}, u32[]{:S(2)}) collective-permute-start(bf16[256,256]{1,0:T(8,128)(2,1)S(1)} %get-tuple-element.22), channel_id=1, source_target_pairs={{0,8},{16,24},{32,40},{48,56},{64,72},{80,88},{96,104},{112,120},{... | collective-permute-start | bytes 393224 | tf_op jit(solution)/shard_map/ppermute | solution.py:275
  45.4 1.0 %collective-permute-done.7.refs_1_ = bf16[768,256]{1,0:T(8,128)(2,1)S(1)} collective-permute-done((bf16[768,256]{1,0:T(8,128)(2,1)S(1)}, bf16[768,256]{1,0:T(8,128)(2,1)S(1)}, u32[]{:S(2)}, u32[]{:S(2)}) %collective-permute-start.7) | collective-permute-done | bytes 393248 | tf_op jit(solution)/shard_map/ppermute | solution.py:275
  46.3 10.6 %collective-permute-done.8.refs_2_ = bf16[768,256]{1,0:T(8,128)(2,1)S(1)} collective-permute-done((bf16[768,256]{1,0:T(8,128)(2,1)S(1)}, bf16[768,256]{1,0:T(8,128)(2,1)S(1)}, u32[]{:S(2)}, u32[]{:S(2)}) %collective-permute-start.8) | collective-permute-done | bytes 393248 | tf_op jit(solution)/shard_map/ppermute | solution.py:275
  56.9 10.5 %far.5 = (bf16[128,512]{1,0:T(8,128)(2,1)S(1)}, bf16[128,512]{1,0:T(8,128)(2,1)S(1)}, bf16[128,512]{1,0:T(8,128)(2,1)S(1)}, bf16[128,512]{1,0:T(8,128)(2,1)S(1)}...) custom-call(s32[2]{0:T(128)S(1)} %pad_add_fusion.place_ref, s32[4,8]{1,0:T(4,128)S(1)} %copy-done.5, ...), custom_call_target="tpu_custom_call" | custom-call | flops 603979776 | bytes 4000000 | tf_op jit(solution)/shard_map/far/pallas_call | solution.py:209
  67.4 3.5 %collective-permute-start.10 = (bf16[128,512]{1,0:T(8,128)(2,1)S(1)}, bf16[128,512]{1,0:T(8,128)(2,1)S(1)}, u32[]{:S(2)}, u32[]{:S(2)}) collective-permute-start(bf16[128,512]{1,0:T(8,128)(2,1)S(1)} %get-tuple-element.27), channel_id=1, source_target_pairs={{0,3},{1,2},{2,1},{3,0},{4,7},{5,6},{6,5},{7,4},{8,11},{9,10},{10,... | collective-permute-start | bytes 393224 | tf_op jit(solution)/shard_map/ppermute | solution.py:278
  71.0 2.5 %collective-permute-start.11 = (bf16[128,512]{1,0:T(8,128)(2,1)S(1)}, bf16[128,512]{1,0:T(8,128)(2,1)S(1)}, u32[]{:S(2)}, u32[]{:S(2)}) collective-permute-start(bf16[128,512]{1,0:T(8,128)(2,1)S(1)} %get-tuple-element.28), channel_id=1, source_target_pairs={{0,4},{1,5},{2,6},{3,7},{4,0},{5,1},{6,2},{7,3},{8,12},{9,13},{10,... | collective-permute-start | bytes 393224 | tf_op jit(solution)/shard_map/ppermute | solution.py:278
  73.4 2.2 %collective-permute-start.13 = (bf16[128,512]{1,0:T(8,128)(2,1)S(1)}, bf16[128,512]{1,0:T(8,128)(2,1)S(1)}, u32[]{:S(2)}, u32[]{:S(2)}) collective-permute-start(bf16[128,512]{1,0:T(8,128)(2,1)S(1)} %get-tuple-element.30), channel_id=1, source_target_pairs={{0,6},{1,7},{2,4},{3,5},{4,2},{5,3},{6,0},{7,1},{8,14},{9,15},{10,... | collective-permute-start | bytes 393224 | tf_op jit(solution)/shard_map/ppermute | solution.py:278
  75.6 1.6 %collective-permute-start.14 = (bf16[128,512]{1,0:T(8,128)(2,1)S(1)}, bf16[128,512]{1,0:T(8,128)(2,1)S(1)}, u32[]{:S(2)}, u32[]{:S(2)}) collective-permute-start(bf16[128,512]{1,0:T(8,128)(2,1)S(1)} %get-tuple-element.31), channel_id=1, source_target_pairs={{0,7},{1,6},{2,5},{3,4},{4,3},{5,2},{6,1},{7,0},{8,15},{9,14},{10,... | collective-permute-start | bytes 393224 | tf_op jit(solution)/shard_map/ppermute | solution.py:278
  77.2 3.8 %far.4 = (bf16[128,512]{1,0:T(8,128)(2,1)S(1)}, bf16[128,512]{1,0:T(8,128)(2,1)S(1)}) custom-call(s32[2]{0:T(128)S(1)} %pad_add_fusion.place_ref, s32[4,8]{1,0:T(4,128)S(1)} %copy-done.6, bf16[1024,512]{1,0:T(8,128)(2,1)S(1)} %copy-done.1, f32[8,128,512]{2,1,0:T(8,128)S(1)} %get-tuple-element.20.part_ref, f32[8,128,128]{2,1,0:T(8,128)S(1)} %get-tuple-element.21.stat_ref, ...), custom_call_target="tpu_custom_call" | custom-call | flops 201326592 | bytes 4000000 | tf_op jit(solution)/shard_map/far/pallas_call | solution.py:209
  81.9 3.2 %collective-permute-done.13.refs_6_ = bf16[128,512]{1,0:T(8,128)(2,1)S(1)} collective-permute-done((bf16[128,512]{1,0:T(8,128)(2,1)S(1)}, bf16[128,512]{1,0:T(8,128)(2,1)S(1)}, u32[]{:S(2)}, u32[]{:S(2)}) %collective-permute-start.13) | collective-permute-done | bytes 131104 | tf_op jit(solution)/shard_map/ppermute | solution.py:278
  85.2 2.8 %collective-permute-done.14.refs_7_ = bf16[128,512]{1,0:T(8,128)(2,1)S(1)} collective-permute-done((bf16[128,512]{1,0:T(8,128)(2,1)S(1)}, bf16[128,512]{1,0:T(8,128)(2,1)S(1)}, u32[]{:S(2)}, u32[]{:S(2)}) %collective-permute-start.14) | collective-permute-done | bytes 131104 | tf_op jit(solution)/shard_map/ppermute | solution.py:278
  88.0 2.5 %norm.1 = (bf16[128,4096]{1,0:T(8,128)(2,1)}, bf16[128,4096]{1,0:T(8,128)(2,1)}) custom-call(s32[2]{0:T(128)S(1)} %pad_add_fusion.place_ref, bf16[128,512]{1,0:T(8,128)(2,1)S(1)} %get-tuple-element.23.refs_0_, bf16[128,512]{1,0:T(8,128)(2,1)S(1)} %collective-permute-done.5.refs_1_, bf16[128,512]{1,0:T(8,128)(2,1)S(1)} %collective-permute-done.9.refs_2_, ...), custom_call_target="tpu_custom_call" | custom-call | flops 4000000 | bytes 4000000 | tf_op jit(solution)/shard_map/norm/pallas_call | solution.py:255
  (30 shorter events, 2.3 us)
Async XLA Ops:
  0.7 1.0 %copy-start.3 = (bf16[1024,128]{1,0:T(8,128)(2,1)S(1)}, bf16[1024,128]{1,0:T(8,128)(2,1)}, u32[]{:S(2)}) copy-start(bf16[1024,128]{1,0:T(8,128)(2,1)} %k_ref.1) | copy-start | bytes 786436
  1.7 0.9 %copy-start.4 = (bf16[1024,128]{1,0:T(8,128)(2,1)S(1)}, bf16[1024,128]{1,0:T(8,128)(2,1)}, u32[]{:S(2)}) copy-start(bf16[1024,128]{1,0:T(8,128)(2,1)} %v_ref.1) | copy-start | bytes 786436
  3.3 26.6 %collective-permute-start = (bf16[1024,256]{1,0:T(8,128)(2,1)S(1)}, bf16[1024,256]{1,0:T(8,128)(2,1)S(1)}, u32[]{:S(2)}, u32[]{:S(2)}) collective-permute-start(bf16[1024,256]{1,0:T(8,128)(2,1)S(1)} %get-tuple-element.17.kv_ref), channel_id=1, source_target_pairs={{0,128},{8,136},{16,144},{24,152},{32,160},{40,168},{48,176},{56,1... | collective-permute-start | bytes 1572872 | tf_op jit(solution)/shard_map/ppermute | solution.py:275
  8.2 23.0 %collective-permute-start.1 = (bf16[1024,256]{1,0:T(8,128)(2,1)S(1)}, bf16[1024,256]{1,0:T(8,128)(2,1)S(1)}, u32[]{:S(2)}, u32[]{:S(2)}) collective-permute-start(bf16[1024,256]{1,0:T(8,128)(2,1)S(1)} %get-tuple-element.17.kv_ref), channel_id=1, source_target_pairs={{0,64},{8,72},{16,80},{24,88},{32,96},{40,104},{48,112},{56,120},{... | collective-permute-start | bytes 1572872 | tf_op jit(solution)/shard_map/ppermute | solution.py:275
  10.5 33.5 %collective-permute-start.6 = (bf16[768,256]{1,0:T(8,128)(2,1)S(1)}, bf16[768,256]{1,0:T(8,128)(2,1)S(1)}, u32[]{:S(2)}, u32[]{:S(2)}) collective-permute-start(bf16[768,256]{1,0:T(8,128)(2,1)S(1)} %get-tuple-element.25), channel_id=1, source_target_pairs={{0,32},{8,40},{16,48},{24,56},{64,96},{72,104},{80,112},{88,120},{... | collective-permute-start | bytes 1179656 | tf_op jit(solution)/shard_map/ppermute | solution.py:275
  16.7 29.7 %collective-permute-start.7 = (bf16[768,256]{1,0:T(8,128)(2,1)S(1)}, bf16[768,256]{1,0:T(8,128)(2,1)S(1)}, u32[]{:S(2)}, u32[]{:S(2)}) collective-permute-start(bf16[768,256]{1,0:T(8,128)(2,1)S(1)} %get-tuple-element.25), channel_id=1, source_target_pairs={{0,16},{8,24},{32,48},{40,56},{64,80},{72,88},{96,112},{104,120},{... | collective-permute-start | bytes 1179656 | tf_op jit(solution)/shard_map/ppermute | solution.py:275
  18.0 39.0 %collective-permute-start.8 = (bf16[768,256]{1,0:T(8,128)(2,1)S(1)}, bf16[768,256]{1,0:T(8,128)(2,1)S(1)}, u32[]{:S(2)}, u32[]{:S(2)}) collective-permute-start(bf16[768,256]{1,0:T(8,128)(2,1)S(1)} %get-tuple-element.25), channel_id=1, source_target_pairs={{0,8},{16,24},{32,40},{48,56},{64,72},{80,88},{96,104},{112,120},{... | collective-permute-start | bytes 1179656 | tf_op jit(solution)/shard_map/ppermute | solution.py:275
  19.3 1.2 %copy-start = (bf16[1024,512]{1,0:T(8,128)(2,1)S(1)}, bf16[1024,512]{1,0:T(8,128)(2,1)}, u32[]{:S(2)}) copy-start(bf16[1024,512]{1,0:T(8,128)(2,1)} %q_ref.7) | copy-start | bytes 3145732
  20.5 0.7 copy-start.5
  21.2 11.4 %copy-start.1 = (bf16[1024,512]{1,0:T(8,128)(2,1)S(1)}, bf16[1024,512]{1,0:T(8,128)(2,1)}, u32[]{:S(2)}) copy-start(bf16[1024,512]{1,0:T(8,128)(2,1)} %q_ref.7) | copy-start | bytes 3145732
  29.9 43.5 %collective-permute-start.2 = (bf16[256,256]{1,0:T(8,128)(2,1)S(1)}, bf16[256,256]{1,0:T(8,128)(2,1)S(1)}, u32[]{:S(2)}, u32[]{:S(2)}) collective-permute-start(bf16[256,256]{1,0:T(8,128)(2,1)S(1)} %get-tuple-element.22), channel_id=1, source_target_pairs={{0,32},{8,40},{16,48},{24,56},{64,96},{72,104},{80,112},{88,120},{... | collective-permute-start | bytes 393224 | tf_op jit(solution)/shard_map/ppermute | solution.py:275
  31.2 42.2 %collective-permute-start.3 = (bf16[256,256]{1,0:T(8,128)(2,1)S(1)}, bf16[256,256]{1,0:T(8,128)(2,1)S(1)}, u32[]{:S(2)}, u32[]{:S(2)}) collective-permute-start(bf16[256,256]{1,0:T(8,128)(2,1)S(1)} %get-tuple-element.22), channel_id=1, source_target_pairs={{0,16},{8,24},{32,48},{40,56},{64,80},{72,88},{96,112},{104,120},{... | collective-permute-start | bytes 393224 | tf_op jit(solution)/shard_map/ppermute | solution.py:275
  44.1 31.6 %collective-permute-start.4 = (bf16[256,256]{1,0:T(8,128)(2,1)S(1)}, bf16[256,256]{1,0:T(8,128)(2,1)S(1)}, u32[]{:S(2)}, u32[]{:S(2)}) collective-permute-start(bf16[256,256]{1,0:T(8,128)(2,1)S(1)} %get-tuple-element.22), channel_id=1, source_target_pairs={{0,8},{16,24},{32,40},{48,56},{64,72},{80,88},{96,104},{112,120},{... | collective-permute-start | bytes 393224 | tf_op jit(solution)/shard_map/ppermute | solution.py:275
  56.9 20.3 %copy-start.6 = (s32[4,8]{1,0:T(4,128)S(1)}, s32[4,8]{1,0:T(4,128)}, u32[]{:S(2)}) copy-start(s32[4,8]{1,0:T(4,128)} %mask_ref.7) | copy-start | bytes 388
  67.4 13.9 %copy-start.7 = (bf16[4096]{0:T(1024)(128)(2,1)S(1)}, bf16[4096]{0:T(1024)(128)(2,1)}, u32[]{:S(2)}) copy-start(bf16[4096]{0:T(1024)(128)(2,1)} %param.11) | copy-start | bytes 24580
  67.4 20.6 %copy-start.2 = (bf16[128,4096]{1,0:T(8,128)(2,1)S(1)}, bf16[128,4096]{1,0:T(8,128)(2,1)}, u32[]{:S(2)}) copy-start(bf16[128,4096]{1,0:T(8,128)(2,1)} %refs_8_.1) | copy-start | bytes 3145732
  67.4 13.6 %collective-permute-start.10 = (bf16[128,512]{1,0:T(8,128)(2,1)S(1)}, bf16[128,512]{1,0:T(8,128)(2,1)S(1)}, u32[]{:S(2)}, u32[]{:S(2)}) collective-permute-start(bf16[128,512]{1,0:T(8,128)(2,1)S(1)} %get-tuple-element.27), channel_id=1, source_target_pairs={{0,3},{1,2},{2,1},{3,0},{4,7},{5,6},{6,5},{7,4},{8,11},{9,10},{10,... | collective-permute-start | bytes 393224 | tf_op jit(solution)/shard_map/ppermute | solution.py:278
  71.0 10.2 %collective-permute-start.11 = (bf16[128,512]{1,0:T(8,128)(2,1)S(1)}, bf16[128,512]{1,0:T(8,128)(2,1)S(1)}, u32[]{:S(2)}, u32[]{:S(2)}) collective-permute-start(bf16[128,512]{1,0:T(8,128)(2,1)S(1)} %get-tuple-element.28), channel_id=1, source_target_pairs={{0,4},{1,5},{2,6},{3,7},{4,0},{5,1},{6,2},{7,3},{8,12},{9,13},{10,... | collective-permute-start | bytes 393224 | tf_op jit(solution)/shard_map/ppermute | solution.py:278
  73.4 8.5 %collective-permute-start.12 = (bf16[128,512]{1,0:T(8,128)(2,1)S(1)}, bf16[128,512]{1,0:T(8,128)(2,1)S(1)}, u32[]{:S(2)}, u32[]{:S(2)}) collective-permute-start(bf16[128,512]{1,0:T(8,128)(2,1)S(1)} %get-tuple-element.29), channel_id=1, source_target_pairs={{0,5},{1,4},{2,7},{3,6},{4,1},{5,0},{6,3},{7,2},{8,13},{9,12},{10,... | collective-permute-start | bytes 393224 | tf_op jit(solution)/shard_map/ppermute | solution.py:278
  73.4 11.7 %collective-permute-start.13 = (bf16[128,512]{1,0:T(8,128)(2,1)S(1)}, bf16[128,512]{1,0:T(8,128)(2,1)S(1)}, u32[]{:S(2)}, u32[]{:S(2)}) collective-permute-start(bf16[128,512]{1,0:T(8,128)(2,1)S(1)} %get-tuple-element.30), channel_id=1, source_target_pairs={{0,6},{1,7},{2,4},{3,5},{4,2},{5,3},{6,0},{7,1},{8,14},{9,15},{10,... | collective-permute-start | bytes 393224 | tf_op jit(solution)/shard_map/ppermute | solution.py:278
  75.6 12.4 %collective-permute-start.14 = (bf16[128,512]{1,0:T(8,128)(2,1)S(1)}, bf16[128,512]{1,0:T(8,128)(2,1)S(1)}, u32[]{:S(2)}, u32[]{:S(2)}) collective-permute-start(bf16[128,512]{1,0:T(8,128)(2,1)S(1)} %get-tuple-element.31), channel_id=1, source_target_pairs={{0,7},{1,6},{2,5},{3,4},{4,3},{5,2},{6,1},{7,0},{8,15},{9,14},{10,... | collective-permute-start | bytes 393224 | tf_op jit(solution)/shard_map/ppermute | solution.py:278
  81.1 6.9 %collective-permute-start.9 = (bf16[128,512]{1,0:T(8,128)(2,1)S(1)}, bf16[128,512]{1,0:T(8,128)(2,1)S(1)}, u32[]{:S(2)}, u32[]{:S(2)}) collective-permute-start(bf16[128,512]{1,0:T(8,128)(2,1)S(1)} %get-tuple-element.26), channel_id=1, source_target_pairs={{0,2},{1,3},{2,0},{3,1},{4,6},{5,7},{6,4},{7,5},{8,10},{9,11},{10,... | collective-permute-start | bytes 393224 | tf_op jit(solution)/shard_map/ppermute | solution.py:278
  81.2 6.8 %collective-permute-start.5 = (bf16[128,512]{1,0:T(8,128)(2,1)S(1)}, bf16[128,512]{1,0:T(8,128)(2,1)S(1)}, u32[]{:S(2)}, u32[]{:S(2)}) collective-permute-start(bf16[128,512]{1,0:T(8,128)(2,1)S(1)} %get-tuple-element.24), channel_id=1, source_target_pairs={{0,1},{1,0},{2,3},{3,2},{4,5},{5,4},{6,7},{7,6},{8,9},{9,8},{10,11... | collective-permute-start | bytes 393224 | tf_op jit(solution)/shard_map/ppermute | solution.py:278

commit v2 on v1

v2 whole, which is shorter than its diff:
```python
import functools

import jax
import jax.numpy as jnp
from jax import lax
from jax.experimental import pallas as pl
from jax.experimental.pallas import tpu as pltpu
from jax.sharding import PartitionSpec as P

DH = 128
BLOCK = 128
EPSILON = 1e-05
NEG = -1e30
KERNEL_VMEM = 16 * 2**20
SCALE = DH ** (-0.5) * 1.4426950408889634
LATE = 3


NEAR, SIDE, HALF, FOURTH, THIRD = 1, 2, 3, 4, 5


def slots(size):
    pairs = {slot: [] for slot in (NEAR, SIDE, HALF, FOURTH, THIRD)}
    for i in range(size):
        low = i & 3
        for slot, bit, taken in (
            (NEAR, 0, low == 3),
            (NEAR, 1, low == 2),
            (SIDE, 0, low == 1),
            (SIDE, 1, low == 3),
            (HALF, 2, i & 4),
            (THIRD, 3, i & 8),
            (FOURTH, 4, i & 16),
        ):
            if taken:
                pairs[slot].append((i - 2**bit, i))
    return pairs


def slot_level(slot, ctx, local_bits):
    bit = [lax.shift_right_logical(ctx, b) & 1 for b in range(5)]
    taken, level = {
        NEAR: (bit[1], 1 - bit[0]),
        SIDE: (bit[0], bit[1]),
        HALF: (bit[2], 2),
        FOURTH: (bit[4], 4),
        THIRD: (bit[3], 3),
    }[slot]
    return jnp.where(taken == 1, local_bits + level, 31)


def held_in(space, *arrays):
    return [pltpu.with_memory_space_constraint(array, space) for array in arrays]


def params():
    return pltpu.CompilerParams(vmem_limit_bytes=KERNEL_VMEM)


def rows_at(index):
    return pl.ds(pl.multiple_of(index * BLOCK, BLOCK), BLOCK)


def in_vmem():
    return pl.BlockSpec(memory_space=pltpu.VMEM)


def order_kernel(place_ref, k_hbm, v_hbm, all_ref, late_ref, rest_ref, k_ref, v_ref, sems):
    copies = [pltpu.make_async_copy(k_hbm, k_ref, sems.at[0]), pltpu.make_async_copy(v_hbm, v_ref, sems.at[1])]
    for copy in copies:
        copy.start()
    for copy in copies:
        copy.wait()
    blocks = k_ref.shape[0] // BLOCK
    for n in range(blocks):
        source = rows_at(place_ref[0] ^ n)
        key, val = k_ref[source, :], v_ref[source, :].T
        part, at = (late_ref, n) if n < LATE else (rest_ref, n - LATE)
        for ref, first in ((all_ref, n), (part, at)):
            ref[first * BLOCK : (first + 1) * BLOCK, :DH] = key
            ref[first * BLOCK : (first + 1) * BLOCK, DH:] = val


def ordered(place, keys, values):
    rows = keys.shape[0]
    hbm = pl.BlockSpec(memory_space=pl.ANY)
    return pl.pallas_call(
        order_kernel,
        in_specs=[pl.BlockSpec(memory_space=pltpu.SMEM), hbm, hbm],
        out_specs=[in_vmem()] * 3,
        out_shape=[
            jax.ShapeDtypeStruct((n, 2 * DH), jnp.bfloat16)
            for n in (rows, LATE * BLOCK, rows - LATE * BLOCK)
        ],
        scratch_shapes=[pltpu.VMEM(keys.shape, jnp.bfloat16)] * 2 + [pltpu.SemaphoreType.DMA((2,))],
        compiler_params=params(),
        name="order",
    )(place, *held_in(pltpu.HBM, keys, values))


def attend(q, keys, vals, biases, causal=None, before=None):
    scores = lax.dot_general(
        jnp.concatenate(keys, 0), q, (((1,), (1,)), ((), ())), preferred_element_type=jnp.float32
    )
    parts = [scores[n * BLOCK : (n + 1) * BLOCK, :] for n in range(len(keys))]
    if causal is not None:
        parts[0] = jnp.where(causal, parts[0], NEG)
    tops = [part.max(0, keepdims=True) * SCALE + bias for part, bias in zip(parts, biases)]
    top = functools.reduce(jnp.maximum, tops if before is None else [before[1]] + tops)
    weights = [jnp.exp2(part * SCALE - (top - bias)) for part, bias in zip(parts, biases)]
    total = functools.reduce(jnp.add, weights).sum(0, keepdims=True)
    weight = jnp.concatenate([w.astype(jnp.bfloat16) for w in weights], 0)
    summed = jnp.dot(jnp.concatenate(vals, 1), weight, preferred_element_type=jnp.float32)
    if before is not None:
        factor = jnp.exp2(before[1] - top)
        total = total + before[2] * factor
        summed = summed + before[0] * factor
    return summed, top, total


def bias_of(bitmaps, level):
    pieces = []
    for bitmap in bitmaps:
        allowed = lax.shift_right_logical(bitmap, level) & 1
        pieces.append(jnp.full((1, BLOCK), (1 - allowed).astype(jnp.float32) * NEG))
    return jnp.concatenate(pieces, 1)


def local_kernel(heads, blocks, place_ref, mask_ref, q_hbm, kv_ref, q_ref, part_ref, stat_ref, sems):
    rank = place_ref[0]
    copies = []
    for j in range(blocks):
        for h in range(heads):
            copies.append(
                pltpu.make_async_copy(
                    q_hbm.at[j * BLOCK : (j + 1) * BLOCK, h * DH : (h + 1) * DH],
                    q_ref.at[rank ^ j, h * BLOCK : (h + 1) * BLOCK, :],
                    sems.at[j, h],
                )
            )
    for copy in copies:
        copy.start()
    shape = (BLOCK, heads * BLOCK)
    causal = lax.broadcasted_iota(jnp.int32, shape, 0) <= (lax.broadcasted_iota(jnp.int32, shape, 1) & (BLOCK - 1))
    for copy in copies:
        copy.wait()
    for j in range(blocks):
        levels = [b for b in range(blocks.bit_length() - 1) if j >> b & 1]
        held = [kv_ref[rows_at(rank ^ other), :] for other in [j] + [j - 2**b for b in levels]]
        bitmaps = [mask_ref[h, j] for h in range(heads)]
        biases = [0.0] + [bias_of(bitmaps, level) for level in levels]
        summed, top, total = attend(
            q_ref[rank ^ j], [kv[:, :DH] for kv in held], [kv[:, DH:] for kv in held], biases, causal
        )
        part_ref[rank ^ j] = summed
        stat_ref[rank ^ j, 0:1, :] = top
        stat_ref[rank ^ j, 1:2, :] = total


def local_part(place, block_masks, queries, kv):
    tokens, width = queries.shape
    heads, blocks = block_masks.shape
    smem = pl.BlockSpec(memory_space=pltpu.SMEM)
    return pl.pallas_call(
        functools.partial(local_kernel, heads, blocks),
        in_specs=[smem, smem, pl.BlockSpec(memory_space=pl.ANY), in_vmem()],
        out_specs=[in_vmem()] * 3,
        out_shape=[
            jax.ShapeDtypeStruct((blocks, heads * BLOCK, DH), jnp.bfloat16),
            jax.ShapeDtypeStruct((blocks, DH, width), jnp.float32),
            jax.ShapeDtypeStruct((blocks, 8, width), jnp.float32),
        ],
        scratch_shapes=[pltpu.SemaphoreType.DMA((blocks, heads))],
        cost_estimate=pl.CostEstimate(
            flops=3 * 4 * tokens * width * BLOCK, bytes_accessed=4_000_000, transcendentals=3 * tokens * heads * BLOCK
        ),
        compiler_params=params(),
        name="local",
    )(place, block_masks, *held_in(pltpu.HBM, queries), kv)


def far_kernel(heads, local_bits, held, first, count, offset, final, place_ref, mask_ref, q_ref, part_ref, stat_ref, *refs):
    arrays = sum(number for _, number in held)
    kv_refs, outs = refs[:arrays], refs[arrays:]
    levels = [slot_level(slot, place_ref[1], local_bits) for slot, _ in held]
    for i in range(count):
        n = first + i
        j = place_ref[0] ^ n
        keys, vals, rest = [], [], kv_refs
        for _, number in held:
            tiles = []
            for ref in rest[:number]:
                at = (n if ref.shape[0] == q_ref.shape[0] * BLOCK else i) * BLOCK
                tiles.append(ref[at : at + BLOCK, :])
            rest = rest[number:]
            tile = functools.reduce(jnp.add, tiles)
            keys.append(tile[:, :DH])
            vals.append(tile[:, DH:])
        bitmaps = [mask_ref[h, j] for h in range(heads)]
        biases = [bias_of(bitmaps, level) for level in levels]
        before = (part_ref[offset + i], stat_ref[offset + i, 0:1, :], stat_ref[offset + i, 1:2, :])
        summed, top, total = attend(q_ref[n], keys, vals, biases, None, before)
        if final:
            result = summed * (1.0 / total)
            for h in range(heads):
                at = slice(h * DH, (h + 1) * DH)
                tile = result[:, at].T.astype(jnp.bfloat16)
                if final == "ranks":
                    outs[0][rows_at(j), at] = tile
                else:
                    outs[i][:, at] = tile
        else:
            outs[0][i] = summed
            outs[1][i, 0:1, :] = top
            outs[1][i, 1:2, :] = total


def far_part(place, block_masks, state, fetched, held, first, count, final=None):
    queries, part, stats = state
    heads, blocks = block_masks.shape
    width = heads * DH
    kvs = []
    numbers = []
    for slot in held:
        arrays = fetched[slot] if isinstance(fetched[slot], list) else [fetched[slot]]
        kvs += arrays
        numbers.append((slot, len(arrays)))
    if final == "ranks":
        out_shape = [jax.ShapeDtypeStruct((blocks * BLOCK, width), jnp.bfloat16)]
    elif final == "order":
        out_shape = [jax.ShapeDtypeStruct((BLOCK, width), jnp.bfloat16)] * count
    else:
        out_shape = [
            jax.ShapeDtypeStruct((count, DH, width), jnp.float32),
            jax.ShapeDtypeStruct((count, 8, width), jnp.float32),
        ]
    smem = pl.BlockSpec(memory_space=pltpu.SMEM)
    offset = first if part.shape[0] == blocks else 0
    outs = pl.pallas_call(
        functools.partial(far_kernel, heads, blocks.bit_length() - 1, numbers, first, count, offset, final),
        in_specs=[smem, smem] + [in_vmem()] * (3 + len(kvs)),
        out_specs=[in_vmem()] * len(out_shape),
        out_shape=out_shape,
        cost_estimate=pl.CostEstimate(
            flops=len(kvs) * 4 * count * BLOCK * width * BLOCK,
            bytes_accessed=4_000_000,
            transcendentals=len(kvs) * count * heads * BLOCK * BLOCK,
        ),
        compiler_params=params(),
        name="far",
    )(place, block_masks, queries, part, stats, *kvs)
    if final:
        return outs
    return [queries] + list(outs)


def norm_kernel(groups, place_ref, *refs):
    near, (far_ref, res_ref, gain_ref, stream_ref, normed_ref, whole) = refs[:LATE], refs[LATE:]
    width = near[0].shape[1]
    square = jnp.zeros((BLOCK, DH), jnp.float32)
    for n in range(groups):
        source = place_ref[0] ^ n
        cols = pl.ds(pl.multiple_of(source * width, width), width)
        attended = near[n][...] if n < LATE else far_ref[rows_at(source), :]
        summed = res_ref[:, cols].astype(jnp.float32) + attended.astype(jnp.float32)
        stream_ref[:, cols] = summed.astype(jnp.bfloat16)
        whole[:, cols] = summed
        for c in range(0, width, DH):
            piece = summed[:, c : c + DH]
            square = square + piece * piece
    mean = square.sum(-1, keepdims=True) / (groups * width)
    factor = lax.rsqrt(mean + EPSILON)
    for n in range(groups):
        cols = slice(n * width, (n + 1) * width)
        normed_ref[:, cols] = (whole[:, cols] * factor * gain_ref[:, cols].astype(jnp.float32)).astype(jnp.bfloat16)


def norm_part(place, near, far, residual, gain):
    vmem = pl.BlockSpec(memory_space=pltpu.VMEM)
    return pl.pallas_call(
        functools.partial(norm_kernel, far.shape[0] // BLOCK),
        in_specs=[pl.BlockSpec(memory_space=pltpu.SMEM)] + [vmem] * (len(near) + 3),
        out_specs=[vmem] * 2,
        out_shape=[jax.ShapeDtypeStruct(residual.shape, jnp.bfloat16)] * 2,
        scratch_shapes=[pltpu.VMEM(residual.shape, jnp.float32)],
        cost_estimate=pl.CostEstimate(flops=4_000_000, bytes_accessed=4_000_000, transcendentals=128),
        compiler_params=params(),
        name="norm",
    )(place, *near, far, residual, gain)


def shards(queries, keys, values, block_masks, residual, norm_gain):
    _, blocks = block_masks.shape
    groups = lax.axis_size("head")
    routes = slots(lax.axis_size("ctx"))
    place = jnp.stack([lax.axis_index("head"), lax.axis_index("ctx")]).astype(jnp.int32)

    def fetched(array, slot):
        return lax.ppermute(array, "ctx", routes[slot])

    def swapped(array, n):
        return lax.ppermute(array, "head", [(i, i ^ n) for i in range(groups)])

    by_three = [(i - 3, i) for i in range(lax.axis_size("ctx")) if i & 7 == 6]

    kv, kv_late, kv_rest = ordered(place, keys, values)
    far = {slot: fetched(kv, slot) for slot in (FOURTH, THIRD)}
    rest = far | {slot: fetched(kv_rest, slot) for slot in (NEAR, SIDE)}
    straight = [(i, j) for i, j in routes[HALF] if j & 7 != 6]
    rest[HALF] = [lax.ppermute(kv_rest, "ctx", straight)]
    rest[HALF] += [lax.ppermute(rest[NEAR], "ctx", by_three)]
    late = far | {slot: fetched(kv_late, slot) for slot in (NEAR, SIDE, HALF)}
    given = (place, block_masks)
    state = local_part(place, block_masks, queries, kv)
    rest_state = far_part(*given, state, rest, (NEAR, SIDE, FOURTH, THIRD), LATE, blocks - LATE)
    (sent,) = far_part(*given, rest_state, rest, (HALF,), LATE, blocks - LATE, "ranks")
    received = lax.all_to_all(sent, "head", split_axis=0, concat_axis=0, tiled=True)
    late_state = far_part(*given, state, late, (FOURTH, THIRD), 0, LATE)
    near = far_part(*given, late_state, late, (NEAR, SIDE, HALF), 0, LATE, "order")
    near = [near[0]] + [swapped(near[n], n) for n in range(1, LATE)]
    return norm_part(place, near, received, residual, norm_gain.reshape(1, -1))


def solution(mesh):
    in_specs = (
        P("ctx", "head"),
        P("ctx", "head"),
        P("ctx", "head"),
        P("head", "ctx"),
        P(("ctx", "head"), None),
        P(),
    )
    out_specs = (P(("ctx", "head"), None), P(("ctx", "head"), None))
    return jax.shard_map(shards, mesh=mesh, in_specs=in_specs, out_specs=out_specs, check_vma=False)
```

time: 90.8 us -> 80.7 us (0.89)
  the two profiles are of different devices: /device:TPU:97 before, /device:TPU:200 now
where the time goes in v2:
time: 80.7 us; the launch traced here: 80 us
  waiting for transfers between devices  33.5 us (42%)
  starting transfers between devices  20.9 us (26%)
  Pallas kernels  19.7 us (24%)
  local copies, waits for them, and re-layouts  4.98 us (6%)
  between operations  0.87 us (1%)
    ppermute x7, waiting for transfers between devices, fetched(): return lax.ppermute(array, 'ctx', routes[slot])  29.2 us
    ppermute x7, starting transfers between devices, fetched(): return lax.ppermute(array, 'ctx', routes[slot])  13 us
    pallas_call x4, Pallas kernels, far_part(): pl.pallas_call(functools.partial(far_kernel, heads, blocks.bit_length() -...  9.47 us
    pallas_call x1, Pallas kernels, local_part(): pl.pallas_call(functools.partial(local_kernel, heads, blocks), in_specs=[...  5.34 us
    unnamed x18, local copies, waits for them, and re-layouts  4.97 us
    ppermute x2, waiting for transfers between devices, swapped(): return lax.ppermute(array, 'head', [(i, i ^ n) for i in range(groups)])  4.35 us
    all_to_all x1, starting transfers between devices, shards(): lax.all_to_all(sent, 'head', split_axis=0, concat_axis=0, tiled=True)  4.3 us
    pallas_call x1, Pallas kernels, norm_part(): pl.pallas_call(functools.partial(norm_kernel, far.shape[0] // BLOCK), in_...  3.13 us
  transfers between devices with their start and end apart: 12, of which 5 were waited for; matrix products, arithmetic and copies ran while one was open for 0% of the time, Pallas kernels for 16%

profile of v2, /device:TPU:200, one launch (start us, length us, event | category | flops | bytes accessed | tf_op | source)
XLA Modules:
  0.0 80.0 jit_solution(4275363007160168528)
XLA Ops:
  0.7 1.7 %order.1 = (bf16[1024,256]{1,0:T(8,128)(2,1)S(1)}, bf16[384,256]{1,0:T(8,128)(2,1)S(1)}, bf16[640,256]{1,0:T(8,128)(2,1)S(1)}) custom-call(s32[2]{0:T(128)S(1)} %pad_add_fusion.place_ref, bf16[1024,128]{1,0:T(8,128)(2,1)} %k_hbm.1, bf16[1024,128]{1,0:T(8,128)(2,1)} %v_hbm.1), custom_call_target="tpu_custom_call" | custom-call | tf_op jit(solution)/shard_map/order/pallas_call | solution.py:87
  2.5 2.9 %collective-permute-start.7 = (bf16[640,256]{1,0:T(8,128)(2,1)S(1)}, bf16[640,256]{1,0:T(8,128)(2,1)S(1)}, u32[]{:S(2)}, u32[]{:S(2)}) collective-permute-start(bf16[640,256]{1,0:T(8,128)(2,1)S(1)} %get-tuple-element.25), channel_id=1, source_target_pairs={{0,16},{16,24},{32,48},{48,56},{64,80},{80,88},{96,112},{112,120},... | collective-permute-start | bytes 983048 | tf_op jit(solution)/shard_map/ppermute | solution.py:299
  5.4 4.2 %collective-permute-start = (bf16[1024,256]{1,0:T(8,128)(2,1)S(1)}, bf16[1024,256]{1,0:T(8,128)(2,1)S(1)}, u32[]{:S(2)}, u32[]{:S(2)}) collective-permute-start(bf16[1024,256]{1,0:T(8,128)(2,1)S(1)} %get-tuple-element.15.kv_ref), channel_id=1, source_target_pairs={{0,128},{8,136},{16,144},{24,152},{32,160},{40,168},{48,176},{56,1... | collective-permute-start | bytes 1572872 | tf_op jit(solution)/shard_map/ppermute | solution.py:299
  9.6 1.3 %collective-permute-start.1 = (bf16[1024,256]{1,0:T(8,128)(2,1)S(1)}, bf16[1024,256]{1,0:T(8,128)(2,1)S(1)}, u32[]{:S(2)}, u32[]{:S(2)}) collective-permute-start(bf16[1024,256]{1,0:T(8,128)(2,1)S(1)} %get-tuple-element.15.kv_ref), channel_id=1, source_target_pairs={{0,64},{8,72},{16,80},{24,88},{32,96},{40,104},{48,112},{56,120},{... | collective-permute-start | bytes 1572872 | tf_op jit(solution)/shard_map/ppermute | solution.py:299
  12.3 2.8 %collective-permute-done.7.refs_0_ = bf16[640,256]{1,0:T(8,128)(2,1)S(1)} collective-permute-done((bf16[640,256]{1,0:T(8,128)(2,1)S(1)}, bf16[640,256]{1,0:T(8,128)(2,1)S(1)}, u32[]{:S(2)}, u32[]{:S(2)}) %collective-permute-start.7) | collective-permute-done | bytes 327712 | tf_op jit(solution)/shard_map/ppermute | solution.py:299
  15.1 1.3 %collective-permute-start.10 = (bf16[640,256]{1,0:T(8,128)(2,1)S(1)}, bf16[640,256]{1,0:T(8,128)(2,1)S(1)}, u32[]{:S(2)}, u32[]{:S(2)}) collective-permute-start(bf16[640,256]{1,0:T(8,128)(2,1)S(1)} %collective-permute-done.7.refs_0_), channel_id=1, source_target_pairs={{24,48},{88,112},{152,176},{216,240},{25,49},{89,113},{153,177},{2... | collective-permute-start | bytes 983048 | tf_op jit(solution)/shard_map/ppermute | solution.py:311
  17.1 5.3 %local.1 = (bf16[8,512,128]{2,1,0:T(8,128)(2,1)S(1)}, f32[8,128,512]{2,1,0:T(8,128)S(1)}, f32[8,8,512]{2,1,0:T(8,128)S(1)}) custom-call(s32[2]{0:T(128)S(1)} %pad_add_fusion.place_ref, s32[4,8]{1,0:T(4,128)S(1)} %copy-done.6, bf16[1024,512]{1,0:T(8,128)(2,1)} %q_hbm.1, bf16[1024,256]{1,0:T(8,128)(2,1)S(1)} %get-tuple-element.15.kv_ref), custom_call_target="tpu_custom_call" | custom-call | flops 805306368 | bytes 4000000 | tf_op jit(solution)/shard_map/local/pallas_call | solution.py:164
  22.5 11.0 %collective-permute-done.1.refs_1_.refs_3_ = bf16[1024,256]{1,0:T(8,128)(2,1)S(1)} collective-permute-done((bf16[1024,256]{1,0:T(8,128)(2,1)S(1)}, bf16[1024,256]{1,0:T(8,128)(2,1)S(1)}, u32[]{:S(2)}, u32[]{:S(2)}) %collective-permute-start.1) | collective-permute-done | bytes 524320 | tf_op jit(solution)/shard_map/ppermute | solution.py:299
  33.5 3.4 %far.6 = (f32[5,128,512]{2,1,0:T(8,128)S(1)}, f32[5,8,512]{2,1,0:T(8,128)S(1)}) custom-call(s32[2]{0:T(128)S(1)} %pad_add_fusion.place_ref, s32[4,8]{1,0:T(4,128)S(1)} %copy-done.7, bf16[8,512,128]{2,1,0:T(8,128)(2,1)S(1)} %get-tuple-element.16.q_ref, f32[8,128,512]{2,1,0:T(8,128)S(1)} %get-tuple-element.17.part_ref, ...), custom_call_target="tpu_custom_call" | custom-call | flops 671088640 | bytes 4000000 | tf_op jit(solution)/shard_map/far/pallas_call | solution.py:239
  37.0 2.1 %far.7 = bf16[1024,512]{1,0:T(8,128)(2,1)S(1)} custom-call(s32[2]{0:T(128)S(1)} %pad_add_fusion.place_ref, s32[4,8]{1,0:T(4,128)S(1)} %copy-done.7, bf16[8,512,128]{2,1,0:T(8,128)(2,1)S(1)} %get-tuple-element.16.q_ref, f32[5,128,512]{2,1,0:T(8,128)S(1)} %get-tuple-element.26.part_ref, f32[5,8,512]{2,1,0:T(8,128)S(1)} %get-tuple-element.27.stat_ref, ...), custom_call_target="tpu_custom_call" | custom-call | flops 335544320 | bytes 4000000 | tf_op jit(solution)/shard_map/far/pallas_call | solution.py:239
  39.2 1.0 %copy-done = bf16[1024,512]{1,0:T(8,128)(2,1)} copy-done((bf16[1024,512]{1,0:T(8,128)(2,1)}, bf16[1024,512]{1,0:T(8,128)(2,1)S(1)}, u32[]{:S(2)}) %copy-start) | copy-done | bytes 1048600
  40.1 4.3 %all-to-all-start = ((bf16[8,128,512]{2,1,0:T(8,128)(2,1)}), bf16[8,128,512]{2,1,0:T(8,128)(2,1)}, u32[]{:S(2)}, u32[]{:S(2)}) async-start(bf16[8,128,512]{2,1,0:T(8,128)(2,1)} %bitcast.4), calls=%async_computation | async-start | bytes 2097152 | tf_op jit(solution)/shard_map/all_to_all | solution.py:317
  44.4 1.9 %collective-permute-start.2 = (bf16[384,256]{1,0:T(8,128)(2,1)S(1)}, bf16[384,256]{1,0:T(8,128)(2,1)S(1)}, u32[]{:S(2)}, u32[]{:S(2)}) collective-permute-start(bf16[384,256]{1,0:T(8,128)(2,1)S(1)} %get-tuple-element.21), channel_id=1, source_target_pairs={{0,16},{16,24},{32,48},{48,56},{64,80},{80,88},{96,112},{112,120},... | collective-permute-start | bytes 589832 | tf_op jit(solution)/shard_map/ppermute | solution.py:299
  47.0 1.3 %collective-permute-start.4 = (bf16[384,256]{1,0:T(8,128)(2,1)S(1)}, bf16[384,256]{1,0:T(8,128)(2,1)S(1)}, u32[]{:S(2)}, u32[]{:S(2)}) collective-permute-start(bf16[384,256]{1,0:T(8,128)(2,1)S(1)} %get-tuple-element.21), channel_id=1, source_target_pairs={{0,32},{8,40},{16,48},{24,56},{64,96},{72,104},{80,112},{88,120},{... | collective-permute-start | bytes 589832 | tf_op jit(solution)/shard_map/ppermute | solution.py:299
  48.3 1.0 %copy-done.2 = bf16[1024,256]{1,0:T(8,128)(2,1)S(1)} copy-done((bf16[1024,256]{1,0:T(8,128)(2,1)S(1)}, bf16[1024,256]{1,0:T(8,128)(2,1)}, u32[]{:S(2)}) %copy-start.2) | copy-done | bytes 524312
  49.4 1.0 %copy-done.4 = bf16[1024,256]{1,0:T(8,128)(2,1)S(1)} copy-done((bf16[1024,256]{1,0:T(8,128)(2,1)S(1)}, bf16[1024,256]{1,0:T(8,128)(2,1)}, u32[]{:S(2)}) %copy-start.4) | copy-done | bytes 524312
  50.4 1.8 %far.4 = (f32[3,128,512]{2,1,0:T(8,128)S(1)}, f32[3,8,512]{2,1,0:T(8,128)S(1)}) custom-call(s32[2]{0:T(128)S(1)} %pad_add_fusion.place_ref, s32[4,8]{1,0:T(4,128)S(1)} %copy-done.7, bf16[8,512,128]{2,1,0:T(8,128)(2,1)S(1)} %get-tuple-element.16.q_ref, f32[8,128,512]{2,1,0:T(8,128)S(1)} %get-tuple-element.17.part_ref, ...), custom_call_target="tpu_custom_call" | custom-call | flops 201326592 | bytes 4000000 | tf_op jit(solution)/shard_map/far/pallas_call | solution.py:239
  52.2 2.8 %collective-permute-done.2.refs_0_ = bf16[384,256]{1,0:T(8,128)(2,1)S(1)} collective-permute-done((bf16[384,256]{1,0:T(8,128)(2,1)S(1)}, bf16[384,256]{1,0:T(8,128)(2,1)S(1)}, u32[]{:S(2)}, u32[]{:S(2)}) %collective-permute-start.2) | collective-permute-done | bytes 196640 | tf_op jit(solution)/shard_map/ppermute | solution.py:299
  55.0 12.5 %collective-permute-done.4.refs_2_ = bf16[384,256]{1,0:T(8,128)(2,1)S(1)} collective-permute-done((bf16[384,256]{1,0:T(8,128)(2,1)S(1)}, bf16[384,256]{1,0:T(8,128)(2,1)S(1)}, u32[]{:S(2)}, u32[]{:S(2)}) %collective-permute-start.4) | collective-permute-done | bytes 196640 | tf_op jit(solution)/shard_map/ppermute | solution.py:299
  67.5 2.1 %far.5 = (bf16[128,512]{1,0:T(8,128)(2,1)S(1)}, bf16[128,512]{1,0:T(8,128)(2,1)S(1)}, bf16[128,512]{1,0:T(8,128)(2,1)S(1)}) custom-call(s32[2]{0:T(128)S(1)} %pad_add_fusion.place_ref, s32[4,8]{1,0:T(4,128)S(1)} %copy-done.7, bf16[8,512,128]{2,1,0:T(8,128)(2,1)S(1)} %get-tuple-element.16.q_ref, f32[3,128,512]{2,1,0:T(8,128)S(1)} %get-tuple-element.19.part_ref, ...), custom_call_target="tpu_custom_call" | custom-call | flops 301989888 | bytes 4000000 | tf_op jit(solution)/shard_map/far/pallas_call | solution.py:239
  69.8 1.5 %collective-permute-start.6 = (bf16[128,512]{1,0:T(8,128)(2,1)S(1)}, bf16[128,512]{1,0:T(8,128)(2,1)S(1)}, u32[]{:S(2)}, u32[]{:S(2)}) collective-permute-start(bf16[128,512]{1,0:T(8,128)(2,1)S(1)} %get-tuple-element.24), channel_id=1, source_target_pairs={{0,2},{1,3},{2,0},{3,1},{4,6},{5,7},{6,4},{7,5},{8,10},{9,11},{10,... | collective-permute-start | bytes 393224 | tf_op jit(solution)/shard_map/ppermute | solution.py:302
  71.3 4.3 %collective-permute-done.6.refs_2_ = bf16[128,512]{1,0:T(8,128)(2,1)S(1)} collective-permute-done((bf16[128,512]{1,0:T(8,128)(2,1)S(1)}, bf16[128,512]{1,0:T(8,128)(2,1)S(1)}, u32[]{:S(2)}, u32[]{:S(2)}) %collective-permute-start.6) | collective-permute-done | bytes 131104 | tf_op jit(solution)/shard_map/ppermute | solution.py:302
  75.7 1.2 %copy-done.5 = bf16[128,4096]{1,0:T(8,128)(2,1)S(1)} copy-done((bf16[128,4096]{1,0:T(8,128)(2,1)S(1)}, bf16[128,4096]{1,0:T(8,128)(2,1)}, u32[]{:S(2)}) %copy-start.5) | copy-done | bytes 1048600
  76.9 3.1 %norm.1 = (bf16[128,4096]{1,0:T(8,128)(2,1)}, bf16[128,4096]{1,0:T(8,128)(2,1)}) custom-call(s32[2]{0:T(128)S(1)} %pad_add_fusion.place_ref, bf16[128,512]{1,0:T(8,128)(2,1)S(1)} %get-tuple-element.22.refs_0_, bf16[128,512]{1,0:T(8,128)(2,1)S(1)} %collective-permute-done.5.refs_1_, bf16[128,512]{1,0:T(8,128)(2,1)S(1)} %collective-permute-done.6.refs_2_, ...), custom_call_target="tpu_custom_call" | custom-call | flops 4000000 | bytes 4000000 | tf_op jit(solution)/shard_map/norm/pallas_call | solution.py:280
  (27 shorter events, 3.0 us)
Async XLA Ops:
  0.6 32.9 %copy-start.7 = (s32[4,8]{1,0:T(4,128)S(1)}, s32[4,8]{1,0:T(4,128)}, u32[]{:S(2)}) copy-start(s32[4,8]{1,0:T(4,128)} %mask_ref.9) | copy-start | bytes 388
  2.5 12.7 %collective-permute-start.7 = (bf16[640,256]{1,0:T(8,128)(2,1)S(1)}, bf16[640,256]{1,0:T(8,128)(2,1)S(1)}, u32[]{:S(2)}, u32[]{:S(2)}) collective-permute-start(bf16[640,256]{1,0:T(8,128)(2,1)S(1)} %get-tuple-element.25), channel_id=1, source_target_pairs={{0,16},{16,24},{32,48},{48,56},{64,80},{80,88},{96,112},{112,120},... | collective-permute-start | bytes 983048 | tf_op jit(solution)/shard_map/ppermute | solution.py:299
  5.4 17.1 %collective-permute-start = (bf16[1024,256]{1,0:T(8,128)(2,1)S(1)}, bf16[1024,256]{1,0:T(8,128)(2,1)S(1)}, u32[]{:S(2)}, u32[]{:S(2)}) collective-permute-start(bf16[1024,256]{1,0:T(8,128)(2,1)S(1)} %get-tuple-element.15.kv_ref), channel_id=1, source_target_pairs={{0,128},{8,136},{16,144},{24,152},{32,160},{40,168},{48,176},{56,1... | collective-permute-start | bytes 1572872 | tf_op jit(solution)/shard_map/ppermute | solution.py:299
  9.6 23.9 %collective-permute-start.1 = (bf16[1024,256]{1,0:T(8,128)(2,1)S(1)}, bf16[1024,256]{1,0:T(8,128)(2,1)S(1)}, u32[]{:S(2)}, u32[]{:S(2)}) collective-permute-start(bf16[1024,256]{1,0:T(8,128)(2,1)S(1)} %get-tuple-element.15.kv_ref), channel_id=1, source_target_pairs={{0,64},{8,72},{16,80},{24,88},{32,96},{40,104},{48,112},{56,120},{... | collective-permute-start | bytes 1572872 | tf_op jit(solution)/shard_map/ppermute | solution.py:299
  10.9 11.5 %collective-permute-start.8 = (bf16[640,256]{1,0:T(8,128)(2,1)S(1)}, bf16[640,256]{1,0:T(8,128)(2,1)S(1)}, u32[]{:S(2)}, u32[]{:S(2)}) collective-permute-start(bf16[640,256]{1,0:T(8,128)(2,1)S(1)} %get-tuple-element.25), channel_id=1, source_target_pairs={{0,8},{8,24},{32,40},{40,56},{64,72},{72,88},{96,104},{104,120},{1... | collective-permute-start | bytes 983048 | tf_op jit(solution)/shard_map/ppermute | solution.py:299
  11.6 25.4 %collective-permute-start.9 = (bf16[640,256]{1,0:T(8,128)(2,1)S(1)}, bf16[640,256]{1,0:T(8,128)(2,1)S(1)}, u32[]{:S(2)}, u32[]{:S(2)}) collective-permute-start(bf16[640,256]{1,0:T(8,128)(2,1)S(1)} %get-tuple-element.25), channel_id=1, source_target_pairs={{0,32},{8,40},{24,56},{64,96},{72,104},{88,120},{128,160},{136,168... | collective-permute-start | bytes 983048 | tf_op jit(solution)/shard_map/ppermute | solution.py:310
  15.1 21.9 %collective-permute-start.10 = (bf16[640,256]{1,0:T(8,128)(2,1)S(1)}, bf16[640,256]{1,0:T(8,128)(2,1)S(1)}, u32[]{:S(2)}, u32[]{:S(2)}) collective-permute-start(bf16[640,256]{1,0:T(8,128)(2,1)S(1)} %collective-permute-done.7.refs_0_), channel_id=1, source_target_pairs={{24,48},{88,112},{152,176},{216,240},{25,49},{89,113},{153,177},{2... | collective-permute-start | bytes 983048 | tf_op jit(solution)/shard_map/ppermute | solution.py:311
  16.4 0.7 copy-start.6
  22.5 14.5 %copy-start.1 = (bf16[1024,256]{1,0:T(8,128)(2,1)}, bf16[1024,256]{1,0:T(8,128)(2,1)S(1)}, u32[]{:S(2)}) copy-start(bf16[1024,256]{1,0:T(8,128)(2,1)S(1)} %collective-permute-done.refs_0_.refs_2_) | copy-start | bytes 1572868
  33.5 3.5 %copy-start.3 = (bf16[1024,256]{1,0:T(8,128)(2,1)}, bf16[1024,256]{1,0:T(8,128)(2,1)S(1)}, u32[]{:S(2)}) copy-start(bf16[1024,256]{1,0:T(8,128)(2,1)S(1)} %collective-permute-done.1.refs_1_.refs_3_) | copy-start | bytes 1572868
  39.2 1.0 %copy-start = (bf16[1024,512]{1,0:T(8,128)(2,1)}, bf16[1024,512]{1,0:T(8,128)(2,1)S(1)}, u32[]{:S(2)}) copy-start(bf16[1024,512]{1,0:T(8,128)(2,1)S(1)} %far.7) | copy-start | bytes 3145732
  40.1 35.5 %all-to-all-start = ((bf16[8,128,512]{2,1,0:T(8,128)(2,1)}), bf16[8,128,512]{2,1,0:T(8,128)(2,1)}, u32[]{:S(2)}, u32[]{:S(2)}) async-start(bf16[8,128,512]{2,1,0:T(8,128)(2,1)} %bitcast.4), calls=%async_computation | async-start | bytes 2097152 | tf_op jit(solution)/shard_map/all_to_all | solution.py:317
  44.4 10.6 %collective-permute-start.2 = (bf16[384,256]{1,0:T(8,128)(2,1)S(1)}, bf16[384,256]{1,0:T(8,128)(2,1)S(1)}, u32[]{:S(2)}, u32[]{:S(2)}) collective-permute-start(bf16[384,256]{1,0:T(8,128)(2,1)S(1)} %get-tuple-element.21), channel_id=1, source_target_pairs={{0,16},{16,24},{32,48},{48,56},{64,80},{80,88},{96,112},{112,120},... | collective-permute-start | bytes 589832 | tf_op jit(solution)/shard_map/ppermute | solution.py:299
  46.4 8.7 %collective-permute-start.3 = (bf16[384,256]{1,0:T(8,128)(2,1)S(1)}, bf16[384,256]{1,0:T(8,128)(2,1)S(1)}, u32[]{:S(2)}, u32[]{:S(2)}) collective-permute-start(bf16[384,256]{1,0:T(8,128)(2,1)S(1)} %get-tuple-element.21), channel_id=1, source_target_pairs={{0,8},{8,24},{32,40},{40,56},{64,72},{72,88},{96,104},{104,120},{1... | collective-permute-start | bytes 589832 | tf_op jit(solution)/shard_map/ppermute | solution.py:299
  47.0 20.5 %collective-permute-start.4 = (bf16[384,256]{1,0:T(8,128)(2,1)S(1)}, bf16[384,256]{1,0:T(8,128)(2,1)S(1)}, u32[]{:S(2)}, u32[]{:S(2)}) collective-permute-start(bf16[384,256]{1,0:T(8,128)(2,1)S(1)} %get-tuple-element.21), channel_id=1, source_target_pairs={{0,32},{8,40},{16,48},{24,56},{64,96},{72,104},{80,112},{88,120},{... | collective-permute-start | bytes 589832 | tf_op jit(solution)/shard_map/ppermute | solution.py:299
  48.3 1.0 %copy-start.2 = (bf16[1024,256]{1,0:T(8,128)(2,1)S(1)}, bf16[1024,256]{1,0:T(8,128)(2,1)}, u32[]{:S(2)}) copy-start(bf16[1024,256]{1,0:T(8,128)(2,1)} %copy-done.1) | copy-start | bytes 1572868
  49.4 1.0 %copy-start.4 = (bf16[1024,256]{1,0:T(8,128)(2,1)S(1)}, bf16[1024,256]{1,0:T(8,128)(2,1)}, u32[]{:S(2)}) copy-start(bf16[1024,256]{1,0:T(8,128)(2,1)} %copy-done.3) | copy-start | bytes 1572868
  52.2 19.1 %copy-start.8 = (bf16[4096]{0:T(1024)(128)(2,1)S(1)}, bf16[4096]{0:T(1024)(128)(2,1)}, u32[]{:S(2)}) copy-start(bf16[4096]{0:T(1024)(128)(2,1)} %param.11) | copy-start | bytes 24580
  69.7 1.6 %collective-permute-start.5 = (bf16[128,512]{1,0:T(8,128)(2,1)S(1)}, bf16[128,512]{1,0:T(8,128)(2,1)S(1)}, u32[]{:S(2)}, u32[]{:S(2)}) collective-permute-start(bf16[128,512]{1,0:T(8,128)(2,1)S(1)} %get-tuple-element.23), channel_id=1, source_target_pairs={{0,1},{1,0},{2,3},{3,2},{4,5},{5,4},{6,7},{7,6},{8,9},{9,8},{10,11... | collective-permute-start | bytes 393224 | tf_op jit(solution)/shard_map/ppermute | solution.py:302
  69.8 5.8 %collective-permute-start.6 = (bf16[128,512]{1,0:T(8,128)(2,1)S(1)}, bf16[128,512]{1,0:T(8,128)(2,1)S(1)}, u32[]{:S(2)}, u32[]{:S(2)}) collective-permute-start(bf16[128,512]{1,0:T(8,128)(2,1)S(1)} %get-tuple-element.24), channel_id=1, source_target_pairs={{0,2},{1,3},{2,0},{3,1},{4,6},{5,7},{6,4},{7,5},{8,10},{9,11},{10,... | collective-permute-start | bytes 393224 | tf_op jit(solution)/shard_map/ppermute | solution.py:302
  75.7 1.2 %copy-start.5 = (bf16[128,4096]{1,0:T(8,128)(2,1)S(1)}, bf16[128,4096]{1,0:T(8,128)(2,1)}, u32[]{:S(2)}) copy-start(bf16[128,4096]{1,0:T(8,128)(2,1)} %refs_4_.1) | copy-start | bytes 3145732

commit v3 on v2

v3 whole, which is shorter than its diff:
```python
import functools

import jax
import jax.numpy as jnp
from jax import lax
from jax.experimental import pallas as pl
from jax.experimental.pallas import tpu as pltpu
from jax.sharding import PartitionSpec as P

DH = 128
BLOCK = 128
BLOCKS = 8
HEADS = 4
EPSILON = 1e-05
NEG = -1e30
KERNEL_VMEM = 16 * 2**20
SCALE = DH ** (-0.5) * 1.4426950408889634
LATE = 2
FIRST = 2
SWAPS = [n for n in (6, 4, 7, 5, 3, 2) if n >= LATE]


NEAR, SIDE, HALF, FOURTH, THIRD = 1, 2, 3, 4, 5
SIDE_ONWARD, HALF_STRAIGHT = 6, 7


def slots(size):
    pairs = {slot: [] for slot in (NEAR, SIDE, HALF, FOURTH, THIRD)}
    for i in range(size):
        low = i & 3
        for slot, bit, taken in (
            (NEAR, 0, low == 3),
            (NEAR, 1, low == 2),
            (SIDE, 0, low == 1),
            (SIDE, 1, low == 3),
            (HALF, 2, i & 4),
            (THIRD, 3, i & 8),
            (FOURTH, 4, i & 16),
        ):
            if taken:
                pairs[slot].append((i - 2**bit, i))
    return pairs


def slot_level(slot, ctx, local_bits):
    bit = [lax.shift_right_logical(ctx, b) & 1 for b in range(5)]
    six = bit[2] & bit[1] & (1 - bit[0])
    taken, level = {
        SIDE_ONWARD: (bit[0] | six, jnp.where(six == 1, 2, bit[1])),
        HALF_STRAIGHT: (bit[2] & (1 - six), 2),
        NEAR: (bit[1], 1 - bit[0]),
        SIDE: (bit[0], bit[1]),
        HALF: (bit[2], 2),
        FOURTH: (bit[4], 4),
        THIRD: (bit[3], 3),
    }[slot]
    return jnp.where(taken == 1, local_bits + level, 31)


def held_in(space, *arrays):
    return [pltpu.with_memory_space_constraint(array, space) for array in arrays]


def params():
    return pltpu.CompilerParams(vmem_limit_bytes=KERNEL_VMEM)


def rows_at(index):
    return pl.ds(pl.multiple_of(index * BLOCK, BLOCK), BLOCK)


def in_vmem():
    return pl.BlockSpec(memory_space=pltpu.VMEM)


def order_kernel(info_ref, k_hbm, v_hbm, q_hbm, all_ref, late_ref, rest_ref, q_ref, k_ref, v_ref, sems):
    rank = info_ref[0, 0]
    copies = [pltpu.make_async_copy(k_hbm, k_ref, sems.at[0, 0]), pltpu.make_async_copy(v_hbm, v_ref, sems.at[0, 1])]
    for n in range(BLOCKS):
        for h in range(HEADS):
            source = q_hbm.at[rows_at(rank ^ n), h * DH : (h + 1) * DH]
            copies.append(
                pltpu.make_async_copy(source, q_ref.at[n, h * BLOCK : (h + 1) * BLOCK, :], sems.at[1 + n, h])
            )
    for copy in copies:
        copy.start()
    for copy in copies[:2]:
        copy.wait()
    for n in range(BLOCKS):
        source = rows_at(rank ^ n)
        key, val = k_ref[source, :], v_ref[source, :].T
        part, at = (late_ref, n) if n < LATE else (rest_ref, n - LATE)
        for ref, first in ((all_ref, n), (part, at)):
            ref[first * BLOCK : (first + 1) * BLOCK, :DH] = key
            ref[first * BLOCK : (first + 1) * BLOCK, DH:] = val
    for copy in copies[2:]:
        copy.wait()


def ordered(info, keys, values, queries):
    rows = keys.shape[0]
    hbm = pl.BlockSpec(memory_space=pl.ANY)
    return pl.pallas_call(
        order_kernel,
        in_specs=[pl.BlockSpec(memory_space=pltpu.SMEM), hbm, hbm, hbm],
        out_specs=[in_vmem()] * 4,
        out_shape=[
            jax.ShapeDtypeStruct((n, 2 * DH), jnp.bfloat16)
            for n in (rows, LATE * BLOCK, rows - LATE * BLOCK)
        ]
        + [jax.ShapeDtypeStruct((BLOCKS, HEADS * BLOCK, DH), jnp.bfloat16)],
        scratch_shapes=[pltpu.VMEM(keys.shape, jnp.bfloat16)] * 2 + [pltpu.SemaphoreType.DMA((1 + BLOCKS, HEADS))],
        compiler_params=params(),
        name="order",
    )(info, *held_in(pltpu.HBM, keys, values, queries))


def attend(q, keys, vals, biases, causal=None, before=None):
    scores = lax.dot_general(
        jnp.concatenate(keys, 0), q, (((1,), (1,)), ((), ())), preferred_element_type=jnp.float32
    )
    parts = [scores[n * BLOCK : (n + 1) * BLOCK, :] for n in range(len(keys))]
    if causal is not None:
        parts[0] = jnp.where(causal, parts[0], NEG)
    tops = [part.max(0, keepdims=True) * SCALE + bias for part, bias in zip(parts, biases)]
    top = functools.reduce(jnp.maximum, tops if before is None else [before[1]] + tops)
    weights = [jnp.exp2(part * SCALE - (top - bias)) for part, bias in zip(parts, biases)]
    total = functools.reduce(jnp.add, weights).sum(0, keepdims=True)
    weight = jnp.concatenate([w.astype(jnp.bfloat16) for w in weights], 0)
    summed = jnp.dot(jnp.concatenate(vals, 1), weight, preferred_element_type=jnp.float32)
    if before is not None:
        factor = jnp.exp2(before[1] - top)
        total = total + before[2] * factor
        summed = summed + before[0] * factor
    return summed, top, total


def bitmap_at(info_ref, h, j):
    return info_ref[1 + h, j]


def bias_of(bitmaps, level):
    pieces = []
    for bitmap in bitmaps:
        allowed = lax.shift_right_logical(bitmap, level) & 1
        pieces.append(jnp.full((1, BLOCK), (1 - allowed).astype(jnp.float32) * NEG))
    return jnp.concatenate(pieces, 1)


def local_kernel(first, count, turn, info_ref, q_ref, kv_ref, *refs):
    part_ref, stat_ref = refs[-2:]
    rank = info_ref[0, 0]

    def body():
        shape = (BLOCK, HEADS * BLOCK)
        causal = lax.broadcasted_iota(jnp.int32, shape, 0) <= (
            lax.broadcasted_iota(jnp.int32, shape, 1) & (BLOCK - 1)
        )
        for i in range(count):
            n = first + i
            j = rank ^ n
            levels = range(BLOCKS.bit_length() - 1)
            others = [n] + [n ^ 2**b for b in levels]
            held = [kv_ref[m * BLOCK : (m + 1) * BLOCK, :] for m in others]
            bitmaps = [bitmap_at(info_ref, h, j) & j for h in range(HEADS)]
            biases = [0.0] + [bias_of(bitmaps, level) for level in levels]
            summed, top, total = attend(
                q_ref[n], [kv[:, :DH] for kv in held], [kv[:, DH:] for kv in held], biases, causal
            )
            part_ref[i] = summed
            stat_ref[i, 0:1, :] = top
            stat_ref[i, 1:2, :] = total

    if turn is None:
        body()
    else:
        pl.when(((info_ref[0, 1] & 7) < FIRST) == (turn == 0))(body)


def local_part(info, queries, kv, first, count, turn=None, state=()):
    width = HEADS * DH
    return pl.pallas_call(
        functools.partial(local_kernel, first, count, turn),
        in_specs=[pl.BlockSpec(memory_space=pltpu.SMEM)] + [in_vmem()] * (2 + len(state)),
        out_specs=[in_vmem()] * 2,
        out_shape=[
            jax.ShapeDtypeStruct((count, DH, width), jnp.float32),
            jax.ShapeDtypeStruct((count, 8, width), jnp.float32),
        ],
        input_output_aliases={3 + n: n for n in range(len(state))},
        cost_estimate=pl.CostEstimate(
            flops=4 * 4 * count * BLOCK * width * BLOCK, bytes_accessed=4_000_000, transcendentals=4 * count * BLOCK * width
        ),
        compiler_params=params(),
        name="local",
    )(info, queries, kv, *state)


def far_kernel(held, first, count, final, info_ref, q_ref, part_ref, stat_ref, *refs):
    arrays = sum(number for _, number in held)
    kv_refs, outs = refs[:arrays], refs[arrays:]
    levels = [slot_level(slot, info_ref[0, 1], BLOCKS.bit_length() - 1) for slot, _ in held]
    blocks = [n - first for n in final] if final else range(count)
    for place, i in enumerate(blocks):
        j = info_ref[0, 0] ^ (first + i)
        keys, vals, rest = [], [], kv_refs
        for _, number in held:
            tiles = []
            for ref in rest[:number]:
                at = (first + i if ref.shape[0] == BLOCKS * BLOCK else i) * BLOCK
                tiles.append(ref[at : at + BLOCK, :])
            rest = rest[number:]
            tile = functools.reduce(jnp.add, tiles)
            keys.append(tile[:, :DH])
            vals.append(tile[:, DH:])
        bitmaps = [bitmap_at(info_ref, h, j) for h in range(HEADS)]
        biases = [bias_of(bitmaps, level) for level in levels]
        before = (part_ref[i], stat_ref[i, 0:1, :], stat_ref[i, 1:2, :])
        summed, top, total = attend(q_ref[first + i], keys, vals, biases, None, before)
        if final:
            result = summed * (1.0 / total)
            for h in range(HEADS):
                at = slice(h * DH, (h + 1) * DH)
                outs[place][:, at] = result[:, at].T.astype(jnp.bfloat16)
        else:
            outs[0][i] = summed
            outs[1][i, 0:1, :] = top
            outs[1][i, 1:2, :] = total


def far_part(info, queries, state, fetched, held, first, final=()):
    part, stats = state
    count, _, width = part.shape
    kvs, numbers = [], []
    for slot in held:
        arrays = fetched[slot] if isinstance(fetched[slot], list) else [fetched[slot]]
        kvs += arrays
        numbers.append((slot, len(arrays)))
    if final:
        out_shape = [jax.ShapeDtypeStruct((BLOCK, width), jnp.bfloat16)] * len(final)
    else:
        out_shape = [
            jax.ShapeDtypeStruct((count, DH, width), jnp.float32),
            jax.ShapeDtypeStruct((count, 8, width), jnp.float32),
        ]
    outs = pl.pallas_call(
        functools.partial(far_kernel, numbers, first, count, final),
        in_specs=[pl.BlockSpec(memory_space=pltpu.SMEM)] + [in_vmem()] * (3 + len(kvs)),
        out_specs=[in_vmem()] * len(out_shape),
        out_shape=out_shape,
        cost_estimate=pl.CostEstimate(
            flops=len(kvs) * 4 * count * BLOCK * width * BLOCK,
            bytes_accessed=4_000_000,
            transcendentals=len(kvs) * count * BLOCK * width,
        ),
        compiler_params=params(),
        name="far",
    )(info, *held_in(pltpu.VMEM, queries, part, stats, *kvs))
    return list(outs)


def norm_kernel(info_ref, *refs):
    parts = refs[:BLOCKS]
    res_ref, gain_ref, stream_hbm, normed_hbm, whole, stream_ref, normed_ref, sems = refs[BLOCKS:]
    width = parts[0].shape[1]
    square = jnp.zeros((BLOCK, DH), jnp.float32)
    copies = []
    for n in range(BLOCKS):
        source = info_ref[0, 0] ^ n
        cols = pl.ds(pl.multiple_of(source * width, width), width)
        summed = res_ref[:, cols].astype(jnp.float32) + parts[n][...].astype(jnp.float32)
        stream_ref[n] = summed.astype(jnp.bfloat16)
        copies.append(pltpu.make_async_copy(stream_ref.at[n], stream_hbm.at[:, cols], sems.at[0, n]))
        copies[-1].start()
        whole[n] = summed
        for c in range(0, width, DH):
            piece = summed[:, c : c + DH]
            square = square + piece * piece
    mean = square.sum(-1, keepdims=True) / (BLOCKS * width)
    factor = lax.rsqrt(mean + EPSILON)
    for n in range(BLOCKS):
        source = info_ref[0, 0] ^ n
        cols = pl.ds(pl.multiple_of(source * width, width), width)
        normed_ref[n] = (whole[n] * factor * gain_ref[:, cols].astype(jnp.float32)).astype(jnp.bfloat16)
        copies.append(pltpu.make_async_copy(normed_ref.at[n], normed_hbm.at[:, cols], sems.at[1, n]))
        copies[-1].start()
    for copy in copies:
        copy.wait()


def norm_part(info, parts, residual, gain):
    width = parts[0].shape[1]
    return pl.pallas_call(
        norm_kernel,
        in_specs=[pl.BlockSpec(memory_space=pltpu.SMEM)] + [in_vmem()] * (len(parts) + 2),
        out_specs=[pl.BlockSpec(memory_space=pl.ANY)] * 2,
        out_shape=[jax.ShapeDtypeStruct(residual.shape, jnp.bfloat16)] * 2,
        scratch_shapes=[
            pltpu.VMEM((BLOCKS, BLOCK, width), jnp.float32),
            pltpu.VMEM((BLOCKS, BLOCK, width), jnp.bfloat16),
            pltpu.VMEM((BLOCKS, BLOCK, width), jnp.bfloat16),
            pltpu.SemaphoreType.DMA((2, BLOCKS)),
        ],
        cost_estimate=pl.CostEstimate(flops=4_000_000, bytes_accessed=4_000_000, transcendentals=128),
        compiler_params=params(),
        name="norm",
    )(info, *held_in(pltpu.VMEM, *parts), residual, gain)


def shards(queries, keys, values, block_masks, residual, norm_gain):
    groups = lax.axis_size("head")
    routes = slots(lax.axis_size("ctx"))
    at = lax.broadcasted_iota(jnp.int32, (1, BLOCKS), 1)
    place = jnp.where(at == 0, lax.axis_index("head"), lax.axis_index("ctx")).astype(jnp.int32)
    info = jnp.concatenate([place, block_masks], 0)

    def fetched(array, slot):
        return lax.ppermute(array, "ctx", routes[slot])

    def swapped(array, n):
        return lax.ppermute(array, "head", [(i, i ^ n) for i in range(groups)])

    by_three = [(i - 3, i) for i in range(lax.axis_size("ctx")) if i & 7 == 6]

    kv, kv_late, kv_rest, queries = ordered(info, keys, values, queries)
    far = {slot: fetched(kv, slot) for slot in (FOURTH, THIRD)}
    rest = far | {slot: fetched(kv_rest, slot) for slot in (NEAR, SIDE)}
    straight = [(i, j) for i, j in routes[HALF] if j & 7 != 6]
    rest[HALF_STRAIGHT] = lax.ppermute(kv_rest, "ctx", straight)
    rest[SIDE_ONWARD] = [rest[SIDE], lax.ppermute(rest[NEAR], "ctx", by_three)]
    late = far | {slot: fetched(kv_late, slot) for slot in (NEAR, SIDE, HALF)}
    far_blocks = BLOCKS - LATE
    state = local_part(info, queries, kv, LATE, far_blocks, 0)
    state = local_part(info, queries, kv, LATE, far_blocks, 1, state)
    late_state = local_part(info, queries, kv, 0, LATE)
    state = far_part(info, queries, state, rest, (NEAR, HALF_STRAIGHT, FOURTH, THIRD), LATE)
    sent = {}
    for some in (SWAPS[:2], SWAPS[2:]):
        sent |= zip(some, far_part(info, queries, state, rest, (SIDE_ONWARD,), LATE, some))
    late_state = far_part(info, queries, late_state, late, (FOURTH, THIRD), 0)
    parts = far_part(info, queries, late_state, late, (NEAR, SIDE, HALF), 0, range(LATE))
    parts += [sent[n] for n in range(LATE, BLOCKS)]
    parts = parts[:1] + [swapped(parts[n], n) for n in range(1, BLOCKS)]
    return norm_part(info, parts, residual, norm_gain.reshape(1, -1))


def solution(mesh):
    in_specs = (
        P("ctx", "head"),
        P("ctx", "head"),
        P("ctx", "head"),
        P("head", "ctx"),
        P(("ctx", "head"), None),
        P(),
    )
    out_specs = (P(("ctx", "head"), None), P(("ctx", "head"), None))
    return jax.shard_map(shards, mesh=mesh, in_specs=in_specs, out_specs=out_specs, check_vma=False)
```

time: 80.7 us -> 85.2 us (1.056)
  the two profiles are of different devices: /device:TPU:200 before, /device:TPU:193 now
where the time goes in v3:
time: 85.2 us; the launch traced here: 84.9 us
  waiting for transfers between devices  36.6 us (43%)
  starting transfers between devices  25.2 us (30%)
  Pallas kernels  21.4 us (25%)
  between operations  1 us (1%)
    ppermute x7, waiting for transfers between devices, fetched(): return lax.ppermute(array, 'ctx', routes[slot])  24.7 us
    ppermute x7, starting transfers between devices, fetched(): return lax.ppermute(array, 'ctx', routes[slot])  14.4 us
    ppermute x7, waiting for transfers between devices, swapped(): return lax.ppermute(array, 'head', [(i, i ^ n) for i in range(groups)])  11.9 us
    pallas_call x5, Pallas kernels, far_part(): pl.pallas_call(functools.partial(far_kernel, numbers, first, count, final...  10.4 us
    ppermute x7, starting transfers between devices, swapped(): return lax.ppermute(array, 'head', [(i, i ^ n) for i in range(groups)])  8.8 us
    pallas_call x3, Pallas kernels, local_part(): pl.pallas_call(functools.partial(local_kernel, first, count, turn), in_sp...  6.42 us
    pallas_call x1, Pallas kernels, norm_part(): pl.pallas_call(norm_kernel, in_specs=[pl.BlockSpec(memory_space=pltpu.SME...  2.41 us
    pallas_call x1, Pallas kernels, ordered(): pl.pallas_call(order_kernel, in_specs=[pl.BlockSpec(memory_space=pltpu.SM...  2.21 us
  transfers between devices with their start and end apart: 16, of which 7 were waited for; matrix products, arithmetic and copies ran while one was open for 0% of the time, Pallas kernels for 20%

profile of v3, /device:TPU:193, one launch (start us, length us, event | category | flops | bytes accessed | tf_op | source)
XLA Modules:
  0.0 84.9 jit_solution(4358461193289396714)
XLA Ops:
  1.3 2.2 %order.1 = (bf16[1024,256]{1,0:T(8,128)(2,1)S(1)}, bf16[256,256]{1,0:T(8,128)(2,1)S(1)}, bf16[768,256]{1,0:T(8,128)(2,1)S(1)}, bf16[8,512,128]{2,1,0:T(8,128)(2,1)S(1)}) custom-call(s32[5,8]{1,0:T(8,128)S(1)} %pad_add_fusion.info_ref, bf16[1024,128]{1,0:T(8,128)(2,1)} %k_hbm.1, bf16[1024,128]{1,0:T(8,128)(2,1)} %v_hbm.1, bf16[1024,512]{1,0:T(8,128)(2,1)} %q_hbm.1), custom_call_target="tpu_custom_call" | custom-call | tf_op jit(solution)/shard_map/order/pallas_call | solution.py:103
  3.6 4.9 %collective-permute-start = (bf16[1024,256]{1,0:T(8,128)(2,1)S(1)}, bf16[1024,256]{1,0:T(8,128)(2,1)S(1)}, u32[]{:S(2)}, u32[]{:S(2)}) collective-permute-start(bf16[1024,256]{1,0:T(8,128)(2,1)S(1)} %get-tuple-element.25.kv_ref), channel_id=1, source_target_pairs={{0,128},{8,136},{16,144},{24,152},{32,160},{40,168},{48,176},{56,1... | collective-permute-start | bytes 1572872 | tf_op jit(solution)/shard_map/ppermute | solution.py:318
  8.4 2.3 %collective-permute-start.1 = (bf16[1024,256]{1,0:T(8,128)(2,1)S(1)}, bf16[1024,256]{1,0:T(8,128)(2,1)S(1)}, u32[]{:S(2)}, u32[]{:S(2)}) collective-permute-start(bf16[1024,256]{1,0:T(8,128)(2,1)S(1)} %get-tuple-element.25.kv_ref), channel_id=1, source_target_pairs={{0,64},{8,72},{16,80},{24,88},{32,96},{40,104},{48,112},{56,120},{... | collective-permute-start | bytes 1572872 | tf_op jit(solution)/shard_map/ppermute | solution.py:318
  10.8 2.6 %collective-permute-start.6 = (bf16[768,256]{1,0:T(8,128)(2,1)S(1)}, bf16[768,256]{1,0:T(8,128)(2,1)S(1)}, u32[]{:S(2)}, u32[]{:S(2)}) collective-permute-start(bf16[768,256]{1,0:T(8,128)(2,1)S(1)} %get-tuple-element.37), channel_id=1, source_target_pairs={{0,16},{16,24},{32,48},{48,56},{64,80},{80,88},{96,112},{112,120},... | collective-permute-start | bytes 1179656 | tf_op jit(solution)/shard_map/ppermute | solution.py:318
  13.4 1.9 %collective-permute-start.2 = (bf16[256,256]{1,0:T(8,128)(2,1)S(1)}, bf16[256,256]{1,0:T(8,128)(2,1)S(1)}, u32[]{:S(2)}, u32[]{:S(2)}) collective-permute-start(bf16[256,256]{1,0:T(8,128)(2,1)S(1)} %get-tuple-element.30), channel_id=1, source_target_pairs={{0,16},{16,24},{32,48},{48,56},{64,80},{80,88},{96,112},{112,120},... | collective-permute-start | bytes 393224 | tf_op jit(solution)/shard_map/ppermute | solution.py:318
  16.0 9.8 %collective-permute-done.2.refs_0_ = bf16[256,256]{1,0:T(8,128)(2,1)S(1)} collective-permute-done((bf16[256,256]{1,0:T(8,128)(2,1)S(1)}, bf16[256,256]{1,0:T(8,128)(2,1)S(1)}, u32[]{:S(2)}, u32[]{:S(2)}) %collective-permute-start.2) | collective-permute-done | bytes 131104 | tf_op jit(solution)/shard_map/ppermute | solution.py:318
  26.5 1.3 %collective-permute-start.9 = (bf16[768,256]{1,0:T(8,128)(2,1)S(1)}, bf16[768,256]{1,0:T(8,128)(2,1)S(1)}, u32[]{:S(2)}, u32[]{:S(2)}) collective-permute-start(bf16[768,256]{1,0:T(8,128)(2,1)S(1)} %collective-permute-done.6.refs_0_), channel_id=1, source_target_pairs={{24,48},{88,112},{152,176},{216,240},{25,49},{89,113},{153,177},{2... | collective-permute-start | bytes 1179656 | tf_op jit(solution)/shard_map/ppermute | solution.py:330
  28.5 1.7 %collective-permute-done.1.refs_1_.refs_3_ = bf16[1024,256]{1,0:T(8,128)(2,1)S(1)} collective-permute-done((bf16[1024,256]{1,0:T(8,128)(2,1)S(1)}, bf16[1024,256]{1,0:T(8,128)(2,1)S(1)}, u32[]{:S(2)}, u32[]{:S(2)}) %collective-permute-start.1) | collective-permute-done | bytes 524320 | tf_op jit(solution)/shard_map/ppermute | solution.py:318
  32.1 1.8 %local.3 = (f32[2,128,512]{2,1,0:T(8,128)S(1)}, f32[2,8,512]{2,1,0:T(8,128)S(1)}) custom-call(s32[5,8]{1,0:T(8,128)S(1)} %pad_add_fusion.info_ref, bf16[8,512,128]{2,1,0:T(8,128)(2,1)S(1)} %get-tuple-element.24.q_ref, bf16[1024,256]{1,0:T(8,128)(2,1)S(1)} %get-tuple-element.25.kv_ref), custom_call_target="tpu_custom_call" | custom-call | flops 268435456 | bytes 4000000 | tf_op jit(solution)/shard_map/local/pallas_call | solution.py:182
  34.0 4.0 %local.5 = (f32[6,128,512]{2,1,0:T(8,128)S(1)}, f32[6,8,512]{2,1,0:T(8,128)S(1)}) custom-call(s32[5,8]{1,0:T(8,128)S(1)} %pad_add_fusion.info_ref, bf16[8,512,128]{2,1,0:T(8,128)(2,1)S(1)} %get-tuple-element.24.q_ref, bf16[1024,256]{1,0:T(8,128)(2,1)S(1)} %get-tuple-element.25.kv_ref, ...), custom_call_target="tpu_custom_call", output_to_operand_aliasing={{0}: (3, {}), {1}: (4, {})} | custom-call | flops 805306368 | bytes 4000000 | tf_op jit(solution)/shard_map/local/pallas_call | solution.py:182
  37.9 1.5 %far.5 = (f32[2,128,512]{2,1,0:T(8,128)S(1)}, f32[2,8,512]{2,1,0:T(8,128)S(1)}) custom-call(s32[5,8]{1,0:T(8,128)S(1)} %pad_add_fusion.info_ref, bf16[8,512,128]{2,1,0:T(8,128)(2,1)S(1)} %get-tuple-element.24.q_ref, f32[2,128,512]{2,1,0:T(8,128)S(1)} %get-tuple-element.26.part_ref, f32[2,8,512]{2,1,0:T(8,128)S(1)} %get-tuple-element.27.stat_ref, ...), custom_call_target="tpu_custom_call" | custom-call | flops 134217728 | bytes 4000000 | tf_op jit(solution)/shard_map/far/pallas_call | solution.py:246
  39.4 13.2 %collective-permute-done.4.refs_2_ = bf16[256,256]{1,0:T(8,128)(2,1)S(1)} collective-permute-done((bf16[256,256]{1,0:T(8,128)(2,1)S(1)}, bf16[256,256]{1,0:T(8,128)(2,1)S(1)}, u32[]{:S(2)}, u32[]{:S(2)}) %collective-permute-start.4) | collective-permute-done | bytes 131104 | tf_op jit(solution)/shard_map/ppermute | solution.py:318
  52.6 1.7 %far.6 = (bf16[128,512]{1,0:T(8,128)(2,1)S(1)}, bf16[128,512]{1,0:T(8,128)(2,1)S(1)}) custom-call(s32[5,8]{1,0:T(8,128)S(1)} %pad_add_fusion.info_ref, bf16[8,512,128]{2,1,0:T(8,128)(2,1)S(1)} %get-tuple-element.24.q_ref, f32[2,128,512]{2,1,0:T(8,128)S(1)} %get-tuple-element.28.part_ref, f32[2,8,512]{2,1,0:T(8,128)S(1)} %get-tuple-element.29.stat_ref, ...), custom_call_target="tpu_custom_call" | custom-call | flops 201326592 | bytes 4000000 | tf_op jit(solution)/shard_map/far/pallas_call | solution.py:246
  55.1 4.0 %far.7 = (f32[6,128,512]{2,1,0:T(8,128)S(1)}, f32[6,8,512]{2,1,0:T(8,128)S(1)}) custom-call(s32[5,8]{1,0:T(8,128)S(1)} %pad_add_fusion.info_ref, bf16[8,512,128]{2,1,0:T(8,128)(2,1)S(1)} %get-tuple-element.24.q_ref, f32[6,128,512]{2,1,0:T(8,128)S(1)} %get-tuple-element.35.part_ref, f32[6,8,512]{2,1,0:T(8,128)S(1)} %get-tuple-element.36.stat_ref, ...), custom_call_target="tpu_custom_call" | custom-call | flops 805306368 | bytes 4000000 | tf_op jit(solution)/shard_map/far/pallas_call | solution.py:246
  59.2 1.9 %far.8 = (bf16[128,512]{1,0:T(8,128)(2,1)S(1)}, bf16[128,512]{1,0:T(8,128)(2,1)S(1)}, bf16[128,512]{1,0:T(8,128)(2,1)S(1)}, bf16[128,512]{1,0:T(8,128)(2,1)S(1)}) custom-call(s32[5,8]{1,0:T(8,128)S(1)} %pad_add_fusion.info_ref, bf16[8,512,128]{2,1,0:T(8,128)(2,1)S(1)} %get-tuple-element.24.q_ref, f32[6,128,512]{2,1,0:T(8,128)S(1)} %get-tuple-element.38.part_ref, ...), custom_call_target="tpu_custom_call" | custom-call | flops 402653184 | bytes 4000000 | tf_op jit(solution)/shard_map/far/pallas_call | solution.py:246
  61.1 1.3 %collective-permute-start.10 = (bf16[128,512]{1,0:T(8,128)(2,1)S(1)}, bf16[128,512]{1,0:T(8,128)(2,1)S(1)}, u32[]{:S(2)}, u32[]{:S(2)}) collective-permute-start(bf16[128,512]{1,0:T(8,128)(2,1)S(1)} %get-tuple-element.40), channel_id=1, source_target_pairs={{0,2},{1,3},{2,0},{3,1},{4,6},{5,7},{6,4},{7,5},{8,10},{9,11},{10,... | collective-permute-start | bytes 393224 | tf_op jit(solution)/shard_map/ppermute | solution.py:321
  62.8 1.3 %far.9 = (bf16[128,512]{1,0:T(8,128)(2,1)S(1)}, bf16[128,512]{1,0:T(8,128)(2,1)S(1)}) custom-call(s32[5,8]{1,0:T(8,128)S(1)} %pad_add_fusion.info_ref, bf16[8,512,128]{2,1,0:T(8,128)(2,1)S(1)} %get-tuple-element.24.q_ref, f32[6,128,512]{2,1,0:T(8,128)S(1)} %get-tuple-element.38.part_ref, f32[6,8,512]{2,1,0:T(8,128)S(1)} %get-tuple-element.39.stat_ref, ...), custom_call_target="tpu_custom_call" | custom-call | flops 402653184 | bytes 4000000 | tf_op jit(solution)/shard_map/far/pallas_call | solution.py:246
  64.2 2.8 %collective-permute-start.12 = (bf16[128,512]{1,0:T(8,128)(2,1)S(1)}, bf16[128,512]{1,0:T(8,128)(2,1)S(1)}, u32[]{:S(2)}, u32[]{:S(2)}) collective-permute-start(bf16[128,512]{1,0:T(8,128)(2,1)S(1)} %get-tuple-element.42), channel_id=1, source_target_pairs={{0,4},{1,5},{2,6},{3,7},{4,0},{5,1},{6,2},{7,3},{8,12},{9,13},{10,... | collective-permute-start | bytes 393224 | tf_op jit(solution)/shard_map/ppermute | solution.py:321
  67.6 2.5 %collective-permute-start.14 = (bf16[128,512]{1,0:T(8,128)(2,1)S(1)}, bf16[128,512]{1,0:T(8,128)(2,1)S(1)}, u32[]{:S(2)}, u32[]{:S(2)}) collective-permute-start(bf16[128,512]{1,0:T(8,128)(2,1)S(1)} %get-tuple-element.44), channel_id=1, source_target_pairs={{0,6},{1,7},{2,4},{3,5},{4,2},{5,3},{6,0},{7,1},{8,14},{9,15},{10,... | collective-permute-start | bytes 393224 | tf_op jit(solution)/shard_map/ppermute | solution.py:321
  70.5 3.6 %collective-permute-done.12.refs_4_ = bf16[128,512]{1,0:T(8,128)(2,1)S(1)} collective-permute-done((bf16[128,512]{1,0:T(8,128)(2,1)S(1)}, bf16[128,512]{1,0:T(8,128)(2,1)S(1)}, u32[]{:S(2)}, u32[]{:S(2)}) %collective-permute-start.12) | collective-permute-done | bytes 131104 | tf_op jit(solution)/shard_map/ppermute | solution.py:321
  74.1 3.0 %collective-permute-done.13.refs_5_ = bf16[128,512]{1,0:T(8,128)(2,1)S(1)} collective-permute-done((bf16[128,512]{1,0:T(8,128)(2,1)S(1)}, bf16[128,512]{1,0:T(8,128)(2,1)S(1)}, u32[]{:S(2)}, u32[]{:S(2)}) %collective-permute-start.13) | collective-permute-done | bytes 131104 | tf_op jit(solution)/shard_map/ppermute | solution.py:321
  77.1 2.5 %collective-permute-done.14.refs_6_ = bf16[128,512]{1,0:T(8,128)(2,1)S(1)} collective-permute-done((bf16[128,512]{1,0:T(8,128)(2,1)S(1)}, bf16[128,512]{1,0:T(8,128)(2,1)S(1)}, u32[]{:S(2)}, u32[]{:S(2)}) %collective-permute-start.14) | collective-permute-done | bytes 131104 | tf_op jit(solution)/shard_map/ppermute | solution.py:321
  79.6 2.8 %collective-permute-done.15.refs_7_ = bf16[128,512]{1,0:T(8,128)(2,1)S(1)} collective-permute-done((bf16[128,512]{1,0:T(8,128)(2,1)S(1)}, bf16[128,512]{1,0:T(8,128)(2,1)S(1)}, u32[]{:S(2)}, u32[]{:S(2)}) %collective-permute-start.15) | collective-permute-done | bytes 131104 | tf_op jit(solution)/shard_map/ppermute | solution.py:321
  82.4 2.4 %norm.1 = (bf16[128,4096]{1,0:T(8,128)(2,1)}, bf16[128,4096]{1,0:T(8,128)(2,1)}) custom-call(s32[5,8]{1,0:T(8,128)S(1)} %pad_add_fusion.info_ref, bf16[128,512]{1,0:T(8,128)(2,1)S(1)} %get-tuple-element.31.refs_0_, bf16[128,512]{1,0:T(8,128)(2,1)S(1)} %collective-permute-done.5.refs_1_, bf16[128,512]{1,0:T(8,128)(2,1)S(1)} %collective-permute-done.10.refs_2_, ...), custom_call_target="tpu_custom_call" | custom-call | flops 4000000 | bytes 4000000 | tf_op jit(solution)/shard_map/norm/pallas_call | solution.py:293
  (25 shorter events, 6.8 us)
Async XLA Ops:
  3.6 24.2 %collective-permute-start = (bf16[1024,256]{1,0:T(8,128)(2,1)S(1)}, bf16[1024,256]{1,0:T(8,128)(2,1)S(1)}, u32[]{:S(2)}, u32[]{:S(2)}) collective-permute-start(bf16[1024,256]{1,0:T(8,128)(2,1)S(1)} %get-tuple-element.25.kv_ref), channel_id=1, source_target_pairs={{0,128},{8,136},{16,144},{24,152},{32,160},{40,168},{48,176},{56,1... | collective-permute-start | bytes 1572872 | tf_op jit(solution)/shard_map/ppermute | solution.py:318
  8.4 21.8 %collective-permute-start.1 = (bf16[1024,256]{1,0:T(8,128)(2,1)S(1)}, bf16[1024,256]{1,0:T(8,128)(2,1)S(1)}, u32[]{:S(2)}, u32[]{:S(2)}) collective-permute-start(bf16[1024,256]{1,0:T(8,128)(2,1)S(1)} %get-tuple-element.25.kv_ref), channel_id=1, source_target_pairs={{0,64},{8,72},{16,80},{24,88},{32,96},{40,104},{48,112},{56,120},{... | collective-permute-start | bytes 1572872 | tf_op jit(solution)/shard_map/ppermute | solution.py:318
  10.8 15.7 %collective-permute-start.6 = (bf16[768,256]{1,0:T(8,128)(2,1)S(1)}, bf16[768,256]{1,0:T(8,128)(2,1)S(1)}, u32[]{:S(2)}, u32[]{:S(2)}) collective-permute-start(bf16[768,256]{1,0:T(8,128)(2,1)S(1)} %get-tuple-element.37), channel_id=1, source_target_pairs={{0,16},{16,24},{32,48},{48,56},{64,80},{80,88},{96,112},{112,120},... | collective-permute-start | bytes 1179656 | tf_op jit(solution)/shard_map/ppermute | solution.py:318
  13.4 12.4 %collective-permute-start.2 = (bf16[256,256]{1,0:T(8,128)(2,1)S(1)}, bf16[256,256]{1,0:T(8,128)(2,1)S(1)}, u32[]{:S(2)}, u32[]{:S(2)}) collective-permute-start(bf16[256,256]{1,0:T(8,128)(2,1)S(1)} %get-tuple-element.30), channel_id=1, source_target_pairs={{0,16},{16,24},{32,48},{48,56},{64,80},{80,88},{96,112},{112,120},... | collective-permute-start | bytes 393224 | tf_op jit(solution)/shard_map/ppermute | solution.py:318
  15.3 39.8 %collective-permute-start.7 = (bf16[768,256]{1,0:T(8,128)(2,1)S(1)}, bf16[768,256]{1,0:T(8,128)(2,1)S(1)}, u32[]{:S(2)}, u32[]{:S(2)}) collective-permute-start(bf16[768,256]{1,0:T(8,128)(2,1)S(1)} %get-tuple-element.37), channel_id=1, source_target_pairs={{0,32},{8,40},{24,56},{64,96},{72,104},{88,120},{128,160},{136,168... | collective-permute-start | bytes 1179656 | tf_op jit(solution)/shard_map/ppermute | solution.py:329
  25.8 33.4 %collective-permute-start.8 = (bf16[768,256]{1,0:T(8,128)(2,1)S(1)}, bf16[768,256]{1,0:T(8,128)(2,1)S(1)}, u32[]{:S(2)}, u32[]{:S(2)}) collective-permute-start(bf16[768,256]{1,0:T(8,128)(2,1)S(1)} %get-tuple-element.37), channel_id=1, source_target_pairs={{0,8},{8,24},{32,40},{40,56},{64,72},{72,88},{96,104},{104,120},{1... | collective-permute-start | bytes 1179656 | tf_op jit(solution)/shard_map/ppermute | solution.py:318
  26.5 32.7 %collective-permute-start.9 = (bf16[768,256]{1,0:T(8,128)(2,1)S(1)}, bf16[768,256]{1,0:T(8,128)(2,1)S(1)}, u32[]{:S(2)}, u32[]{:S(2)}) collective-permute-start(bf16[768,256]{1,0:T(8,128)(2,1)S(1)} %collective-permute-done.6.refs_0_), channel_id=1, source_target_pairs={{24,48},{88,112},{152,176},{216,240},{25,49},{89,113},{153,177},{2... | collective-permute-start | bytes 1179656 | tf_op jit(solution)/shard_map/ppermute | solution.py:330
  27.8 11.6 %collective-permute-start.3 = (bf16[256,256]{1,0:T(8,128)(2,1)S(1)}, bf16[256,256]{1,0:T(8,128)(2,1)S(1)}, u32[]{:S(2)}, u32[]{:S(2)}) collective-permute-start(bf16[256,256]{1,0:T(8,128)(2,1)S(1)} %get-tuple-element.30), channel_id=1, source_target_pairs={{0,8},{8,24},{32,40},{40,56},{64,72},{72,88},{96,104},{104,120},{1... | collective-permute-start | bytes 393224 | tf_op jit(solution)/shard_map/ppermute | solution.py:318
  30.2 22.4 %collective-permute-start.4 = (bf16[256,256]{1,0:T(8,128)(2,1)S(1)}, bf16[256,256]{1,0:T(8,128)(2,1)S(1)}, u32[]{:S(2)}, u32[]{:S(2)}) collective-permute-start(bf16[256,256]{1,0:T(8,128)(2,1)S(1)} %get-tuple-element.30), channel_id=1, source_target_pairs={{0,32},{8,40},{16,48},{24,56},{64,96},{72,104},{80,112},{88,120},{... | collective-permute-start | bytes 393224 | tf_op jit(solution)/shard_map/ppermute | solution.py:318
  54.4 13.3 %collective-permute-start.5 = (bf16[128,512]{1,0:T(8,128)(2,1)S(1)}, bf16[128,512]{1,0:T(8,128)(2,1)S(1)}, u32[]{:S(2)}, u32[]{:S(2)}) collective-permute-start(bf16[128,512]{1,0:T(8,128)(2,1)S(1)} %get-tuple-element.32), channel_id=1, source_target_pairs={{0,1},{1,0},{2,3},{3,2},{4,5},{5,4},{6,7},{7,6},{8,9},{9,8},{10,11... | collective-permute-start | bytes 393224 | tf_op jit(solution)/shard_map/ppermute | solution.py:321
  61.1 9.0 %collective-permute-start.10 = (bf16[128,512]{1,0:T(8,128)(2,1)S(1)}, bf16[128,512]{1,0:T(8,128)(2,1)S(1)}, u32[]{:S(2)}, u32[]{:S(2)}) collective-permute-start(bf16[128,512]{1,0:T(8,128)(2,1)S(1)} %get-tuple-element.40), channel_id=1, source_target_pairs={{0,2},{1,3},{2,0},{3,1},{4,6},{5,7},{6,4},{7,5},{8,10},{9,11},{10,... | collective-permute-start | bytes 393224 | tf_op jit(solution)/shard_map/ppermute | solution.py:321
  62.4 8.1 %copy-start.1 = (bf16[4096]{0:T(1024)(128)(2,1)S(1)}, bf16[4096]{0:T(1024)(128)(2,1)}, u32[]{:S(2)}) copy-start(bf16[4096]{0:T(1024)(128)(2,1)} %param.11) | copy-start | bytes 24580
  62.4 20.0 %copy-start = (bf16[128,4096]{1,0:T(8,128)(2,1)S(1)}, bf16[128,4096]{1,0:T(8,128)(2,1)}, u32[]{:S(2)}) copy-start(bf16[128,4096]{1,0:T(8,128)(2,1)} %refs_8_.1) | copy-start | bytes 3145732
  62.4 8.1 %collective-permute-start.11 = (bf16[128,512]{1,0:T(8,128)(2,1)S(1)}, bf16[128,512]{1,0:T(8,128)(2,1)S(1)}, u32[]{:S(2)}, u32[]{:S(2)}) collective-permute-start(bf16[128,512]{1,0:T(8,128)(2,1)S(1)} %get-tuple-element.41), channel_id=1, source_target_pairs={{0,3},{1,2},{2,1},{3,0},{4,7},{5,6},{6,5},{7,4},{8,11},{9,10},{10,... | collective-permute-start | bytes 393224 | tf_op jit(solution)/shard_map/ppermute | solution.py:321
  64.2 9.9 %collective-permute-start.12 = (bf16[128,512]{1,0:T(8,128)(2,1)S(1)}, bf16[128,512]{1,0:T(8,128)(2,1)S(1)}, u32[]{:S(2)}, u32[]{:S(2)}) collective-permute-start(bf16[128,512]{1,0:T(8,128)(2,1)S(1)} %get-tuple-element.42), channel_id=1, source_target_pairs={{0,4},{1,5},{2,6},{3,7},{4,0},{5,1},{6,2},{7,3},{8,12},{9,13},{10,... | collective-permute-start | bytes 393224 | tf_op jit(solution)/shard_map/ppermute | solution.py:321
  67.0 10.1 %collective-permute-start.13 = (bf16[128,512]{1,0:T(8,128)(2,1)S(1)}, bf16[128,512]{1,0:T(8,128)(2,1)S(1)}, u32[]{:S(2)}, u32[]{:S(2)}) collective-permute-start(bf16[128,512]{1,0:T(8,128)(2,1)S(1)} %get-tuple-element.43), channel_id=1, source_target_pairs={{0,5},{1,4},{2,7},{3,6},{4,1},{5,0},{6,3},{7,2},{8,13},{9,12},{10,... | collective-permute-start | bytes 393224 | tf_op jit(solution)/shard_map/ppermute | solution.py:321
  67.6 11.9 %collective-permute-start.14 = (bf16[128,512]{1,0:T(8,128)(2,1)S(1)}, bf16[128,512]{1,0:T(8,128)(2,1)S(1)}, u32[]{:S(2)}, u32[]{:S(2)}) collective-permute-start(bf16[128,512]{1,0:T(8,128)(2,1)S(1)} %get-tuple-element.44), channel_id=1, source_target_pairs={{0,6},{1,7},{2,4},{3,5},{4,2},{5,3},{6,0},{7,1},{8,14},{9,15},{10,... | collective-permute-start | bytes 393224 | tf_op jit(solution)/shard_map/ppermute | solution.py:321
  70.1 12.3 %collective-permute-start.15 = (bf16[128,512]{1,0:T(8,128)(2,1)S(1)}, bf16[128,512]{1,0:T(8,128)(2,1)S(1)}, u32[]{:S(2)}, u32[]{:S(2)}) collective-permute-start(bf16[128,512]{1,0:T(8,128)(2,1)S(1)} %get-tuple-element.45), channel_id=1, source_target_pairs={{0,7},{1,6},{2,5},{3,4},{4,3},{5,2},{6,1},{7,0},{8,15},{9,14},{10,... | collective-permute-start | bytes 393224 | tf_op jit(solution)/shard_map/ppermute | solution.py:321

commit v4 on v3

--- a/solution.py
+++ b/solution.py
@@ -17,7 +17,8 @@
 SCALE = DH ** (-0.5) * 1.4426950408889634
 LATE = 2
 FIRST = 2
-SWAPS = [n for n in (6, 4, 7, 5, 3, 2) if n >= LATE]
+SWAPS = (4, 6, 3, 5, 7, 2)
+EARLY = (0, 3, 4, 6)
 
 
 NEAR, SIDE, HALF, FOURTH, THIRD = 1, 2, 3, 4, 5
@@ -115,24 +116,38 @@
     )(info, *held_in(pltpu.HBM, keys, values, queries))
 
 
-def attend(q, keys, vals, biases, causal=None, before=None):
-    scores = lax.dot_general(
+def scores_of(q, keys):
+    return lax.dot_general(
         jnp.concatenate(keys, 0), q, (((1,), (1,)), ((), ())), preferred_element_type=jnp.float32
     )
-    parts = [scores[n * BLOCK : (n + 1) * BLOCK, :] for n in range(len(keys))]
+
+
+def staggered(items, *stages):
+    items = list(items)
+    values = {}
+    for step in range(len(items) + len(stages) - 1):
+        for number, stage in enumerate(stages):
+            at = step - number
+            if 0 <= at < len(items):
+                values[at] = stage(items[at], *([values[at]] if number else []))
+
+
+def weighted(scores, count, biases, causal=None, before=None):
+    parts = [scores[n * BLOCK : (n + 1) * BLOCK, :] for n in range(count)]
     if causal is not None:
         parts[0] = jnp.where(causal, parts[0], NEG)
     tops = [part.max(0, keepdims=True) * SCALE + bias for part, bias in zip(parts, biases)]
-    top = functools.reduce(jnp.maximum, tops if before is None else [before[1]] + tops)
+    top = functools.reduce(jnp.maximum, tops if before is None else [before[0]] + tops)
     weights = [jnp.exp2(part * SCALE - (top - bias)) for part, bias in zip(parts, biases)]
-    total = functools.reduce(jnp.add, weights).sum(0, keepdims=True)
     weight = jnp.concatenate([w.astype(jnp.bfloat16) for w in weights], 0)
-    summed = jnp.dot(jnp.concatenate(vals, 1), weight, preferred_element_type=jnp.float32)
-    if before is not None:
-        factor = jnp.exp2(before[1] - top)
-        total = total + before[2] * factor
-        summed = summed + before[0] * factor
-    return summed, top, total
+    return weight, top, None if before is None else jnp.exp2(before[0] - top)
+
+
+def summed_of(vals, weight):
+    val = jnp.concatenate(vals, 1)
+    val = jnp.concatenate([val, jnp.ones((16, val.shape[1]), jnp.bfloat16)], 0)
+    summed = jnp.dot(val, weight, preferred_element_type=jnp.float32)
+    return summed[:DH], summed[DH : DH + 1]
 
 
 def bitmap_at(info_ref, h, j):
@@ -156,20 +171,28 @@
         causal = lax.broadcasted_iota(jnp.int32, shape, 0) <= (
             lax.broadcasted_iota(jnp.int32, shape, 1) & (BLOCK - 1)
         )
-        for i in range(count):
+        levels = range(BLOCKS.bit_length() - 1)
+
+        def blocks_of(i):
             n = first + i
-            j = rank ^ n
-            levels = range(BLOCKS.bit_length() - 1)
-            others = [n] + [n ^ 2**b for b in levels]
-            held = [kv_ref[m * BLOCK : (m + 1) * BLOCK, :] for m in others]
+            return [kv_ref[m * BLOCK : (m + 1) * BLOCK, :] for m in [n] + [n ^ 2**b for b in levels]]
+
+        def start(i):
+            return scores_of(q_ref[first + i], [kv[:, :DH] for kv in blocks_of(i)])
+
+        def weigh(i, scores):
+            j = rank ^ (first + i)
             bitmaps = [bitmap_at(info_ref, h, j) & j for h in range(HEADS)]
             biases = [0.0] + [bias_of(bitmaps, level) for level in levels]
-            summed, top, total = attend(
-                q_ref[n], [kv[:, :DH] for kv in held], [kv[:, DH:] for kv in held], biases, causal
-            )
-            part_ref[i] = summed
+            return weighted(scores, 1 + len(levels), biases, causal)
+
+        def finish(i, found):
+            weight, top, _ = found
+            part_ref[i], total = summed_of([kv[:, DH:] for kv in blocks_of(i)], weight)
             stat_ref[i, 0:1, :] = top
             stat_ref[i, 1:2, :] = total
+
+        staggered(range(count), start, weigh, finish)
 
     if turn is None:
         body()
@@ -201,22 +224,34 @@
     kv_refs, outs = refs[:arrays], refs[arrays:]
     levels = [slot_level(slot, info_ref[0, 1], BLOCKS.bit_length() - 1) for slot, _ in held]
     blocks = [n - first for n in final] if final else range(count)
-    for place, i in enumerate(blocks):
-        j = info_ref[0, 0] ^ (first + i)
-        keys, vals, rest = [], [], kv_refs
+
+    def tiles_of(i, part):
+        tiles, rest = [], kv_refs
         for _, number in held:
-            tiles = []
+            pieces = []
             for ref in rest[:number]:
                 at = (first + i if ref.shape[0] == BLOCKS * BLOCK else i) * BLOCK
-                tiles.append(ref[at : at + BLOCK, :])
+                pieces.append(ref[at : at + BLOCK, part])
             rest = rest[number:]
-            tile = functools.reduce(jnp.add, tiles)
-            keys.append(tile[:, :DH])
-            vals.append(tile[:, DH:])
+            tiles.append(functools.reduce(jnp.add, pieces))
+        return tiles
+
+    def start(item):
+        return scores_of(q_ref[first + item[1]], tiles_of(item[1], slice(0, DH)))
+
+    def weigh(item, scores):
+        _, i = item
+        j = info_ref[0, 0] ^ (first + i)
         bitmaps = [bitmap_at(info_ref, h, j) for h in range(HEADS)]
         biases = [bias_of(bitmaps, level) for level in levels]
-        before = (part_ref[i], stat_ref[i, 0:1, :], stat_ref[i, 1:2, :])
-        summed, top, total = attend(q_ref[first + i], keys, vals, biases, None, before)
+        return weighted(scores, len(levels), biases, None, (stat_ref[i, 0:1, :],))
+
+    def finish(item, found):
+        place, i = item
+        weight, top, factor = found
+        summed, total = summed_of(tiles_of(i, slice(DH, 2 * DH)), weight)
+        summed = summed + part_ref[i] * factor
+        total = total + stat_ref[i, 1:2, :] * factor
         if final:
             result = summed * (1.0 / total)
             for h in range(HEADS):
@@ -226,6 +261,8 @@
             outs[0][i] = summed
             outs[1][i, 0:1, :] = top
             outs[1][i, 1:2, :] = total
+
+    staggered(enumerate(blocks), start, weigh, finish)
 
 
 def far_part(info, queries, state, fetched, held, first, final=()):
@@ -259,52 +296,97 @@
     return list(outs)
 
 
-def norm_kernel(info_ref, *refs):
-    parts = refs[:BLOCKS]
-    res_ref, gain_ref, stream_hbm, normed_hbm, whole, stream_ref, normed_ref, sems = refs[BLOCKS:]
-    width = parts[0].shape[1]
+def added(info_ref, n, part_ref, res_ref, stream_ref, stream_hbm, sem):
+    width = part_ref.shape[1]
+    cols = pl.ds(pl.multiple_of((info_ref[0, 0] ^ n) * width, width), width)
+    summed = res_ref[:, cols].astype(jnp.float32) + part_ref[...].astype(jnp.float32)
+    stream_ref[...] = summed.astype(jnp.bfloat16)
+    copy = pltpu.make_async_copy(stream_ref, stream_hbm.at[:, cols], sem)
+    copy.start()
+    square = jnp.zeros((BLOCK, DH), jnp.float32)
+    for c in range(0, width, DH):
+        piece = summed[:, c : c + DH]
+        square = square + piece * piece
+    return summed, square, copy
+
+
+def sums_kernel(groups, info_ref, *refs):
+    parts = refs[: len(groups)]
+    res_ref, stream_hbm, whole_ref, square_ref, stream_ref, sems = refs[len(groups) :]
     square = jnp.zeros((BLOCK, DH), jnp.float32)
     copies = []
-    for n in range(BLOCKS):
-        source = info_ref[0, 0] ^ n
-        cols = pl.ds(pl.multiple_of(source * width, width), width)
-        summed = res_ref[:, cols].astype(jnp.float32) + parts[n][...].astype(jnp.float32)
-        stream_ref[n] = summed.astype(jnp.bfloat16)
-        copies.append(pltpu.make_async_copy(stream_ref.at[n], stream_hbm.at[:, cols], sems.at[0, n]))
-        copies[-1].start()
-        whole[n] = summed
-        for c in range(0, width, DH):
-            piece = summed[:, c : c + DH]
-            square = square + piece * piece
+    for i, n in enumerate(groups):
+        summed, more, copy = added(info_ref, n, parts[i], res_ref, stream_ref.at[i], stream_hbm, sems.at[i])
+        whole_ref[i] = summed
+        square = square + more
+        copies.append(copy)
+    square_ref[...] = square
+    for copy in copies:
+        copy.wait()
+
+
+def sums_part(info, groups, parts, residual):
+    count, width = len(groups), parts[0].shape[1]
+    return pl.pallas_call(
+        functools.partial(sums_kernel, groups),
+        in_specs=[pl.BlockSpec(memory_space=pltpu.SMEM)] + [in_vmem()] * (count + 1),
+        out_specs=[pl.BlockSpec(memory_space=pl.ANY), in_vmem(), in_vmem()],
+        out_shape=[
+            jax.ShapeDtypeStruct(residual.shape, jnp.bfloat16),
+            jax.ShapeDtypeStruct((count, BLOCK, width), jnp.float32),
+            jax.ShapeDtypeStruct((BLOCK, DH), jnp.float32),
+        ],
+        scratch_shapes=[pltpu.VMEM((count, BLOCK, width), jnp.bfloat16), pltpu.SemaphoreType.DMA((count,))],
+        cost_estimate=pl.CostEstimate(flops=2_000_000, bytes_accessed=2_000_000, transcendentals=0),
+        compiler_params=params(),
+        name="sums",
+    )(info, *held_in(pltpu.VMEM, *parts), residual)
+
+
+def norm_kernel(groups, before, info_ref, *refs):
+    parts = refs[: len(groups)]
+    res_ref, gain_ref, _, held_ref, square_ref, stream_hbm, normed_hbm = refs[len(groups) : len(groups) + 7]
+    whole, stream_ref, normed_ref, sems = refs[len(groups) + 7 :]
+    width = parts[0].shape[1]
+    square = square_ref[...]
+    copies = []
+    for i, n in enumerate(groups):
+        summed, more, copy = added(info_ref, n, parts[i], res_ref, stream_ref.at[i], stream_hbm, sems.at[0, n])
+        whole[i] = summed
+        square = square + more
+        copies.append(copy)
     mean = square.sum(-1, keepdims=True) / (BLOCKS * width)
     factor = lax.rsqrt(mean + EPSILON)
     for n in range(BLOCKS):
-        source = info_ref[0, 0] ^ n
-        cols = pl.ds(pl.multiple_of(source * width, width), width)
-        normed_ref[n] = (whole[n] * factor * gain_ref[:, cols].astype(jnp.float32)).astype(jnp.bfloat16)
+        cols = pl.ds(pl.multiple_of((info_ref[0, 0] ^ n) * width, width), width)
+        summed = held_ref[before.index(n)] if n in before else whole[groups.index(n)]
+        normed_ref[n] = (summed * factor * gain_ref[:, cols].astype(jnp.float32)).astype(jnp.bfloat16)
         copies.append(pltpu.make_async_copy(normed_ref.at[n], normed_hbm.at[:, cols], sems.at[1, n]))
         copies[-1].start()
     for copy in copies:
         copy.wait()
 
 
-def norm_part(info, parts, residual, gain):
-    width = parts[0].shape[1]
+def norm_part(info, groups, parts, before, held, residual, gain):
+    count, width = len(groups), parts[0].shape[1]
+    stream, whole, square = held
+    hbm = pl.BlockSpec(memory_space=pl.ANY)
     return pl.pallas_call(
-        norm_kernel,
-        in_specs=[pl.BlockSpec(memory_space=pltpu.SMEM)] + [in_vmem()] * (len(parts) + 2),
-        out_specs=[pl.BlockSpec(memory_space=pl.ANY)] * 2,
+        functools.partial(norm_kernel, groups, before),
+        in_specs=[pl.BlockSpec(memory_space=pltpu.SMEM)] + [in_vmem()] * (count + 2) + [hbm] + [in_vmem()] * 2,
+        out_specs=[hbm] * 2,
         out_shape=[jax.ShapeDtypeStruct(residual.shape, jnp.bfloat16)] * 2,
         scratch_shapes=[
-            pltpu.VMEM((BLOCKS, BLOCK, width), jnp.float32),
-            pltpu.VMEM((BLOCKS, BLOCK, width), jnp.bfloat16),
+            pltpu.VMEM((count, BLOCK, width), jnp.float32),
+            pltpu.VMEM((count, BLOCK, width), jnp.bfloat16),
             pltpu.VMEM((BLOCKS, BLOCK, width), jnp.bfloat16),
             pltpu.SemaphoreType.DMA((2, BLOCKS)),
         ],
+        input_output_aliases={3 + count: 0},
         cost_estimate=pl.CostEstimate(flops=4_000_000, bytes_accessed=4_000_000, transcendentals=128),
         compiler_params=params(),
         name="norm",
-    )(info, *held_in(pltpu.VMEM, *parts), residual, gain)
+    )(info, *held_in(pltpu.VMEM, *parts), residual, gain, stream, *held_in(pltpu.VMEM, whole, square))
 
 
 def shards(queries, keys, values, block_masks, residual, norm_gain):
@@ -333,15 +415,19 @@
     state = local_part(info, queries, kv, LATE, far_blocks, 0)
     state = local_part(info, queries, kv, LATE, far_blocks, 1, state)
     late_state = local_part(info, queries, kv, 0, LATE)
-    state = far_part(info, queries, state, rest, (NEAR, HALF_STRAIGHT, FOURTH, THIRD), LATE)
+    state = far_part(info, queries, state, rest, (NEAR, FOURTH, THIRD), LATE)
     sent = {}
-    for some in (SWAPS[:2], SWAPS[2:]):
-        sent |= zip(some, far_part(info, queries, state, rest, (SIDE_ONWARD,), LATE, some))
+    for some in (SWAPS[:4], SWAPS[4:]):
+        sent |= zip(some, far_part(info, queries, state, rest, (SIDE_ONWARD, HALF_STRAIGHT), LATE, some))
     late_state = far_part(info, queries, late_state, late, (FOURTH, THIRD), 0)
     parts = far_part(info, queries, late_state, late, (NEAR, SIDE, HALF), 0, range(LATE))
     parts += [sent[n] for n in range(LATE, BLOCKS)]
     parts = parts[:1] + [swapped(parts[n], n) for n in range(1, BLOCKS)]
-    return norm_part(info, parts, residual, norm_gain.reshape(1, -1))
+    soon = [n for n in range(BLOCKS) if n in EARLY]
+    last = [n for n in range(BLOCKS) if n not in EARLY]
+    held = sums_part(info, soon, [parts[n] for n in soon], residual)
+    gain = norm_gain.reshape(1, -1)
+    return norm_part(info, last, [parts[n] for n in last], soon, held, residual, gain)
 
 
 def solution(mesh):

time: 85.2 us -> 73.8 us (0.87)
  the two profiles are of different devices: /device:TPU:193 before, /device:TPU:33 now
where the time goes in v4:
time: 73.8 us; the launch traced here: 73.5 us
  starting transfers between devices  46.8 us (63%)
  Pallas kernels  18.5 us (25%)
  waiting for transfers between devices  6.53 us (9%)
  between operations  0.93 us (1%)
    ppermute x7, starting transfers between devices, fetched(): return lax.ppermute(array, 'ctx', routes[slot])  25.1 us
    ppermute x7, starting transfers between devices, swapped(): return lax.ppermute(array, 'head', [(i, i ^ n) for i in range(groups)])  14.9 us
    pallas_call x5, Pallas kernels, far_part(): pl.pallas_call(functools.partial(far_kernel, numbers, first, count, final...  8.06 us
    ppermute x7, waiting for transfers between devices, swapped(): return lax.ppermute(array, 'head', [(i, i ^ n) for i in range(groups)])  6.51 us
    ppermute x1, starting transfers between devices, shards(): rest[HALF_STRAIGHT] = lax.ppermute(kv_rest, 'ctx', straight)  6.14 us
    pallas_call x3, Pallas kernels, local_part(): pl.pallas_call(functools.partial(local_kernel, first, count, turn), in_sp...  4.78 us
    pallas_call x1, Pallas kernels, ordered(): pl.pallas_call(order_kernel, in_specs=[pl.BlockSpec(memory_space=pltpu.SM...  2.19 us
    pallas_call x1, Pallas kernels, norm_part(): pl.pallas_call(functools.partial(norm_kernel, groups, before), in_specs=[...  2.06 us
  transfers between devices with their start and end apart: 16, of which 2 were waited for; matrix products, arithmetic and copies ran while one was open for 0% of the time, Pallas kernels for 19%

profile of v4, /device:TPU:33, one launch (start us, length us, event | category | flops | bytes accessed | tf_op | source)
XLA Modules:
  0.0 73.5 jit_solution(4269134205518298883)
XLA Ops:
  0.6 0.7 pad_add_fusion.info_ref
  1.3 2.2 %order.1 = (bf16[1024,256]{1,0:T(8,128)(2,1)S(1)}, bf16[256,256]{1,0:T(8,128)(2,1)S(1)}, bf16[768,256]{1,0:T(8,128)(2,1)S(1)}, bf16[8,512,128]{2,1,0:T(8,128)(2,1)S(1)}) custom-call(s32[5,8]{1,0:T(8,128)S(1)} %pad_add_fusion.info_ref, bf16[1024,128]{1,0:T(8,128)(2,1)} %k_hbm.1, bf16[1024,128]{1,0:T(8,128)(2,1)} %v_hbm.1, bf16[1024,512]{1,0:T(8,128)(2,1)} %q_hbm.1), custom_call_target="tpu_custom_call" | custom-call | tf_op jit(solution)/shard_map/order/pallas_call | solution.py:104
  3.5 0.7 collective-permute-start.6
  4.2 4.9 %collective-permute-start = (bf16[1024,256]{1,0:T(8,128)(2,1)S(1)}, bf16[1024,256]{1,0:T(8,128)(2,1)S(1)}, u32[]{:S(2)}, u32[]{:S(2)}) collective-permute-start(bf16[1024,256]{1,0:T(8,128)(2,1)S(1)} %get-tuple-element.28.kv_ref), channel_id=1, source_target_pairs={{0,128},{8,136},{16,144},{24,152},{32,160},{40,168},{48,176},{56,1... | collective-permute-start | bytes 1572872 | tf_op jit(solution)/shard_map/ppermute | solution.py:400
  9.1 2.3 %collective-permute-start.1 = (bf16[1024,256]{1,0:T(8,128)(2,1)S(1)}, bf16[1024,256]{1,0:T(8,128)(2,1)S(1)}, u32[]{:S(2)}, u32[]{:S(2)}) collective-permute-start(bf16[1024,256]{1,0:T(8,128)(2,1)S(1)} %get-tuple-element.28.kv_ref), channel_id=1, source_target_pairs={{0,64},{8,72},{16,80},{24,88},{32,96},{40,104},{48,112},{56,120},{... | collective-permute-start | bytes 1572872 | tf_op jit(solution)/shard_map/ppermute | solution.py:400
  11.4 5.5 %collective-permute-start.7 = (bf16[768,256]{1,0:T(8,128)(2,1)S(1)}, bf16[768,256]{1,0:T(8,128)(2,1)S(1)}, u32[]{:S(2)}, u32[]{:S(2)}) collective-permute-start(bf16[768,256]{1,0:T(8,128)(2,1)S(1)} %get-tuple-element.39), channel_id=1, source_target_pairs={{0,8},{8,24},{32,40},{40,56},{64,72},{72,88},{96,104},{104,120},{1... | collective-permute-start | bytes 1179656 | tf_op jit(solution)/shard_map/ppermute | solution.py:400
  16.9 6.1 %collective-permute-start.9 = (bf16[768,256]{1,0:T(8,128)(2,1)S(1)}, bf16[768,256]{1,0:T(8,128)(2,1)S(1)}, u32[]{:S(2)}, u32[]{:S(2)}) collective-permute-start(bf16[768,256]{1,0:T(8,128)(2,1)S(1)} %get-tuple-element.39), channel_id=1, source_target_pairs={{0,32},{8,40},{24,56},{64,96},{72,104},{88,120},{128,160},{136,168... | collective-permute-start | bytes 1179656 | tf_op jit(solution)/shard_map/ppermute | solution.py:411
  23.1 0.7 collective-permute-start.8
  23.8 2.6 %local.4 = (f32[6,128,512]{2,1,0:T(8,128)S(1)}, f32[6,8,512]{2,1,0:T(8,128)S(1)}) custom-call(s32[5,8]{1,0:T(8,128)S(1)} %pad_add_fusion.info_ref, bf16[8,512,128]{2,1,0:T(8,128)(2,1)S(1)} %get-tuple-element.27.q_ref, bf16[1024,256]{1,0:T(8,128)(2,1)S(1)} %get-tuple-element.28.kv_ref), custom_call_target="tpu_custom_call" | custom-call | flops 805306368 | bytes 4000000 | tf_op jit(solution)/shard_map/local/pallas_call | solution.py:205
  27.8 3.7 %collective-permute-start.3 = (bf16[256,256]{1,0:T(8,128)(2,1)S(1)}, bf16[256,256]{1,0:T(8,128)(2,1)S(1)}, u32[]{:S(2)}, u32[]{:S(2)}) collective-permute-start(bf16[256,256]{1,0:T(8,128)(2,1)S(1)} %get-tuple-element.33), channel_id=1, source_target_pairs={{0,8},{8,24},{32,40},{40,56},{64,72},{72,88},{96,104},{104,120},{1... | collective-permute-start | bytes 393224 | tf_op jit(solution)/shard_map/ppermute | solution.py:400
  31.5 7.3 %collective-permute-start.4 = (bf16[256,256]{1,0:T(8,128)(2,1)S(1)}, bf16[256,256]{1,0:T(8,128)(2,1)S(1)}, u32[]{:S(2)}, u32[]{:S(2)}) collective-permute-start(bf16[256,256]{1,0:T(8,128)(2,1)S(1)} %get-tuple-element.33), channel_id=1, source_target_pairs={{0,32},{8,40},{16,48},{24,56},{64,96},{72,104},{80,112},{88,120},{... | collective-permute-start | bytes 393224 | tf_op jit(solution)/shard_map/ppermute | solution.py:400
  38.8 2.3 %far.7 = (f32[6,128,512]{2,1,0:T(8,128)S(1)}, f32[6,8,512]{2,1,0:T(8,128)S(1)}) custom-call(s32[5,8]{1,0:T(8,128)S(1)} %pad_add_fusion.info_ref, bf16[8,512,128]{2,1,0:T(8,128)(2,1)S(1)} %get-tuple-element.27.q_ref, f32[6,128,512]{2,1,0:T(8,128)S(1)} %get-tuple-element.37.part_ref, f32[6,8,512]{2,1,0:T(8,128)S(1)} %get-tuple-element.38.stat_ref, ...), custom_call_target="tpu_custom_call" | custom-call | flops 603979776 | bytes 4000000 | tf_op jit(solution)/shard_map/far/pallas_call | solution.py:283
  41.1 1.7 %far.9 = (bf16[128,512]{1,0:T(8,128)(2,1)S(1)}, bf16[128,512]{1,0:T(8,128)(2,1)S(1)}, bf16[128,512]{1,0:T(8,128)(2,1)S(1)}, bf16[128,512]{1,0:T(8,128)(2,1)S(1)}) custom-call(s32[5,8]{1,0:T(8,128)S(1)} %pad_add_fusion.info_ref, bf16[8,512,128]{2,1,0:T(8,128)(2,1)S(1)} %get-tuple-element.27.q_ref, f32[6,128,512]{2,1,0:T(8,128)S(1)} %get-tuple-element.40.part_ref, ...), custom_call_target="tpu_custom_call" | custom-call | flops 603979776 | bytes 4000000 | tf_op jit(solution)/shard_map/far/pallas_call | solution.py:283
  42.8 7.5 %collective-permute-start.13 = (bf16[128,512]{1,0:T(8,128)(2,1)S(1)}, bf16[128,512]{1,0:T(8,128)(2,1)S(1)}, u32[]{:S(2)}, u32[]{:S(2)}) collective-permute-start(bf16[128,512]{1,0:T(8,128)(2,1)S(1)} %get-tuple-element.46), channel_id=1, source_target_pairs={{0,3},{1,2},{2,1},{3,0},{4,7},{5,6},{6,5},{7,4},{8,11},{9,10},{10,... | collective-permute-start | bytes 393224 | tf_op jit(solution)/shard_map/ppermute | solution.py:403
  50.3 2.4 %collective-permute-start.14 = (bf16[128,512]{1,0:T(8,128)(2,1)S(1)}, bf16[128,512]{1,0:T(8,128)(2,1)S(1)}, u32[]{:S(2)}, u32[]{:S(2)}) collective-permute-start(bf16[128,512]{1,0:T(8,128)(2,1)S(1)} %get-tuple-element.47), channel_id=1, source_target_pairs={{0,4},{1,5},{2,6},{3,7},{4,0},{5,1},{6,2},{7,3},{8,12},{9,13},{10,... | collective-permute-start | bytes 393224 | tf_op jit(solution)/shard_map/ppermute | solution.py:403
  52.8 1.5 %local.3 = (f32[2,128,512]{2,1,0:T(8,128)S(1)}, f32[2,8,512]{2,1,0:T(8,128)S(1)}) custom-call(s32[5,8]{1,0:T(8,128)S(1)} %pad_add_fusion.info_ref, bf16[8,512,128]{2,1,0:T(8,128)(2,1)S(1)} %get-tuple-element.27.q_ref, bf16[1024,256]{1,0:T(8,128)(2,1)S(1)} %get-tuple-element.28.kv_ref), custom_call_target="tpu_custom_call" | custom-call | flops 268435456 | bytes 4000000 | tf_op jit(solution)/shard_map/local/pallas_call | solution.py:205
  54.3 1.2 %far.5 = (f32[2,128,512]{2,1,0:T(8,128)S(1)}, f32[2,8,512]{2,1,0:T(8,128)S(1)}) custom-call(s32[5,8]{1,0:T(8,128)S(1)} %pad_add_fusion.info_ref, bf16[8,512,128]{2,1,0:T(8,128)(2,1)S(1)} %get-tuple-element.27.q_ref, f32[2,128,512]{2,1,0:T(8,128)S(1)} %get-tuple-element.29.part_ref, f32[2,8,512]{2,1,0:T(8,128)S(1)} %get-tuple-element.30.stat_ref, ...), custom_call_target="tpu_custom_call" | custom-call | flops 134217728 | bytes 4000000 | tf_op jit(solution)/shard_map/far/pallas_call | solution.py:283
  55.6 1.5 %far.6 = (bf16[128,512]{1,0:T(8,128)(2,1)S(1)}, bf16[128,512]{1,0:T(8,128)(2,1)S(1)}) custom-call(s32[5,8]{1,0:T(8,128)S(1)} %pad_add_fusion.info_ref, bf16[8,512,128]{2,1,0:T(8,128)(2,1)S(1)} %get-tuple-element.27.q_ref, f32[2,128,512]{2,1,0:T(8,128)S(1)} %get-tuple-element.31.part_ref, f32[2,8,512]{2,1,0:T(8,128)S(1)} %get-tuple-element.32.stat_ref, ...), custom_call_target="tpu_custom_call" | custom-call | flops 201326592 | bytes 4000000 | tf_op jit(solution)/shard_map/far/pallas_call | solution.py:283
  57.6 1.3 %far.8 = (bf16[128,512]{1,0:T(8,128)(2,1)S(1)}, bf16[128,512]{1,0:T(8,128)(2,1)S(1)}) custom-call(s32[5,8]{1,0:T(8,128)S(1)} %pad_add_fusion.info_ref, bf16[8,512,128]{2,1,0:T(8,128)(2,1)S(1)} %get-tuple-element.27.q_ref, f32[6,128,512]{2,1,0:T(8,128)S(1)} %get-tuple-element.40.part_ref, f32[6,8,512]{2,1,0:T(8,128)S(1)} %get-tuple-element.41.stat_ref, ...), custom_call_target="tpu_custom_call" | custom-call | flops 603979776 | bytes 4000000 | tf_op jit(solution)/shard_map/far/pallas_call | solution.py:283
  59.0 4.4 %collective-permute-start.11 = (bf16[128,512]{1,0:T(8,128)(2,1)S(1)}, bf16[128,512]{1,0:T(8,128)(2,1)S(1)}, u32[]{:S(2)}, u32[]{:S(2)}) collective-permute-start(bf16[128,512]{1,0:T(8,128)(2,1)S(1)} %get-tuple-element.43), channel_id=1, source_target_pairs={{0,5},{1,4},{2,7},{3,6},{4,1},{5,0},{6,3},{7,2},{8,13},{9,12},{10,... | collective-permute-start | bytes 393224 | tf_op jit(solution)/shard_map/ppermute | solution.py:403
  63.5 1.5 %sums.1 = (bf16[128,4096]{1,0:T(8,128)(2,1)}, f32[4,128,512]{2,1,0:T(8,128)S(1)}, f32[128,128]{1,0:T(8,128)S(1)}) custom-call(s32[5,8]{1,0:T(8,128)S(1)} %pad_add_fusion.info_ref, bf16[128,512]{1,0:T(8,128)(2,1)S(1)} %get-tuple-element.45.refs_0_, bf16[128,512]{1,0:T(8,128)(2,1)S(1)} %collective-permute-done.13.refs_1_, ...), custom_call_target="tpu_custom_call" | custom-call | flops 2000000 | bytes 2000000 | tf_op jit(solution)/shard_map/sums/pallas_call | solution.py:330
  65.0 4.3 %collective-permute-done.11.refs_2_ = bf16[128,512]{1,0:T(8,128)(2,1)S(1)} collective-permute-done((bf16[128,512]{1,0:T(8,128)(2,1)S(1)}, bf16[128,512]{1,0:T(8,128)(2,1)S(1)}, u32[]{:S(2)}, u32[]{:S(2)}) %collective-permute-start.11) | collective-permute-done | bytes 131104 | tf_op jit(solution)/shard_map/ppermute | solution.py:403
  69.2 2.2 %collective-permute-done.12.refs_3_ = bf16[128,512]{1,0:T(8,128)(2,1)S(1)} collective-permute-done((bf16[128,512]{1,0:T(8,128)(2,1)S(1)}, bf16[128,512]{1,0:T(8,128)(2,1)S(1)}, u32[]{:S(2)}, u32[]{:S(2)}) %collective-permute-start.12) | collective-permute-done | bytes 131104 | tf_op jit(solution)/shard_map/ppermute | solution.py:403
  71.4 2.1 %norm.1 = (bf16[128,4096]{1,0:T(8,128)(2,1)}, bf16[128,4096]{1,0:T(8,128)(2,1)}) custom-call(s32[5,8]{1,0:T(8,128)S(1)} %pad_add_fusion.info_ref, bf16[128,512]{1,0:T(8,128)(2,1)S(1)} %collective-permute-done.5.refs_0_, bf16[128,512]{1,0:T(8,128)(2,1)S(1)} %collective-permute-done.10.refs_1_, ...), custom_call_target="tpu_custom_call", output_to_operand_aliasing={{0}: (7, {})} | custom-call | flops 4000000 | bytes 4000000 | tf_op jit(solution)/shard_map/norm/pallas_call | solution.py:374
  (26 shorter events, 1.9 us)
Async XLA Ops:
  3.5 19.6 %collective-permute-start.6 = (bf16[768,256]{1,0:T(8,128)(2,1)S(1)}, bf16[768,256]{1,0:T(8,128)(2,1)S(1)}, u32[]{:S(2)}, u32[]{:S(2)}) collective-permute-start(bf16[768,256]{1,0:T(8,128)(2,1)S(1)} %get-tuple-element.39), channel_id=1, source_target_pairs={{0,16},{16,24},{32,48},{48,56},{64,80},{80,88},{96,112},{112,120},... | collective-permute-start | bytes 1179656 | tf_op jit(solution)/shard_map/ppermute | solution.py:400
  4.2 23.5 %collective-permute-start = (bf16[1024,256]{1,0:T(8,128)(2,1)S(1)}, bf16[1024,256]{1,0:T(8,128)(2,1)S(1)}, u32[]{:S(2)}, u32[]{:S(2)}) collective-permute-start(bf16[1024,256]{1,0:T(8,128)(2,1)S(1)} %get-tuple-element.28.kv_ref), channel_id=1, source_target_pairs={{0,128},{8,136},{16,144},{24,152},{32,160},{40,168},{48,176},{56,1... | collective-permute-start | bytes 1572872 | tf_op jit(solution)/shard_map/ppermute | solution.py:400
  9.1 22.4 %collective-permute-start.1 = (bf16[1024,256]{1,0:T(8,128)(2,1)S(1)}, bf16[1024,256]{1,0:T(8,128)(2,1)S(1)}, u32[]{:S(2)}, u32[]{:S(2)}) collective-permute-start(bf16[1024,256]{1,0:T(8,128)(2,1)S(1)} %get-tuple-element.28.kv_ref), channel_id=1, source_target_pairs={{0,64},{8,72},{16,80},{24,88},{32,96},{40,104},{48,112},{56,120},{... | collective-permute-start | bytes 1572872 | tf_op jit(solution)/shard_map/ppermute | solution.py:400
  11.4 15.6 %collective-permute-start.7 = (bf16[768,256]{1,0:T(8,128)(2,1)S(1)}, bf16[768,256]{1,0:T(8,128)(2,1)S(1)}, u32[]{:S(2)}, u32[]{:S(2)}) collective-permute-start(bf16[768,256]{1,0:T(8,128)(2,1)S(1)} %get-tuple-element.39), channel_id=1, source_target_pairs={{0,8},{8,24},{32,40},{40,56},{64,72},{72,88},{96,104},{104,120},{1... | collective-permute-start | bytes 1179656 | tf_op jit(solution)/shard_map/ppermute | solution.py:400
  16.9 24.1 %collective-permute-start.9 = (bf16[768,256]{1,0:T(8,128)(2,1)S(1)}, bf16[768,256]{1,0:T(8,128)(2,1)S(1)}, u32[]{:S(2)}, u32[]{:S(2)}) collective-permute-start(bf16[768,256]{1,0:T(8,128)(2,1)S(1)} %get-tuple-element.39), channel_id=1, source_target_pairs={{0,32},{8,40},{24,56},{64,96},{72,104},{88,120},{128,160},{136,168... | collective-permute-start | bytes 1179656 | tf_op jit(solution)/shard_map/ppermute | solution.py:411
  23.1 18.0 %collective-permute-start.8 = (bf16[768,256]{1,0:T(8,128)(2,1)S(1)}, bf16[768,256]{1,0:T(8,128)(2,1)S(1)}, u32[]{:S(2)}, u32[]{:S(2)}) collective-permute-start(bf16[768,256]{1,0:T(8,128)(2,1)S(1)} %collective-permute-done.6.refs_0_), channel_id=1, source_target_pairs={{24,48},{88,112},{152,176},{216,240},{25,49},{89,113},{153,177},{2... | collective-permute-start | bytes 1179656 | tf_op jit(solution)/shard_map/ppermute | solution.py:412
  27.1 28.5 %collective-permute-start.2 = (bf16[256,256]{1,0:T(8,128)(2,1)S(1)}, bf16[256,256]{1,0:T(8,128)(2,1)S(1)}, u32[]{:S(2)}, u32[]{:S(2)}) collective-permute-start(bf16[256,256]{1,0:T(8,128)(2,1)S(1)} %get-tuple-element.33), channel_id=1, source_target_pairs={{0,16},{16,24},{32,48},{48,56},{64,80},{80,88},{96,112},{112,120},... | collective-permute-start | bytes 393224 | tf_op jit(solution)/shard_map/ppermute | solution.py:400
  27.8 27.8 %collective-permute-start.3 = (bf16[256,256]{1,0:T(8,128)(2,1)S(1)}, bf16[256,256]{1,0:T(8,128)(2,1)S(1)}, u32[]{:S(2)}, u32[]{:S(2)}) collective-permute-start(bf16[256,256]{1,0:T(8,128)(2,1)S(1)} %get-tuple-element.33), channel_id=1, source_target_pairs={{0,8},{8,24},{32,40},{40,56},{64,72},{72,88},{96,104},{104,120},{1... | collective-permute-start | bytes 393224 | tf_op jit(solution)/shard_map/ppermute | solution.py:400
  31.5 24.0 %collective-permute-start.4 = (bf16[256,256]{1,0:T(8,128)(2,1)S(1)}, bf16[256,256]{1,0:T(8,128)(2,1)S(1)}, u32[]{:S(2)}, u32[]{:S(2)}) collective-permute-start(bf16[256,256]{1,0:T(8,128)(2,1)S(1)} %get-tuple-element.33), channel_id=1, source_target_pairs={{0,32},{8,40},{16,48},{24,56},{64,96},{72,104},{80,112},{88,120},{... | collective-permute-start | bytes 393224 | tf_op jit(solution)/shard_map/ppermute | solution.py:400
  42.8 16.2 %collective-permute-start.13 = (bf16[128,512]{1,0:T(8,128)(2,1)S(1)}, bf16[128,512]{1,0:T(8,128)(2,1)S(1)}, u32[]{:S(2)}, u32[]{:S(2)}) collective-permute-start(bf16[128,512]{1,0:T(8,128)(2,1)S(1)} %get-tuple-element.46), channel_id=1, source_target_pairs={{0,3},{1,2},{2,1},{3,0},{4,7},{5,6},{6,5},{7,4},{8,11},{9,10},{10,... | collective-permute-start | bytes 393224 | tf_op jit(solution)/shard_map/ppermute | solution.py:403
  50.3 13.1 %collective-permute-start.14 = (bf16[128,512]{1,0:T(8,128)(2,1)S(1)}, bf16[128,512]{1,0:T(8,128)(2,1)S(1)}, u32[]{:S(2)}, u32[]{:S(2)}) collective-permute-start(bf16[128,512]{1,0:T(8,128)(2,1)S(1)} %get-tuple-element.47), channel_id=1, source_target_pairs={{0,4},{1,5},{2,6},{3,7},{4,0},{5,1},{6,2},{7,3},{8,12},{9,13},{10,... | collective-permute-start | bytes 393224 | tf_op jit(solution)/shard_map/ppermute | solution.py:403
  57.1 7.9 %collective-permute-start.5 = (bf16[128,512]{1,0:T(8,128)(2,1)S(1)}, bf16[128,512]{1,0:T(8,128)(2,1)S(1)}, u32[]{:S(2)}, u32[]{:S(2)}) collective-permute-start(bf16[128,512]{1,0:T(8,128)(2,1)S(1)} %get-tuple-element.34), channel_id=1, source_target_pairs={{0,1},{1,0},{2,3},{3,2},{4,5},{5,4},{6,7},{7,6},{8,9},{9,8},{10,11... | collective-permute-start | bytes 393224 | tf_op jit(solution)/shard_map/ppermute | solution.py:403
  57.2 6.3 %copy-start.1 = (bf16[4096]{0:T(1024)(128)(2,1)S(1)}, bf16[4096]{0:T(1024)(128)(2,1)}, u32[]{:S(2)}) copy-start(bf16[4096]{0:T(1024)(128)(2,1)} %param.11) | copy-start | bytes 24580
  57.2 6.3 %copy-start = (bf16[128,4096]{1,0:T(8,128)(2,1)S(1)}, bf16[128,4096]{1,0:T(8,128)(2,1)}, u32[]{:S(2)}) copy-start(bf16[128,4096]{1,0:T(8,128)(2,1)} %refs_4_.3) | copy-start | bytes 3145732
  57.2 6.3 %collective-permute-start.15 = (bf16[128,512]{1,0:T(8,128)(2,1)S(1)}, bf16[128,512]{1,0:T(8,128)(2,1)S(1)}, u32[]{:S(2)}, u32[]{:S(2)}) collective-permute-start(bf16[128,512]{1,0:T(8,128)(2,1)S(1)} %get-tuple-element.48), channel_id=1, source_target_pairs={{0,6},{1,7},{2,4},{3,5},{4,2},{5,3},{6,0},{7,1},{8,14},{9,15},{10,... | collective-permute-start | bytes 393224 | tf_op jit(solution)/shard_map/ppermute | solution.py:403
  58.9 6.0 %collective-permute-start.10 = (bf16[128,512]{1,0:T(8,128)(2,1)S(1)}, bf16[128,512]{1,0:T(8,128)(2,1)S(1)}, u32[]{:S(2)}, u32[]{:S(2)}) collective-permute-start(bf16[128,512]{1,0:T(8,128)(2,1)S(1)} %get-tuple-element.42), channel_id=1, source_target_pairs={{0,2},{1,3},{2,0},{3,1},{4,6},{5,7},{6,4},{7,5},{8,10},{9,11},{10,... | collective-permute-start | bytes 393224 | tf_op jit(solution)/shard_map/ppermute | solution.py:403
  59.0 10.2 %collective-permute-start.11 = (bf16[128,512]{1,0:T(8,128)(2,1)S(1)}, bf16[128,512]{1,0:T(8,128)(2,1)S(1)}, u32[]{:S(2)}, u32[]{:S(2)}) collective-permute-start(bf16[128,512]{1,0:T(8,128)(2,1)S(1)} %get-tuple-element.43), channel_id=1, source_target_pairs={{0,5},{1,4},{2,7},{3,6},{4,1},{5,0},{6,3},{7,2},{8,13},{9,12},{10,... | collective-permute-start | bytes 393224 | tf_op jit(solution)/shard_map/ppermute | solution.py:403
  63.4 8.0 %collective-permute-start.12 = (bf16[128,512]{1,0:T(8,128)(2,1)S(1)}, bf16[128,512]{1,0:T(8,128)(2,1)S(1)}, u32[]{:S(2)}, u32[]{:S(2)}) collective-permute-start(bf16[128,512]{1,0:T(8,128)(2,1)S(1)} %get-tuple-element.44), channel_id=1, source_target_pairs={{0,7},{1,6},{2,5},{3,4},{4,3},{5,2},{6,1},{7,0},{8,15},{9,14},{10,... | collective-permute-start | bytes 393224 | tf_op jit(solution)/shard_map/ppermute | solution.py:403

commit v5 on v4

--- a/solution.py
+++ b/solution.py
@@ -18,7 +18,7 @@
 LATE = 2
 FIRST = 2
 SWAPS = (4, 6, 3, 5, 7, 2)
-EARLY = (0, 3, 4, 6)
+EARLY = (0, 1, 3, 4, 6)
 
 
 NEAR, SIDE, HALF, FOURTH, THIRD = 1, 2, 3, 4, 5
@@ -76,13 +76,9 @@
 
 def order_kernel(info_ref, k_hbm, v_hbm, q_hbm, all_ref, late_ref, rest_ref, q_ref, k_ref, v_ref, sems):
     rank = info_ref[0, 0]
-    copies = [pltpu.make_async_copy(k_hbm, k_ref, sems.at[0, 0]), pltpu.make_async_copy(v_hbm, v_ref, sems.at[0, 1])]
+    copies = [pltpu.make_async_copy(k_hbm, k_ref, sems.at[0]), pltpu.make_async_copy(v_hbm, v_ref, sems.at[1])]
     for n in range(BLOCKS):
-        for h in range(HEADS):
-            source = q_hbm.at[rows_at(rank ^ n), h * DH : (h + 1) * DH]
-            copies.append(
-                pltpu.make_async_copy(source, q_ref.at[n, h * BLOCK : (h + 1) * BLOCK, :], sems.at[1 + n, h])
-            )
+        copies.append(pltpu.make_async_copy(q_hbm.at[rows_at(rank ^ n), :], q_ref.at[n], sems.at[2 + n]))
     for copy in copies:
         copy.start()
     for copy in copies[:2]:
@@ -98,7 +94,7 @@
         copy.wait()
 
 
-def ordered(info, keys, values, queries):
+def ordered(place, keys, values, queries):
     rows = keys.shape[0]
     hbm = pl.BlockSpec(memory_space=pl.ANY)
     return pl.pallas_call(
@@ -109,14 +105,15 @@
             jax.ShapeDtypeStruct((n, 2 * DH), jnp.bfloat16)
             for n in (rows, LATE * BLOCK, rows - LATE * BLOCK)
         ]
-        + [jax.ShapeDtypeStruct((BLOCKS, HEADS * BLOCK, DH), jnp.bfloat16)],
-        scratch_shapes=[pltpu.VMEM(keys.shape, jnp.bfloat16)] * 2 + [pltpu.SemaphoreType.DMA((1 + BLOCKS, HEADS))],
+        + [jax.ShapeDtypeStruct((BLOCKS, BLOCK, HEADS * DH), jnp.bfloat16)],
+        scratch_shapes=[pltpu.VMEM(keys.shape, jnp.bfloat16)] * 2 + [pltpu.SemaphoreType.DMA((2 + BLOCKS,))],
         compiler_params=params(),
         name="order",
-    )(info, *held_in(pltpu.HBM, keys, values, queries))
+    )(place, *held_in(pltpu.HBM, keys, values, queries))
 
 
 def scores_of(q, keys):
+    q = jnp.concatenate([q[:, h * DH : (h + 1) * DH] for h in range(HEADS)], 0)
     return lax.dot_general(
         jnp.concatenate(keys, 0), q, (((1,), (1,)), ((), ())), preferred_element_type=jnp.float32
     )
@@ -162,7 +159,7 @@
     return jnp.concatenate(pieces, 1)
 
 
-def local_kernel(first, count, turn, info_ref, q_ref, kv_ref, *refs):
+def local_kernel(turn, info_ref, q_ref, kv_ref, *refs):
     part_ref, stat_ref = refs[-2:]
     rank = info_ref[0, 0]
 
@@ -173,15 +170,14 @@
         )
         levels = range(BLOCKS.bit_length() - 1)
 
-        def blocks_of(i):
-            n = first + i
+        def blocks_of(n):
             return [kv_ref[m * BLOCK : (m + 1) * BLOCK, :] for m in [n] + [n ^ 2**b for b in levels]]
 
         def start(i):
-            return scores_of(q_ref[first + i], [kv[:, :DH] for kv in blocks_of(i)])
+            return scores_of(q_ref[i], [kv[:, :DH] for kv in blocks_of(i)])
 
         def weigh(i, scores):
-            j = rank ^ (first + i)
+            j = rank ^ i
             bitmaps = [bitmap_at(info_ref, h, j) & j for h in range(HEADS)]
             biases = [0.0] + [bias_of(bitmaps, level) for level in levels]
             return weighted(scores, 1 + len(levels), biases, causal)
@@ -192,18 +188,15 @@
             stat_ref[i, 0:1, :] = top
             stat_ref[i, 1:2, :] = total
 
-        staggered(range(count), start, weigh, finish)
-
-    if turn is None:
-        body()
-    else:
-        pl.when(((info_ref[0, 1] & 7) < FIRST) == (turn == 0))(body)
-
-
-def local_part(info, queries, kv, first, count, turn=None, state=()):
-    width = HEADS * DH
+        staggered(range(BLOCKS), start, weigh, finish)
+
+    pl.when(((info_ref[0, 1] & 7) < FIRST) == (turn == 0))(body)
+
+
+def local_part(info, queries, kv, turn, state=()):
+    count, width = BLOCKS, HEADS * DH
     return pl.pallas_call(
-        functools.partial(local_kernel, first, count, turn),
+        functools.partial(local_kernel, turn),
         in_specs=[pl.BlockSpec(memory_space=pltpu.SMEM)] + [in_vmem()] * (2 + len(state)),
         out_specs=[in_vmem()] * 2,
         out_shape=[
@@ -223,6 +216,7 @@
     arrays = sum(number for _, number in held)
     kv_refs, outs = refs[:arrays], refs[arrays:]
     levels = [slot_level(slot, info_ref[0, 1], BLOCKS.bit_length() - 1) for slot, _ in held]
+    base = first if part_ref.shape[0] == BLOCKS else 0
     blocks = [n - first for n in final] if final else range(count)
 
     def tiles_of(i, part):
@@ -244,14 +238,14 @@
         j = info_ref[0, 0] ^ (first + i)
         bitmaps = [bitmap_at(info_ref, h, j) for h in range(HEADS)]
         biases = [bias_of(bitmaps, level) for level in levels]
-        return weighted(scores, len(levels), biases, None, (stat_ref[i, 0:1, :],))
+        return weighted(scores, len(levels), biases, None, (stat_ref[base + i, 0:1, :],))
 
     def finish(item, found):
         place, i = item
         weight, top, factor = found
         summed, total = summed_of(tiles_of(i, slice(DH, 2 * DH)), weight)
-        summed = summed + part_ref[i] * factor
-        total = total + stat_ref[i, 1:2, :] * factor
+        summed = summed + part_ref[base + i] * factor
+        total = total + stat_ref[base + i, 1:2, :] * factor
         if final:
             result = summed * (1.0 / total)
             for h in range(HEADS):
@@ -267,7 +261,7 @@
 
 def far_part(info, queries, state, fetched, held, first, final=()):
     part, stats = state
-    count, _, width = part.shape
+    count, width = BLOCKS - LATE if first else LATE, part.shape[2]
     kvs, numbers = [], []
     for slot in held:
         arrays = fetched[slot] if isinstance(fetched[slot], list) else [fetched[slot]]
@@ -404,23 +398,23 @@
 
     by_three = [(i - 3, i) for i in range(lax.axis_size("ctx")) if i & 7 == 6]
 
-    kv, kv_late, kv_rest, queries = ordered(info, keys, values, queries)
+    kv, kv_late, kv_rest, queries = ordered(place, keys, values, queries)
     far = {slot: fetched(kv, slot) for slot in (FOURTH, THIRD)}
     rest = far | {slot: fetched(kv_rest, slot) for slot in (NEAR, SIDE)}
-    straight = [(i, j) for i, j in routes[HALF] if j & 7 != 6]
-    rest[HALF_STRAIGHT] = lax.ppermute(kv_rest, "ctx", straight)
+    some = [(i, j) for i, j in routes[HALF] if j & 7 in (4, 5)]
+    rest[HALF_STRAIGHT] = [lax.ppermute(kv_rest, "ctx", some)]
+    some = [(i, j) for i, j in routes[HALF] if j & 7 == 7]
+    rest[HALF_STRAIGHT] += [lax.ppermute(kv_rest, "ctx", some)]
     rest[SIDE_ONWARD] = [rest[SIDE], lax.ppermute(rest[NEAR], "ctx", by_three)]
     late = far | {slot: fetched(kv_late, slot) for slot in (NEAR, SIDE, HALF)}
-    far_blocks = BLOCKS - LATE
-    state = local_part(info, queries, kv, LATE, far_blocks, 0)
-    state = local_part(info, queries, kv, LATE, far_blocks, 1, state)
-    late_state = local_part(info, queries, kv, 0, LATE)
-    state = far_part(info, queries, state, rest, (NEAR, FOURTH, THIRD), LATE)
+    own = local_part(info, queries, kv, 0)
+    own = local_part(info, queries, kv, 1, own)
+    state = far_part(info, queries, own, rest, (NEAR, FOURTH), LATE)
+    state = far_part(info, queries, state, rest, (THIRD,), LATE)
     sent = {}
-    for some in (SWAPS[:4], SWAPS[4:]):
+    for some in (SWAPS,):
         sent |= zip(some, far_part(info, queries, state, rest, (SIDE_ONWARD, HALF_STRAIGHT), LATE, some))
-    late_state = far_part(info, queries, late_state, late, (FOURTH, THIRD), 0)
-    parts = far_part(info, queries, late_state, late, (NEAR, SIDE, HALF), 0, range(LATE))
+    parts = far_part(info, queries, own, late, (FOURTH, THIRD, NEAR, SIDE, HALF), 0, range(LATE))
     parts += [sent[n] for n in range(LATE, BLOCKS)]
     parts = parts[:1] + [swapped(parts[n], n) for n in range(1, BLOCKS)]
     soon = [n for n in range(BLOCKS) if n in EARLY]

time: 73.8 us -> 93.7 us (1.27)
  the two profiles are of different devices: /device:TPU:33 before, /device:TPU:97 now
where the time goes in v5:
time: 93.7 us; the launch traced here: 93.4 us
  starting transfers between devices  58.8 us (63%)
  waiting for transfers between devices  16.9 us (18%)
  Pallas kernels  16.7 us (18%)
  between operations  1.06 us (1%)
    ppermute x7, starting transfers between devices, swapped(): return lax.ppermute(array, 'head', [(i, i ^ n) for i in range(groups)])  30.3 us
    ppermute x7, starting transfers between devices, fetched(): return lax.ppermute(array, 'ctx', routes[slot])  18.5 us
    ppermute x7, waiting for transfers between devices, fetched(): return lax.ppermute(array, 'ctx', routes[slot])  8.9 us
    ppermute x7, waiting for transfers between devices, swapped(): return lax.ppermute(array, 'head', [(i, i ^ n) for i in range(groups)])  7.95 us
    ppermute x1, starting transfers between devices, shards(): rest[HALF_STRAIGHT] += [lax.ppermute(kv_rest, 'ctx', some)]  7.71 us
    pallas_call x4, Pallas kernels, far_part(): pl.pallas_call(functools.partial(far_kernel, numbers, first, count, final...  7.39 us
    pallas_call x2, Pallas kernels, local_part(): pl.pallas_call(functools.partial(local_kernel, turn), in_specs=[pl.BlockS...  3.84 us
    pallas_call x1, Pallas kernels, norm_part(): pl.pallas_call(functools.partial(norm_kernel, groups, before), in_specs=[...  1.97 us
  transfers between devices with their start and end apart: 17, of which 6 were waited for; matrix products, arithmetic and copies ran while one was open for 0% of the time, Pallas kernels for 14%

profile of v5, /device:TPU:97, one launch (start us, length us, event | category | flops | bytes accessed | tf_op | source)
XLA Modules:
  0.0 93.4 jit_solution(3919132882939902560)
XLA Ops:
  0.7 2.0 %order.1 = (bf16[1024,256]{1,0:T(8,128)(2,1)S(1)}, bf16[256,256]{1,0:T(8,128)(2,1)S(1)}, bf16[768,256]{1,0:T(8,128)(2,1)S(1)}, bf16[8,128,512]{2,1,0:T(8,128)(2,1)S(1)}) custom-call(s32[1,8]{1,0:T(1,128)S(1)} %compare_select_fusion.info_ref, bf16[1024,128]{1,0:T(8,128)(2,1)} %k_hbm.1, bf16[1024,128]{1,0:T(8,128)(2,1)} %v_hbm.1, bf16[1024,512]{1,0:T(8,128)(2,1)} %q_hbm.1), custom_call_target="tpu_custom_call" | custom-call | tf_op jit(solution)/shard_map/order/pallas_call | solution.py:100
  2.6 4.9 %collective-permute-start.1 = (bf16[1024,256]{1,0:T(8,128)(2,1)S(1)}, bf16[1024,256]{1,0:T(8,128)(2,1)S(1)}, u32[]{:S(2)}, u32[]{:S(2)}) collective-permute-start(bf16[1024,256]{1,0:T(8,128)(2,1)S(1)} %get-tuple-element.26.kv_ref), channel_id=1, source_target_pairs={{0,128},{8,136},{16,144},{24,152},{32,160},{40,168},{48,176},{56,1... | collective-permute-start | bytes 1572872 | tf_op jit(solution)/shard_map/ppermute | solution.py:394
  7.5 1.3 %collective-permute-start = (bf16[768,256]{1,0:T(8,128)(2,1)S(1)}, bf16[768,256]{1,0:T(8,128)(2,1)S(1)}, u32[]{:S(2)}, u32[]{:S(2)}) collective-permute-start(bf16[768,256]{1,0:T(8,128)(2,1)S(1)} %get-tuple-element.31), channel_id=1, source_target_pairs={{0,16},{16,24},{32,48},{48,56},{64,80},{80,88},{96,112},{112,120},... | collective-permute-start | bytes 1179656 | tf_op jit(solution)/shard_map/ppermute | solution.py:394
  8.8 1.3 %collective-permute-start.10 = (bf16[256,256]{1,0:T(8,128)(2,1)S(1)}, bf16[256,256]{1,0:T(8,128)(2,1)S(1)}, u32[]{:S(2)}, u32[]{:S(2)}) collective-permute-start(bf16[256,256]{1,0:T(8,128)(2,1)S(1)} %get-tuple-element.39), channel_id=1, source_target_pairs={{0,16},{16,24},{32,48},{48,56},{64,80},{80,88},{96,112},{112,120},... | collective-permute-start | bytes 393224 | tf_op jit(solution)/shard_map/ppermute | solution.py:394
  10.1 2.3 %collective-permute-start.2 = (bf16[1024,256]{1,0:T(8,128)(2,1)S(1)}, bf16[1024,256]{1,0:T(8,128)(2,1)S(1)}, u32[]{:S(2)}, u32[]{:S(2)}) collective-permute-start(bf16[1024,256]{1,0:T(8,128)(2,1)S(1)} %get-tuple-element.26.kv_ref), channel_id=1, source_target_pairs={{0,64},{8,72},{16,80},{24,88},{32,96},{40,104},{48,112},{56,120},{... | collective-permute-start | bytes 1572872 | tf_op jit(solution)/shard_map/ppermute | solution.py:394
  12.4 1.3 %collective-permute-start.11 = (bf16[256,256]{1,0:T(8,128)(2,1)S(1)}, bf16[256,256]{1,0:T(8,128)(2,1)S(1)}, u32[]{:S(2)}, u32[]{:S(2)}) collective-permute-start(bf16[256,256]{1,0:T(8,128)(2,1)S(1)} %get-tuple-element.39), channel_id=1, source_target_pairs={{0,8},{8,24},{32,40},{40,56},{64,72},{72,88},{96,104},{104,120},{1... | collective-permute-start | bytes 393224 | tf_op jit(solution)/shard_map/ppermute | solution.py:394
  13.7 8.3 %collective-permute-done.10.refs_2_ = bf16[256,256]{1,0:T(8,128)(2,1)S(1)} collective-permute-done((bf16[256,256]{1,0:T(8,128)(2,1)S(1)}, bf16[256,256]{1,0:T(8,128)(2,1)S(1)}, u32[]{:S(2)}, u32[]{:S(2)}) %collective-permute-start.10) | collective-permute-done | bytes 131104 | tf_op jit(solution)/shard_map/ppermute | solution.py:394
  22.0 6.1 %collective-permute-start.12 = (bf16[256,256]{1,0:T(8,128)(2,1)S(1)}, bf16[256,256]{1,0:T(8,128)(2,1)S(1)}, u32[]{:S(2)}, u32[]{:S(2)}) collective-permute-start(bf16[256,256]{1,0:T(8,128)(2,1)S(1)} %get-tuple-element.39), channel_id=1, source_target_pairs={{0,32},{8,40},{16,48},{24,56},{64,96},{72,104},{80,112},{88,120},{... | collective-permute-start | bytes 393224 | tf_op jit(solution)/shard_map/ppermute | solution.py:394
  28.1 1.3 %collective-permute-start.3 = (bf16[768,256]{1,0:T(8,128)(2,1)S(1)}, bf16[768,256]{1,0:T(8,128)(2,1)S(1)}, u32[]{:S(2)}, u32[]{:S(2)}) collective-permute-start(bf16[768,256]{1,0:T(8,128)(2,1)S(1)} %get-tuple-element.31), channel_id=1, source_target_pairs={{0,8},{8,24},{32,40},{40,56},{64,72},{72,88},{96,104},{104,120},{1... | collective-permute-start | bytes 1179656 | tf_op jit(solution)/shard_map/ppermute | solution.py:394
  30.7 7.7 %collective-permute-start.6 = (bf16[768,256]{1,0:T(8,128)(2,1)S(1)}, bf16[768,256]{1,0:T(8,128)(2,1)S(1)}, u32[]{:S(2)}, u32[]{:S(2)}) collective-permute-start(bf16[768,256]{1,0:T(8,128)(2,1)S(1)} %get-tuple-element.31), channel_id=1, source_target_pairs={{24,56},{88,120},{152,184},{216,248},{25,57},{89,121},{153,185},{2... | collective-permute-start | bytes 1179656 | tf_op jit(solution)/shard_map/ppermute | solution.py:407
  38.5 1.7 %collective-permute-start.4 = (bf16[768,256]{1,0:T(8,128)(2,1)S(1)}, bf16[768,256]{1,0:T(8,128)(2,1)S(1)}, u32[]{:S(2)}, u32[]{:S(2)}) collective-permute-start(bf16[768,256]{1,0:T(8,128)(2,1)S(1)} %collective-permute-done.refs_0_), channel_id=1, source_target_pairs={{24,48},{88,112},{152,176},{216,240},{25,49},{89,113},{153,177},{2... | collective-permute-start | bytes 1179656 | tf_op jit(solution)/shard_map/ppermute | solution.py:408
  40.8 3.2 %local.3 = (f32[8,128,512]{2,1,0:T(8,128)S(1)}, f32[8,8,512]{2,1,0:T(8,128)S(1)}) custom-call(s32[5,8]{1,0:T(8,128)S(1)} %pad_add_fusion.info_ref, bf16[8,128,512]{2,1,0:T(8,128)(2,1)S(1)} %get-tuple-element.25.q_ref, bf16[1024,256]{1,0:T(8,128)(2,1)S(1)} %get-tuple-element.26.kv_ref, ...), custom_call_target="tpu_custom_call", output_to_operand_aliasing={{0}: (3, {}), {1}: (4, {})} | custom-call | flops 1073741824 | bytes 4000000 | tf_op jit(solution)/shard_map/local/pallas_call | solution.py:198
  44.0 1.9 %far.7 = (bf16[128,512]{1,0:T(8,128)(2,1)S(1)}, bf16[128,512]{1,0:T(8,128)(2,1)S(1)}) custom-call(s32[5,8]{1,0:T(8,128)S(1)} %pad_add_fusion.info_ref, bf16[8,128,512]{2,1,0:T(8,128)(2,1)S(1)} %get-tuple-element.25.q_ref, f32[8,128,512]{2,1,0:T(8,128)S(1)} %get-tuple-element.29.part_ref, f32[8,8,512]{2,1,0:T(8,128)S(1)} %get-tuple-element.30.stat_ref, ...), custom_call_target="tpu_custom_call" | custom-call | flops 335544320 | bytes 4000000 | tf_op jit(solution)/shard_map/far/pallas_call | solution.py:277
  45.9 21.5 %collective-permute-start.13 = (bf16[128,512]{1,0:T(8,128)(2,1)S(1)}, bf16[128,512]{1,0:T(8,128)(2,1)S(1)}, u32[]{:S(2)}, u32[]{:S(2)}) collective-permute-start(bf16[128,512]{1,0:T(8,128)(2,1)S(1)} %get-tuple-element.41), channel_id=1, source_target_pairs={{0,1},{1,0},{2,3},{3,2},{4,5},{5,4},{6,7},{7,6},{8,9},{9,8},{10,11... | collective-permute-start | bytes 393224 | tf_op jit(solution)/shard_map/ppermute | solution.py:397
  67.4 1.9 %far.4 = (f32[6,128,512]{2,1,0:T(8,128)S(1)}, f32[6,8,512]{2,1,0:T(8,128)S(1)}) custom-call(s32[5,8]{1,0:T(8,128)S(1)} %pad_add_fusion.info_ref, bf16[8,128,512]{2,1,0:T(8,128)(2,1)S(1)} %get-tuple-element.25.q_ref, f32[8,128,512]{2,1,0:T(8,128)S(1)} %get-tuple-element.29.part_ref, f32[8,8,512]{2,1,0:T(8,128)S(1)} %get-tuple-element.30.stat_ref, ...), custom_call_target="tpu_custom_call" | custom-call | flops 402653184 | bytes 4000000 | tf_op jit(solution)/shard_map/far/pallas_call | solution.py:277
  69.3 1.5 %far.5 = (f32[6,128,512]{2,1,0:T(8,128)S(1)}, f32[6,8,512]{2,1,0:T(8,128)S(1)}) custom-call(s32[5,8]{1,0:T(8,128)S(1)} %pad_add_fusion.info_ref, bf16[8,128,512]{2,1,0:T(8,128)(2,1)S(1)} %get-tuple-element.25.q_ref, f32[6,128,512]{2,1,0:T(8,128)S(1)} %get-tuple-element.32.part_ref, f32[6,8,512]{2,1,0:T(8,128)S(1)} %get-tuple-element.33.stat_ref, ...), custom_call_target="tpu_custom_call" | custom-call | flops 201326592 | bytes 4000000 | tf_op jit(solution)/shard_map/far/pallas_call | solution.py:277
  70.9 2.1 %far.6 = (bf16[128,512]{1,0:T(8,128)(2,1)S(1)}, bf16[128,512]{1,0:T(8,128)(2,1)S(1)}, bf16[128,512]{1,0:T(8,128)(2,1)S(1)}, bf16[128,512]{1,0:T(8,128)(2,1)S(1)}...) custom-call(s32[5,8]{1,0:T(8,128)S(1)} %pad_add_fusion.info_ref, ...), custom_call_target="tpu_custom_call" | custom-call | flops 805306368 | bytes 4000000 | tf_op jit(solution)/shard_map/far/pallas_call | solution.py:277
  74.2 2.5 %collective-permute-start.15 = (bf16[128,512]{1,0:T(8,128)(2,1)S(1)}, bf16[128,512]{1,0:T(8,128)(2,1)S(1)}, u32[]{:S(2)}, u32[]{:S(2)}) collective-permute-start(bf16[128,512]{1,0:T(8,128)(2,1)S(1)} %get-tuple-element.43), channel_id=1, source_target_pairs={{0,4},{1,5},{2,6},{3,7},{4,0},{5,1},{6,2},{7,3},{8,12},{9,13},{10,... | collective-permute-start | bytes 393224 | tf_op jit(solution)/shard_map/ppermute | solution.py:397
  76.9 4.9 %collective-permute-start.8 = (bf16[128,512]{1,0:T(8,128)(2,1)S(1)}, bf16[128,512]{1,0:T(8,128)(2,1)S(1)}, u32[]{:S(2)}, u32[]{:S(2)}) collective-permute-start(bf16[128,512]{1,0:T(8,128)(2,1)S(1)} %get-tuple-element.37), channel_id=1, source_target_pairs={{0,5},{1,4},{2,7},{3,6},{4,1},{5,0},{6,3},{7,2},{8,13},{9,12},{10,... | collective-permute-start | bytes 393224 | tf_op jit(solution)/shard_map/ppermute | solution.py:397
  82.9 2.5 %collective-permute-done.16.refs_4_ = bf16[128,512]{1,0:T(8,128)(2,1)S(1)} collective-permute-done((bf16[128,512]{1,0:T(8,128)(2,1)S(1)}, bf16[128,512]{1,0:T(8,128)(2,1)S(1)}, u32[]{:S(2)}, u32[]{:S(2)}) %collective-permute-start.16) | collective-permute-done | bytes 131104 | tf_op jit(solution)/shard_map/ppermute | solution.py:397
  85.5 1.5 %sums.1 = (bf16[128,4096]{1,0:T(8,128)(2,1)}, f32[5,128,512]{2,1,0:T(8,128)S(1)}, f32[128,128]{1,0:T(8,128)S(1)}) custom-call(s32[5,8]{1,0:T(8,128)S(1)} %pad_add_fusion.info_ref, bf16[128,512]{1,0:T(8,128)(2,1)S(1)} %get-tuple-element.40.refs_0_, bf16[128,512]{1,0:T(8,128)(2,1)S(1)} %collective-permute-done.13.refs_1_, ...), custom_call_target="tpu_custom_call" | custom-call | flops 2000000 | bytes 2000000 | tf_op jit(solution)/shard_map/sums/pallas_call | solution.py:324
  87.0 2.0 %collective-permute-done.8.refs_1_ = bf16[128,512]{1,0:T(8,128)(2,1)S(1)} collective-permute-done((bf16[128,512]{1,0:T(8,128)(2,1)S(1)}, bf16[128,512]{1,0:T(8,128)(2,1)S(1)}, u32[]{:S(2)}, u32[]{:S(2)}) %collective-permute-start.8) | collective-permute-done | bytes 131104 | tf_op jit(solution)/shard_map/ppermute | solution.py:397
  89.0 2.3 %collective-permute-done.9.refs_2_ = bf16[128,512]{1,0:T(8,128)(2,1)S(1)} collective-permute-done((bf16[128,512]{1,0:T(8,128)(2,1)S(1)}, bf16[128,512]{1,0:T(8,128)(2,1)S(1)}, u32[]{:S(2)}, u32[]{:S(2)}) %collective-permute-start.9) | collective-permute-done | bytes 131104 | tf_op jit(solution)/shard_map/ppermute | solution.py:397
  91.3 2.0 %norm.1 = (bf16[128,4096]{1,0:T(8,128)(2,1)}, bf16[128,4096]{1,0:T(8,128)(2,1)}) custom-call(s32[5,8]{1,0:T(8,128)S(1)} %pad_add_fusion.info_ref, bf16[128,512]{1,0:T(8,128)(2,1)S(1)} %collective-permute-done.7.refs_0_, bf16[128,512]{1,0:T(8,128)(2,1)S(1)} %collective-permute-done.8.refs_1_, ...), custom_call_target="tpu_custom_call", output_to_operand_aliasing={{0}: (6, {})} | custom-call | flops 4000000 | bytes 4000000 | tf_op jit(solution)/shard_map/norm/pallas_call | solution.py:368
  (28 shorter events, 4.5 us)
Async XLA Ops:
  0.6 39.5 %copy-start.2 = (s32[4,8]{1,0:T(4,128)S(1)}, s32[4,8]{1,0:T(4,128)}, u32[]{:S(2)}) copy-start(s32[4,8]{1,0:T(4,128)} %param.9) | copy-start | bytes 388
  2.6 35.8 %collective-permute-start.1 = (bf16[1024,256]{1,0:T(8,128)(2,1)S(1)}, bf16[1024,256]{1,0:T(8,128)(2,1)S(1)}, u32[]{:S(2)}, u32[]{:S(2)}) collective-permute-start(bf16[1024,256]{1,0:T(8,128)(2,1)S(1)} %get-tuple-element.26.kv_ref), channel_id=1, source_target_pairs={{0,128},{8,136},{16,144},{24,152},{32,160},{40,168},{48,176},{56,1... | collective-permute-start | bytes 1572872 | tf_op jit(solution)/shard_map/ppermute | solution.py:394
  7.5 23.2 %collective-permute-start = (bf16[768,256]{1,0:T(8,128)(2,1)S(1)}, bf16[768,256]{1,0:T(8,128)(2,1)S(1)}, u32[]{:S(2)}, u32[]{:S(2)}) collective-permute-start(bf16[768,256]{1,0:T(8,128)(2,1)S(1)} %get-tuple-element.31), channel_id=1, source_target_pairs={{0,16},{16,24},{32,48},{48,56},{64,80},{80,88},{96,112},{112,120},... | collective-permute-start | bytes 1179656 | tf_op jit(solution)/shard_map/ppermute | solution.py:394
  8.8 13.2 %collective-permute-start.10 = (bf16[256,256]{1,0:T(8,128)(2,1)S(1)}, bf16[256,256]{1,0:T(8,128)(2,1)S(1)}, u32[]{:S(2)}, u32[]{:S(2)}) collective-permute-start(bf16[256,256]{1,0:T(8,128)(2,1)S(1)} %get-tuple-element.39), channel_id=1, source_target_pairs={{0,16},{16,24},{32,48},{48,56},{64,80},{80,88},{96,112},{112,120},... | collective-permute-start | bytes 393224 | tf_op jit(solution)/shard_map/ppermute | solution.py:394
  10.1 33.9 %collective-permute-start.2 = (bf16[1024,256]{1,0:T(8,128)(2,1)S(1)}, bf16[1024,256]{1,0:T(8,128)(2,1)S(1)}, u32[]{:S(2)}, u32[]{:S(2)}) collective-permute-start(bf16[1024,256]{1,0:T(8,128)(2,1)S(1)} %get-tuple-element.26.kv_ref), channel_id=1, source_target_pairs={{0,64},{8,72},{16,80},{24,88},{32,96},{40,104},{48,112},{56,120},{... | collective-permute-start | bytes 1572872 | tf_op jit(solution)/shard_map/ppermute | solution.py:394
  12.4 15.7 %collective-permute-start.11 = (bf16[256,256]{1,0:T(8,128)(2,1)S(1)}, bf16[256,256]{1,0:T(8,128)(2,1)S(1)}, u32[]{:S(2)}, u32[]{:S(2)}) collective-permute-start(bf16[256,256]{1,0:T(8,128)(2,1)S(1)} %get-tuple-element.39), channel_id=1, source_target_pairs={{0,8},{8,24},{32,40},{40,56},{64,72},{72,88},{96,104},{104,120},{1... | collective-permute-start | bytes 393224 | tf_op jit(solution)/shard_map/ppermute | solution.py:394
  22.0 8.0 %collective-permute-start.12 = (bf16[256,256]{1,0:T(8,128)(2,1)S(1)}, bf16[256,256]{1,0:T(8,128)(2,1)S(1)}, u32[]{:S(2)}, u32[]{:S(2)}) collective-permute-start(bf16[256,256]{1,0:T(8,128)(2,1)S(1)} %get-tuple-element.39), channel_id=1, source_target_pairs={{0,32},{8,40},{16,48},{24,56},{64,96},{72,104},{80,112},{88,120},{... | collective-permute-start | bytes 393224 | tf_op jit(solution)/shard_map/ppermute | solution.py:394
  28.1 42.7 %collective-permute-start.3 = (bf16[768,256]{1,0:T(8,128)(2,1)S(1)}, bf16[768,256]{1,0:T(8,128)(2,1)S(1)}, u32[]{:S(2)}, u32[]{:S(2)}) collective-permute-start(bf16[768,256]{1,0:T(8,128)(2,1)S(1)} %get-tuple-element.31), channel_id=1, source_target_pairs={{0,8},{8,24},{32,40},{40,56},{64,72},{72,88},{96,104},{104,120},{1... | collective-permute-start | bytes 1179656 | tf_op jit(solution)/shard_map/ppermute | solution.py:394
  30.1 40.8 %collective-permute-start.5 = (bf16[768,256]{1,0:T(8,128)(2,1)S(1)}, bf16[768,256]{1,0:T(8,128)(2,1)S(1)}, u32[]{:S(2)}, u32[]{:S(2)}) collective-permute-start(bf16[768,256]{1,0:T(8,128)(2,1)S(1)} %get-tuple-element.31), channel_id=1, source_target_pairs={{0,32},{8,40},{64,96},{72,104},{128,160},{136,168},{192,224},{200,... | collective-permute-start | bytes 1179656 | tf_op jit(solution)/shard_map/ppermute | solution.py:405
  30.7 40.1 %collective-permute-start.6 = (bf16[768,256]{1,0:T(8,128)(2,1)S(1)}, bf16[768,256]{1,0:T(8,128)(2,1)S(1)}, u32[]{:S(2)}, u32[]{:S(2)}) collective-permute-start(bf16[768,256]{1,0:T(8,128)(2,1)S(1)} %get-tuple-element.31), channel_id=1, source_target_pairs={{24,56},{88,120},{152,184},{216,248},{25,57},{89,121},{153,185},{2... | collective-permute-start | bytes 1179656 | tf_op jit(solution)/shard_map/ppermute | solution.py:407
  38.5 32.4 %collective-permute-start.4 = (bf16[768,256]{1,0:T(8,128)(2,1)S(1)}, bf16[768,256]{1,0:T(8,128)(2,1)S(1)}, u32[]{:S(2)}, u32[]{:S(2)}) collective-permute-start(bf16[768,256]{1,0:T(8,128)(2,1)S(1)} %collective-permute-done.refs_0_), channel_id=1, source_target_pairs={{24,48},{88,112},{152,176},{216,240},{25,49},{89,113},{153,177},{2... | collective-permute-start | bytes 1179656 | tf_op jit(solution)/shard_map/ppermute | solution.py:408
  45.9 31.0 %collective-permute-start.13 = (bf16[128,512]{1,0:T(8,128)(2,1)S(1)}, bf16[128,512]{1,0:T(8,128)(2,1)S(1)}, u32[]{:S(2)}, u32[]{:S(2)}) collective-permute-start(bf16[128,512]{1,0:T(8,128)(2,1)S(1)} %get-tuple-element.41), channel_id=1, source_target_pairs={{0,1},{1,0},{2,3},{3,2},{4,5},{5,4},{6,7},{7,6},{8,9},{9,8},{10,11... | collective-permute-start | bytes 393224 | tf_op jit(solution)/shard_map/ppermute | solution.py:397
  70.9 10.9 %copy-start.1 = (bf16[4096]{0:T(1024)(128)(2,1)S(1)}, bf16[4096]{0:T(1024)(128)(2,1)}, u32[]{:S(2)}) copy-start(bf16[4096]{0:T(1024)(128)(2,1)} %param.11) | copy-start | bytes 24580
  70.9 14.6 %copy-start = (bf16[128,4096]{1,0:T(8,128)(2,1)S(1)}, bf16[128,4096]{1,0:T(8,128)(2,1)}, u32[]{:S(2)}) copy-start(bf16[128,4096]{1,0:T(8,128)(2,1)} %refs_3_.1) | copy-start | bytes 3145732
  73.0 8.7 %collective-permute-start.14 = (bf16[128,512]{1,0:T(8,128)(2,1)S(1)}, bf16[128,512]{1,0:T(8,128)(2,1)S(1)}, u32[]{:S(2)}, u32[]{:S(2)}) collective-permute-start(bf16[128,512]{1,0:T(8,128)(2,1)S(1)} %get-tuple-element.42), channel_id=1, source_target_pairs={{0,3},{1,2},{2,1},{3,0},{4,7},{5,6},{6,5},{7,4},{8,11},{9,10},{10,... | collective-permute-start | bytes 393224 | tf_op jit(solution)/shard_map/ppermute | solution.py:397
  74.2 8.7 %collective-permute-start.15 = (bf16[128,512]{1,0:T(8,128)(2,1)S(1)}, bf16[128,512]{1,0:T(8,128)(2,1)S(1)}, u32[]{:S(2)}, u32[]{:S(2)}) collective-permute-start(bf16[128,512]{1,0:T(8,128)(2,1)S(1)} %get-tuple-element.43), channel_id=1, source_target_pairs={{0,4},{1,5},{2,6},{3,7},{4,0},{5,1},{6,2},{7,3},{8,12},{9,13},{10,... | collective-permute-start | bytes 393224 | tf_op jit(solution)/shard_map/ppermute | solution.py:397
  76.7 8.8 %collective-permute-start.16 = (bf16[128,512]{1,0:T(8,128)(2,1)S(1)}, bf16[128,512]{1,0:T(8,128)(2,1)S(1)}, u32[]{:S(2)}, u32[]{:S(2)}) collective-permute-start(bf16[128,512]{1,0:T(8,128)(2,1)S(1)} %get-tuple-element.44), channel_id=1, source_target_pairs={{0,6},{1,7},{2,4},{3,5},{4,2},{5,3},{6,0},{7,1},{8,14},{9,15},{10,... | collective-permute-start | bytes 393224 | tf_op jit(solution)/shard_map/ppermute | solution.py:397
  76.9 10.1 %collective-permute-start.7 = (bf16[128,512]{1,0:T(8,128)(2,1)S(1)}, bf16[128,512]{1,0:T(8,128)(2,1)S(1)}, u32[]{:S(2)}, u32[]{:S(2)}) collective-permute-start(bf16[128,512]{1,0:T(8,128)(2,1)S(1)} %get-tuple-element.36), channel_id=1, source_target_pairs={{0,2},{1,3},{2,0},{3,1},{4,6},{5,7},{6,4},{7,5},{8,10},{9,11},{10,... | collective-permute-start | bytes 393224 | tf_op jit(solution)/shard_map/ppermute | solution.py:397
  76.9 12.1 %collective-permute-start.8 = (bf16[128,512]{1,0:T(8,128)(2,1)S(1)}, bf16[128,512]{1,0:T(8,128)(2,1)S(1)}, u32[]{:S(2)}, u32[]{:S(2)}) collective-permute-start(bf16[128,512]{1,0:T(8,128)(2,1)S(1)} %get-tuple-element.37), channel_id=1, source_target_pairs={{0,5},{1,4},{2,7},{3,6},{4,1},{5,0},{6,3},{7,2},{8,13},{9,12},{10,... | collective-permute-start | bytes 393224 | tf_op jit(solution)/shard_map/ppermute | solution.py:397
  81.8 9.5 %collective-permute-start.9 = (bf16[128,512]{1,0:T(8,128)(2,1)S(1)}, bf16[128,512]{1,0:T(8,128)(2,1)S(1)}, u32[]{:S(2)}, u32[]{:S(2)}) collective-permute-start(bf16[128,512]{1,0:T(8,128)(2,1)S(1)} %get-tuple-element.38), channel_id=1, source_target_pairs={{0,7},{1,6},{2,5},{3,4},{4,3},{5,2},{6,1},{7,0},{8,15},{9,14},{10,... | collective-permute-start | bytes 393224 | tf_op jit(solution)/shard_map/ppermute | solution.py:397
